TPU v7x, 256 devices: a whole 4x4x8 slice. The times are simulated.
256 devices in a mesh: ctx: 256 (over x, z, y, core).
Axes of the slice: x: 4, y: 4, z: 8, core: 2. Of those that a mesh axis runs over, the one named last changes fastest.
Arguments:
- queries: bfloat16 [32768, 2048], P('ctx'), may hold values from -128 to 128
- key_heads: bfloat16 [32768, 512], P('ctx'), may hold values from -8 to 8
- value_heads: bfloat16 [32768, 512], P('ctx'), may hold values from -6 to 6
- out_grad: bfloat16 [32768, 2048], P('ctx'), may hold values from -6 to 6
- segment: int32 [32768], P('ctx'), may hold values from 0 to 63, never falling along the last dimension, each value on 1 to 2048 neighbouring positions
- sink_logits: float32 [32], replicated, may hold values from 0 to 4
Outputs:
- query_grad: bfloat16 [32768, 2048], P('ctx')
- key_grad: bfloat16 [32768, 512], P('ctx')
- value_grad: bfloat16 [32768, 512], P('ctx')
- sink_grad: float32 [32], replicated
Inputs may be any that keep to these rules, and one draw needn't show every extreme that they name: `segment`: never falls along the tokens; each document holds 1 to 2048 tokens, one exactly that many.
All inputs are finite; a program needn't handle non-finite values.
Results may differ from a plain program's by a relative error of at most 0.008.
Values may be sent and summed in bfloat16 or wider, within the bound.
No kernel may reach another device: no remote copies, remote signals or barrier semaphores. Data moves between devices by JAX's collectives and lax.ppermute only.
A program may use at most 128 MiB of HBM per device.

v0:
```python
import functools
import math

import jax
import jax.numpy as jnp
from jax import lax
from jax.sharding import Mesh
from jax.sharding import PartitionSpec as P

QUERY_HEADS = 32
KV_HEADS = 8
HEAD_DIM = 64
WINDOW = 1024
CTX = ("ctx_0", "ctx_1", "ctx_2", "ctx_3")


def passed_along(block, axis, distance):
    devices = range(lax.axis_size(axis))
    route = [(i - distance, i) for i in devices if i - distance in devices]
    return lax.ppermute(block, axis, route)


def by_axis(value, axes):
    return functools.reduce(lax.psum, axes, value)


def group_grads(query_group, key_group, value_group, grad_group, allowed, sink_group):
    score_scale = 1.0 / math.sqrt(HEAD_DIM)
    scores = (
        jnp.einsum("bgd,ld->gbl", query_group, key_group, preferred_element_type=jnp.float32)
        * score_scale
    )
    scores = jnp.where(allowed[None], scores, -jnp.inf)
    sink_grid = sink_group[:, None, None]
    top_value = jnp.maximum(jnp.max(scores, -1, keepdims=True), sink_grid)
    expd = jnp.exp(scores - top_value)
    sink_exp = jnp.exp(sink_grid - top_value)
    denom = jnp.sum(expd, -1, keepdims=True) + sink_exp
    probs = expd / denom
    sink_prob = (sink_exp / denom)[..., 0]
    weights = probs.astype(jnp.bfloat16)
    attended = jnp.einsum("gbl,ld->gbd", weights, value_group, preferred_element_type=jnp.float32)
    delta = jnp.einsum("bgd,gbd->gb", grad_group.astype(jnp.float32), attended)
    dprob = jnp.einsum("bgd,ld->gbl", grad_group, value_group, preferred_element_type=jnp.float32)
    dscore = (probs * (dprob - delta[..., None])).astype(jnp.bfloat16)
    query_part = (
        jnp.einsum("gbl,ld->bgd", dscore, key_group, preferred_element_type=jnp.float32)
        * score_scale
    )
    key_part = (
        jnp.einsum("gbl,bgd->ld", dscore, query_group, preferred_element_type=jnp.float32)
        * score_scale
    )
    value_part = jnp.einsum("gbl,bgd->ld", weights, grad_group, preferred_element_type=jnp.float32)
    sink_part = -jnp.sum(sink_prob * delta, -1)
    return (query_part, key_part, value_part, sink_part)


def per_device(queries, key_heads, value_heads, out_grad, segment, sink_logits):
    tok_rows = queries.shape[0]
    hop_count = WINDOW // tok_rows
    groups = QUERY_HEADS // KV_HEADS
    marked = segment + 1
    own_block = (key_heads, value_heads, marked)
    arrived = []
    current = own_block
    for distance in range(hop_count):
        current = passed_along((current[0], current[1], current[2]), CTX, 1)
        arrived.append(current)
    ordered = arrived[::-1] + [own_block]
    key_all = jnp.concatenate([item[0] for item in ordered], 0)
    value_all = jnp.concatenate([item[1] for item in ordered], 0)
    marks_all = jnp.concatenate([item[2] for item in ordered], 0)
    key_span = key_all.shape[0]
    query_pos = jnp.arange(tok_rows, dtype=jnp.int32)[:, None]
    key_pos = jnp.arange(key_span, dtype=jnp.int32)[None, :]
    allowed = (
        (key_pos > query_pos)
        & (key_pos <= query_pos + WINDOW)
        & (marked[:, None] == marks_all[None, :])
    )
    query_list = []
    key_list = []
    value_list = []
    sink_list = []
    for kv_group in range(KV_HEADS):
        query_group = queries[
            :, kv_group * groups * HEAD_DIM : (kv_group + 1) * groups * HEAD_DIM
        ].reshape(tok_rows, groups, HEAD_DIM)
        grad_group = out_grad[
            :, kv_group * groups * HEAD_DIM : (kv_group + 1) * groups * HEAD_DIM
        ].reshape(tok_rows, groups, HEAD_DIM)
        key_group = key_all[:, kv_group * HEAD_DIM : (kv_group + 1) * HEAD_DIM]
        value_group = value_all[:, kv_group * HEAD_DIM : (kv_group + 1) * HEAD_DIM]
        sink_group = sink_logits[kv_group * groups : (kv_group + 1) * groups]
        query_part, key_part, value_part, sink_part = group_grads(
            query_group, key_group, value_group, grad_group, allowed, sink_group
        )
        query_list.append(query_part.reshape(tok_rows, groups * HEAD_DIM))
        key_list.append(key_part)
        value_list.append(value_part)
        sink_list.append(sink_part)
    query_grad = jnp.concatenate(query_list, 1).astype(jnp.bfloat16)
    key_partial = jnp.concatenate(key_list, 1)
    value_partial = jnp.concatenate(value_list, 1)
    sink_local = jnp.concatenate(sink_list, 0)

    def block_of(array, distance):
        first_row = (hop_count - distance) * tok_rows
        return array[first_row : first_row + tok_rows]

    running = (block_of(key_partial, hop_count), block_of(value_partial, hop_count))
    for distance in range(hop_count - 1, -1, -1):
        moved = passed_along((running[0], running[1]), CTX, -1)
        running = (
            moved[0] + block_of(key_partial, distance),
            moved[1] + block_of(value_partial, distance),
        )
    key_sum, value_sum = running
    sink_grad = by_axis(sink_local, CTX)
    return (query_grad, key_sum.astype(jnp.bfloat16), value_sum.astype(jnp.bfloat16), sink_grad)


def solution(mesh):
    finer = Mesh(mesh.devices.reshape(4, 8, 4, 2), ("ctx_0", "ctx_1", "ctx_2", "ctx_3"))
    in_specs = (P(CTX, None), P(CTX, None), P(CTX, None), P(CTX, None), P(CTX), P())
    out_specs = (P(CTX, None), P(CTX, None), P(CTX, None), P())
    return jax.shard_map(
        per_device, mesh=finer, in_specs=in_specs, out_specs=out_specs, check_vma=False
    )
```

profile of v0, /device:TPU:1, one launch (start us, length us, event | category | flops | bytes accessed | tf_op | source)
XLA Modules:
  0.0 312.2 jit_solution(16978167331562506121)
XLA Ops:
  1.3 4.7 %collective-permute-start.8 = (s32[128]{0:T(128)S(1)}, s32[128]{0:T(128)S(1)}, u32[]{:S(2)}, u32[]{:S(2)}) collective-permute-start(s32[128]{0:T(128)S(1)} %broadcast_add_fusion), channel_id=1, source_target_pairs={{0,1},{1,2},{2,3},{3,4},{4,5},{5,6},{6,7},{7,8},{8,9},{9,10},{10,1... | collective-permute-start | bytes 1544 | tf_op jit(solution)/shard_map/ppermute | solution.py:20
  7.1 1.9 collective-permute-start.16
  10.0 3.6 %collective-permute-start = (bf16[128,512]{0,1:T(8,128)(2,1)S(1)}, bf16[128,512]{0,1:T(8,128)(2,1)S(1)}, u32[]{:S(2)}, u32[]{:S(2)}) collective-permute-start(bf16[128,512]{0,1:T(8,128)(2,1)S(1)} %copy.10), channel_id=1, source_target_pairs={{0,1},{1,2},{2,3},{3,4},{4,5},{5,6},{6,7},{7,8},{8,9},{9,10},{10,1... | collective-permute-start | bytes 393224 | tf_op jit(solution)/shard_map/ppermute | solution.py:20
  13.6 1.9 collective-permute-start.9
  16.7 3.7 %collective-permute-start.10 = (s32[128]{0:T(128)S(1)}, s32[128]{0:T(128)S(1)}, u32[]{:S(2)}, u32[]{:S(2)}) collective-permute-start(s32[128]{0:T(128)S(1)} %collective-permute-done.9), channel_id=1, source_target_pairs={{0,1},{1,2},{2,3},{3,4},{4,5},{5,6},{6,7},{7,8},{8,9},{9,10},{10,1... | collective-permute-start | bytes 1544 | tf_op jit(solution)/shard_map/ppermute | solution.py:20
  21.5 3.7 %collective-permute-start.11 = (s32[128]{0:T(128)S(1)}, s32[128]{0:T(128)S(1)}, u32[]{:S(2)}, u32[]{:S(2)}) collective-permute-start(s32[128]{0:T(128)S(1)} %collective-permute-done.10), channel_id=1, source_target_pairs={{0,1},{1,2},{2,3},{3,4},{4,5},{5,6},{6,7},{7,8},{8,9},{9,10},{10,1... | collective-permute-start | bytes 1544 | tf_op jit(solution)/shard_map/ppermute | solution.py:20
  25.3 1.9 collective-permute-start.1
  27.8 3.3 %collective-permute-start.12 = (s32[128]{0:T(128)S(1)}, s32[128]{0:T(128)S(1)}, u32[]{:S(2)}, u32[]{:S(2)}) collective-permute-start(s32[128]{0:T(128)S(1)} %collective-permute-done.11), channel_id=1, source_target_pairs={{0,1},{1,2},{2,3},{3,4},{4,5},{5,6},{6,7},{7,8},{8,9},{9,10},{10,1... | collective-permute-start | bytes 1544 | tf_op jit(solution)/shard_map/ppermute | solution.py:20
  31.8 4.1 %collective-permute-start.13 = (s32[128]{0:T(128)S(1)}, s32[128]{0:T(128)S(1)}, u32[]{:S(2)}, u32[]{:S(2)}) collective-permute-start(s32[128]{0:T(128)S(1)} %collective-permute-done.12), channel_id=1, source_target_pairs={{0,1},{1,2},{2,3},{3,4},{4,5},{5,6},{6,7},{7,8},{8,9},{9,10},{10,1... | collective-permute-start | bytes 1544 | tf_op jit(solution)/shard_map/ppermute | solution.py:20
  36.7 4.1 %collective-permute-start.14 = (s32[128]{0:T(128)S(1)}, s32[128]{0:T(128)S(1)}, u32[]{:S(2)}, u32[]{:S(2)}) collective-permute-start(s32[128]{0:T(128)S(1)} %collective-permute-done.13), channel_id=1, source_target_pairs={{0,1},{1,2},{2,3},{3,4},{4,5},{5,6},{6,7},{7,8},{8,9},{9,10},{10,1... | collective-permute-start | bytes 1544 | tf_op jit(solution)/shard_map/ppermute | solution.py:20
  41.5 4.1 %collective-permute-start.15 = (s32[128]{0:T(128)S(1)}, s32[128]{0:T(128)S(1)}, u32[]{:S(2)}, u32[]{:S(2)}) collective-permute-start(s32[128]{0:T(128)S(1)} %collective-permute-done.14), channel_id=1, source_target_pairs={{0,1},{1,2},{2,3},{3,4},{4,5},{5,6},{6,7},{7,8},{8,9},{9,10},{10,1... | collective-permute-start | bytes 1544 | tf_op jit(solution)/shard_map/ppermute | solution.py:20
  46.0 2.9 collective-permute-start.17
  48.9 4.2 %collective-permute-start.2 = (bf16[128,512]{0,1:T(8,128)(2,1)S(1)}, bf16[128,512]{0,1:T(8,128)(2,1)S(1)}, u32[]{:S(2)}, u32[]{:S(2)}) collective-permute-start(bf16[128,512]{0,1:T(8,128)(2,1)S(1)} %collective-permute-done.1), channel_id=1, source_target_pairs={{0,1},{1,2},{2,3},{3,4},{4,5},{5,6},{6,7},{7,8},{8,9},{9,10},{10,1... | collective-permute-start | bytes 393224 | tf_op jit(solution)/shard_map/ppermute | solution.py:20
  53.1 4.1 %collective-permute-start.18 = (bf16[128,512]{0,1:T(8,128)(2,1)S(1)}, bf16[128,512]{0,1:T(8,128)(2,1)S(1)}, u32[]{:S(2)}, u32[]{:S(2)}) collective-permute-start(bf16[128,512]{0,1:T(8,128)(2,1)S(1)} %collective-permute-done.17), channel_id=1, source_target_pairs={{0,1},{1,2},{2,3},{3,4},{4,5},{5,6},{6,7},{7,8},{8,9},{9,10},{10,1... | collective-permute-start | bytes 393224 | tf_op jit(solution)/shard_map/ppermute | solution.py:20
  57.2 4.3 %collective-permute-start.3 = (bf16[128,512]{0,1:T(8,128)(2,1)S(1)}, bf16[128,512]{0,1:T(8,128)(2,1)S(1)}, u32[]{:S(2)}, u32[]{:S(2)}) collective-permute-start(bf16[128,512]{0,1:T(8,128)(2,1)S(1)} %collective-permute-done.2), channel_id=1, source_target_pairs={{0,1},{1,2},{2,3},{3,4},{4,5},{5,6},{6,7},{7,8},{8,9},{9,10},{10,1... | collective-permute-start | bytes 393224 | tf_op jit(solution)/shard_map/ppermute | solution.py:20
  61.6 6.2 %collective-permute-start.19 = (bf16[128,512]{0,1:T(8,128)(2,1)S(1)}, bf16[128,512]{0,1:T(8,128)(2,1)S(1)}, u32[]{:S(2)}, u32[]{:S(2)}) collective-permute-start(bf16[128,512]{0,1:T(8,128)(2,1)S(1)} %collective-permute-done.18), channel_id=1, source_target_pairs={{0,1},{1,2},{2,3},{3,4},{4,5},{5,6},{6,7},{7,8},{8,9},{9,10},{10,1... | collective-permute-start | bytes 393224 | tf_op jit(solution)/shard_map/ppermute | solution.py:20
  67.8 6.3 %collective-permute-start.4 = (bf16[128,512]{0,1:T(8,128)(2,1)S(1)}, bf16[128,512]{0,1:T(8,128)(2,1)S(1)}, u32[]{:S(2)}, u32[]{:S(2)}) collective-permute-start(bf16[128,512]{0,1:T(8,128)(2,1)S(1)} %collective-permute-done.3), channel_id=1, source_target_pairs={{0,1},{1,2},{2,3},{3,4},{4,5},{5,6},{6,7},{7,8},{8,9},{9,10},{10,1... | collective-permute-start | bytes 393224 | tf_op jit(solution)/shard_map/ppermute | solution.py:20
  74.1 1.9 collective-permute-start.20
  76.0 4.3 %collective-permute-start.5 = (bf16[128,512]{0,1:T(8,128)(2,1)S(1)}, bf16[128,512]{0,1:T(8,128)(2,1)S(1)}, u32[]{:S(2)}, u32[]{:S(2)}) collective-permute-start(bf16[128,512]{0,1:T(8,128)(2,1)S(1)} %collective-permute-done.4), channel_id=1, source_target_pairs={{0,1},{1,2},{2,3},{3,4},{4,5},{5,6},{6,7},{7,8},{8,9},{9,10},{10,1... | collective-permute-start | bytes 393224 | tf_op jit(solution)/shard_map/ppermute | solution.py:20
  80.4 4.0 %collective-permute-start.21 = (bf16[128,512]{0,1:T(8,128)(2,1)S(1)}, bf16[128,512]{0,1:T(8,128)(2,1)S(1)}, u32[]{:S(2)}, u32[]{:S(2)}) collective-permute-start(bf16[128,512]{0,1:T(8,128)(2,1)S(1)} %collective-permute-done.20), channel_id=1, source_target_pairs={{0,1},{1,2},{2,3},{3,4},{4,5},{5,6},{6,7},{7,8},{8,9},{9,10},{10,1... | collective-permute-start | bytes 393224 | tf_op jit(solution)/shard_map/ppermute | solution.py:20
  84.4 2.2 collective-permute-start.6
  86.6 6.1 %collective-permute-start.22 = (bf16[128,512]{0,1:T(8,128)(2,1)S(1)}, bf16[128,512]{0,1:T(8,128)(2,1)S(1)}, u32[]{:S(2)}, u32[]{:S(2)}) collective-permute-start(bf16[128,512]{0,1:T(8,128)(2,1)S(1)} %collective-permute-done.21), channel_id=1, source_target_pairs={{0,1},{1,2},{2,3},{3,4},{4,5},{5,6},{6,7},{7,8},{8,9},{9,10},{10,1... | collective-permute-start | bytes 393224 | tf_op jit(solution)/shard_map/ppermute | solution.py:20
  92.8 1.9 collective-permute-start.7
  95.0 6.6 %collective-permute-start.23 = (bf16[128,512]{0,1:T(8,128)(2,1)S(1)}, bf16[128,512]{0,1:T(8,128)(2,1)S(1)}, u32[]{:S(2)}, u32[]{:S(2)}) collective-permute-start(bf16[128,512]{0,1:T(8,128)(2,1)S(1)} %collective-permute-done.22), channel_id=1, source_target_pairs={{0,1},{1,2},{2,3},{3,4},{4,5},{5,6},{6,7},{7,8},{8,9},{9,10},{10,1... | collective-permute-start | bytes 393224 | tf_op jit(solution)/shard_map/ppermute | solution.py:20
  135.3 1.9 collective-permute-start.24
  142.3 1.9 collective-permute-start.32
  146.8 1.9 collective-permute-start.25
  148.7 2.2 collective-permute-done.32
  151.6 1.9 collective-permute-start.33
  154.2 1.6 copy.40
  156.7 1.9 collective-permute-start.26
  159.5 1.9 collective-permute-start.34
  165.5 1.9 collective-permute-start.27
  167.5 1.9 collective-permute-start.35
  174.2 1.9 collective-permute-start.28
  176.1 1.9 collective-permute-start.36
  179.5 1.6 copy.43
  182.9 1.9 collective-permute-start.29
  184.8 1.9 collective-permute-start.37
  191.5 1.9 collective-permute-start.30
  193.5 1.9 collective-permute-start.38
  197.0 2.2 collective-permute-done.30
  200.2 1.9 collective-permute-start.31
  203.1 1.9 collective-permute-start.39
  208.4 74.7 %psum.28 = f32[32]{0:T(128)S(1)} all-reduce(f32[32]{0:T(128)S(1)} %concatenate.28), channel_id=1, replica_groups=mesh['ctx_0'=4,'ctx_1'=8,'ctx_2'=4,'ctx_3'=2] {'ctx_0'}, use_global_device_ids=true, to_apply=%region_24.25 | all-reduce | flops 32 | bytes 256 | tf_op jit(solution)/shard_map/psum | solution.py:24
  283.1 10.7 %psum.29 = f32[32]{0:T(128)S(1)} all-reduce(f32[32]{0:T(128)S(1)} %psum.28), channel_id=1, replica_groups=mesh['ctx_0'=4,'ctx_1'=8,'ctx_2'=4,'ctx_3'=2] {'ctx_1'}, use_global_device_ids=true, to_apply=%region_25.26 | all-reduce | flops 32 | bytes 256 | tf_op jit(solution)/shard_map/psum | solution.py:24
  293.8 6.0 %psum.30 = f32[32]{0:T(128)S(1)} all-reduce(f32[32]{0:T(128)S(1)} %psum.29), channel_id=1, replica_groups=mesh['ctx_0'=4,'ctx_1'=8,'ctx_2'=4,'ctx_3'=2] {'ctx_2'}, use_global_device_ids=true, to_apply=%region_26.27 | all-reduce | flops 32 | bytes 256 | tf_op jit(solution)/shard_map/psum | solution.py:24
  299.7 9.9 %psum.31 = f32[32]{0:T(128)} all-reduce(f32[32]{0:T(128)S(1)} %psum.30), channel_id=1, replica_groups=mesh['ctx_0'=4,'ctx_1'=8,'ctx_2'=4,'ctx_3'=2] {'ctx_3'}, use_global_device_ids=true, to_apply=%region_27.28 | all-reduce | flops 32 | bytes 256 | tf_op jit(solution)/shard_map/psum | solution.py:24
  (259 shorter events, 78.4 us)
Async XLA Ops:
  0.6 26.6 %copy-start.2 = (f32[32]{0:T(128)S(1)}, f32[32]{0:T(128)}, u32[]{:S(2)}) copy-start(f32[32]{0:T(128)} %param.11) | copy-start | bytes 388
  1.3 85.3 %copy-start.20 = (s32[128]{0:T(128)S(1)}, s32[128]{0:T(128)}, u32[]{:S(2)}) copy-start(s32[128]{0:T(128)} %param.10) | copy-start | bytes 1540
  1.3 12.3 %collective-permute-start.8 = (s32[128]{0:T(128)S(1)}, s32[128]{0:T(128)S(1)}, u32[]{:S(2)}, u32[]{:S(2)}) collective-permute-start(s32[128]{0:T(128)S(1)} %broadcast_add_fusion), channel_id=1, source_target_pairs={{0,1},{1,2},{2,3},{3,4},{4,5},{5,6},{6,7},{7,8},{8,9},{9,10},{10,1... | collective-permute-start | bytes 1544 | tf_op jit(solution)/shard_map/ppermute | solution.py:20
  7.1 39.0 %collective-permute-start.16 = (bf16[128,512]{0,1:T(8,128)(2,1)S(1)}, bf16[128,512]{0,1:T(8,128)(2,1)S(1)}, u32[]{:S(2)}, u32[]{:S(2)}) collective-permute-start(bf16[128,512]{0,1:T(8,128)(2,1)S(1)} %copy.13), channel_id=1, source_target_pairs={{0,1},{1,2},{2,3},{3,4},{4,5},{5,6},{6,7},{7,8},{8,9},{9,10},{10,1... | collective-permute-start | bytes 393224 | tf_op jit(solution)/shard_map/ppermute | solution.py:20
  10.0 15.2 %collective-permute-start = (bf16[128,512]{0,1:T(8,128)(2,1)S(1)}, bf16[128,512]{0,1:T(8,128)(2,1)S(1)}, u32[]{:S(2)}, u32[]{:S(2)}) collective-permute-start(bf16[128,512]{0,1:T(8,128)(2,1)S(1)} %copy.10), channel_id=1, source_target_pairs={{0,1},{1,2},{2,3},{3,4},{4,5},{5,6},{6,7},{7,8},{8,9},{9,10},{10,1... | collective-permute-start | bytes 393224 | tf_op jit(solution)/shard_map/ppermute | solution.py:20
  13.6 3.0 collective-permute-start.9
  16.7 4.8 %collective-permute-start.10 = (s32[128]{0:T(128)S(1)}, s32[128]{0:T(128)S(1)}, u32[]{:S(2)}, u32[]{:S(2)}) collective-permute-start(s32[128]{0:T(128)S(1)} %collective-permute-done.9), channel_id=1, source_target_pairs={{0,1},{1,2},{2,3},{3,4},{4,5},{5,6},{6,7},{7,8},{8,9},{9,10},{10,1... | collective-permute-start | bytes 1544 | tf_op jit(solution)/shard_map/ppermute | solution.py:20
  21.5 6.3 %collective-permute-start.11 = (s32[128]{0:T(128)S(1)}, s32[128]{0:T(128)S(1)}, u32[]{:S(2)}, u32[]{:S(2)}) collective-permute-start(s32[128]{0:T(128)S(1)} %collective-permute-done.10), channel_id=1, source_target_pairs={{0,1},{1,2},{2,3},{3,4},{4,5},{5,6},{6,7},{7,8},{8,9},{9,10},{10,1... | collective-permute-start | bytes 1544 | tf_op jit(solution)/shard_map/ppermute | solution.py:20
  25.3 23.7 %collective-permute-start.1 = (bf16[128,512]{0,1:T(8,128)(2,1)S(1)}, bf16[128,512]{0,1:T(8,128)(2,1)S(1)}, u32[]{:S(2)}, u32[]{:S(2)}) collective-permute-start(bf16[128,512]{0,1:T(8,128)(2,1)S(1)} %collective-permute-done), channel_id=1, source_target_pairs={{0,1},{1,2},{2,3},{3,4},{4,5},{5,6},{6,7},{7,8},{8,9},{9,10},{10,1... | collective-permute-start | bytes 393224 | tf_op jit(solution)/shard_map/ppermute | solution.py:20
  27.8 76.8 %copy-start.9 = (f32[4]{0:T(128)}, f32[4]{0:T(128)S(1)}, u32[]{:S(2)}) copy-start(f32[4]{0:T(128)S(1)} %get-tuple-element.30) | copy-start | bytes 52
  27.8 94.7 %copy-start.11 = (f32[4]{0:T(128)}, f32[4]{0:T(128)S(1)}, u32[]{:S(2)}) copy-start(f32[4]{0:T(128)S(1)} %get-tuple-element.27) | copy-start | bytes 52
  27.8 4.0 %collective-permute-start.12 = (s32[128]{0:T(128)S(1)}, s32[128]{0:T(128)S(1)}, u32[]{:S(2)}, u32[]{:S(2)}) collective-permute-start(s32[128]{0:T(128)S(1)} %collective-permute-done.11), channel_id=1, source_target_pairs={{0,1},{1,2},{2,3},{3,4},{4,5},{5,6},{6,7},{7,8},{8,9},{9,10},{10,1... | collective-permute-start | bytes 1544 | tf_op jit(solution)/shard_map/ppermute | solution.py:20
  31.8 4.8 %collective-permute-start.13 = (s32[128]{0:T(128)S(1)}, s32[128]{0:T(128)S(1)}, u32[]{:S(2)}, u32[]{:S(2)}) collective-permute-start(s32[128]{0:T(128)S(1)} %collective-permute-done.12), channel_id=1, source_target_pairs={{0,1},{1,2},{2,3},{3,4},{4,5},{5,6},{6,7},{7,8},{8,9},{9,10},{10,1... | collective-permute-start | bytes 1544 | tf_op jit(solution)/shard_map/ppermute | solution.py:20
  36.7 4.8 %collective-permute-start.14 = (s32[128]{0:T(128)S(1)}, s32[128]{0:T(128)S(1)}, u32[]{:S(2)}, u32[]{:S(2)}) collective-permute-start(s32[128]{0:T(128)S(1)} %collective-permute-done.13), channel_id=1, source_target_pairs={{0,1},{1,2},{2,3},{3,4},{4,5},{5,6},{6,7},{7,8},{8,9},{9,10},{10,1... | collective-permute-start | bytes 1544 | tf_op jit(solution)/shard_map/ppermute | solution.py:20
  41.5 11.6 %collective-permute-start.15 = (s32[128]{0:T(128)S(1)}, s32[128]{0:T(128)S(1)}, u32[]{:S(2)}, u32[]{:S(2)}) collective-permute-start(s32[128]{0:T(128)S(1)} %collective-permute-done.14), channel_id=1, source_target_pairs={{0,1},{1,2},{2,3},{3,4},{4,5},{5,6},{6,7},{7,8},{8,9},{9,10},{10,1... | collective-permute-start | bytes 1544 | tf_op jit(solution)/shard_map/ppermute | solution.py:20
  46.0 7.1 %collective-permute-start.17 = (bf16[128,512]{0,1:T(8,128)(2,1)S(1)}, bf16[128,512]{0,1:T(8,128)(2,1)S(1)}, u32[]{:S(2)}, u32[]{:S(2)}) collective-permute-start(bf16[128,512]{0,1:T(8,128)(2,1)S(1)} %collective-permute-done.16), channel_id=1, source_target_pairs={{0,1},{1,2},{2,3},{3,4},{4,5},{5,6},{6,7},{7,8},{8,9},{9,10},{10,1... | collective-permute-start | bytes 393224 | tf_op jit(solution)/shard_map/ppermute | solution.py:20
  48.9 8.3 %collective-permute-start.2 = (bf16[128,512]{0,1:T(8,128)(2,1)S(1)}, bf16[128,512]{0,1:T(8,128)(2,1)S(1)}, u32[]{:S(2)}, u32[]{:S(2)}) collective-permute-start(bf16[128,512]{0,1:T(8,128)(2,1)S(1)} %collective-permute-done.1), channel_id=1, source_target_pairs={{0,1},{1,2},{2,3},{3,4},{4,5},{5,6},{6,7},{7,8},{8,9},{9,10},{10,1... | collective-permute-start | bytes 393224 | tf_op jit(solution)/shard_map/ppermute | solution.py:20
  53.1 8.5 %collective-permute-start.18 = (bf16[128,512]{0,1:T(8,128)(2,1)S(1)}, bf16[128,512]{0,1:T(8,128)(2,1)S(1)}, u32[]{:S(2)}, u32[]{:S(2)}) collective-permute-start(bf16[128,512]{0,1:T(8,128)(2,1)S(1)} %collective-permute-done.17), channel_id=1, source_target_pairs={{0,1},{1,2},{2,3},{3,4},{4,5},{5,6},{6,7},{7,8},{8,9},{9,10},{10,1... | collective-permute-start | bytes 393224 | tf_op jit(solution)/shard_map/ppermute | solution.py:20
  57.2 10.6 %collective-permute-start.3 = (bf16[128,512]{0,1:T(8,128)(2,1)S(1)}, bf16[128,512]{0,1:T(8,128)(2,1)S(1)}, u32[]{:S(2)}, u32[]{:S(2)}) collective-permute-start(bf16[128,512]{0,1:T(8,128)(2,1)S(1)} %collective-permute-done.2), channel_id=1, source_target_pairs={{0,1},{1,2},{2,3},{3,4},{4,5},{5,6},{6,7},{7,8},{8,9},{9,10},{10,1... | collective-permute-start | bytes 393224 | tf_op jit(solution)/shard_map/ppermute | solution.py:20
  61.6 12.5 %collective-permute-start.19 = (bf16[128,512]{0,1:T(8,128)(2,1)S(1)}, bf16[128,512]{0,1:T(8,128)(2,1)S(1)}, u32[]{:S(2)}, u32[]{:S(2)}) collective-permute-start(bf16[128,512]{0,1:T(8,128)(2,1)S(1)} %collective-permute-done.18), channel_id=1, source_target_pairs={{0,1},{1,2},{2,3},{3,4},{4,5},{5,6},{6,7},{7,8},{8,9},{9,10},{10,1... | collective-permute-start | bytes 393224 | tf_op jit(solution)/shard_map/ppermute | solution.py:20
  67.8 8.2 %collective-permute-start.4 = (bf16[128,512]{0,1:T(8,128)(2,1)S(1)}, bf16[128,512]{0,1:T(8,128)(2,1)S(1)}, u32[]{:S(2)}, u32[]{:S(2)}) collective-permute-start(bf16[128,512]{0,1:T(8,128)(2,1)S(1)} %collective-permute-done.3), channel_id=1, source_target_pairs={{0,1},{1,2},{2,3},{3,4},{4,5},{5,6},{6,7},{7,8},{8,9},{9,10},{10,1... | collective-permute-start | bytes 393224 | tf_op jit(solution)/shard_map/ppermute | solution.py:20
  74.1 6.3 %collective-permute-start.20 = (bf16[128,512]{0,1:T(8,128)(2,1)S(1)}, bf16[128,512]{0,1:T(8,128)(2,1)S(1)}, u32[]{:S(2)}, u32[]{:S(2)}) collective-permute-start(bf16[128,512]{0,1:T(8,128)(2,1)S(1)} %collective-permute-done.19), channel_id=1, source_target_pairs={{0,1},{1,2},{2,3},{3,4},{4,5},{5,6},{6,7},{7,8},{8,9},{9,10},{10,1... | collective-permute-start | bytes 393224 | tf_op jit(solution)/shard_map/ppermute | solution.py:20
  76.0 8.4 %collective-permute-start.5 = (bf16[128,512]{0,1:T(8,128)(2,1)S(1)}, bf16[128,512]{0,1:T(8,128)(2,1)S(1)}, u32[]{:S(2)}, u32[]{:S(2)}) collective-permute-start(bf16[128,512]{0,1:T(8,128)(2,1)S(1)} %collective-permute-done.4), channel_id=1, source_target_pairs={{0,1},{1,2},{2,3},{3,4},{4,5},{5,6},{6,7},{7,8},{8,9},{9,10},{10,1... | collective-permute-start | bytes 393224 | tf_op jit(solution)/shard_map/ppermute | solution.py:20
  80.4 6.3 %collective-permute-start.21 = (bf16[128,512]{0,1:T(8,128)(2,1)S(1)}, bf16[128,512]{0,1:T(8,128)(2,1)S(1)}, u32[]{:S(2)}, u32[]{:S(2)}) collective-permute-start(bf16[128,512]{0,1:T(8,128)(2,1)S(1)} %collective-permute-done.20), channel_id=1, source_target_pairs={{0,1},{1,2},{2,3},{3,4},{4,5},{5,6},{6,7},{7,8},{8,9},{9,10},{10,1... | collective-permute-start | bytes 393224 | tf_op jit(solution)/shard_map/ppermute | solution.py:20
  84.4 8.4 %collective-permute-start.6 = (bf16[128,512]{0,1:T(8,128)(2,1)S(1)}, bf16[128,512]{0,1:T(8,128)(2,1)S(1)}, u32[]{:S(2)}, u32[]{:S(2)}) collective-permute-start(bf16[128,512]{0,1:T(8,128)(2,1)S(1)} %collective-permute-done.5), channel_id=1, source_target_pairs={{0,1},{1,2},{2,3},{3,4},{4,5},{5,6},{6,7},{7,8},{8,9},{9,10},{10,1... | collective-permute-start | bytes 393224 | tf_op jit(solution)/shard_map/ppermute | solution.py:20
  86.6 8.3 %collective-permute-start.22 = (bf16[128,512]{0,1:T(8,128)(2,1)S(1)}, bf16[128,512]{0,1:T(8,128)(2,1)S(1)}, u32[]{:S(2)}, u32[]{:S(2)}) collective-permute-start(bf16[128,512]{0,1:T(8,128)(2,1)S(1)} %collective-permute-done.21), channel_id=1, source_target_pairs={{0,1},{1,2},{2,3},{3,4},{4,5},{5,6},{6,7},{7,8},{8,9},{9,10},{10,1... | collective-permute-start | bytes 393224 | tf_op jit(solution)/shard_map/ppermute | solution.py:20
  92.8 8.8 %collective-permute-start.7 = (bf16[128,512]{0,1:T(8,128)(2,1)S(1)}, bf16[128,512]{0,1:T(8,128)(2,1)S(1)}, u32[]{:S(2)}, u32[]{:S(2)}) collective-permute-start(bf16[128,512]{0,1:T(8,128)(2,1)S(1)} %collective-permute-done.6), channel_id=1, source_target_pairs={{0,1},{1,2},{2,3},{3,4},{4,5},{5,6},{6,7},{7,8},{8,9},{9,10},{10,1... | collective-permute-start | bytes 393224 | tf_op jit(solution)/shard_map/ppermute | solution.py:20
  95.0 8.3 %collective-permute-start.23 = (bf16[128,512]{0,1:T(8,128)(2,1)S(1)}, bf16[128,512]{0,1:T(8,128)(2,1)S(1)}, u32[]{:S(2)}, u32[]{:S(2)}) collective-permute-start(bf16[128,512]{0,1:T(8,128)(2,1)S(1)} %collective-permute-done.22), channel_id=1, source_target_pairs={{0,1},{1,2},{2,3},{3,4},{4,5},{5,6},{6,7},{7,8},{8,9},{9,10},{10,1... | collective-permute-start | bytes 393224 | tf_op jit(solution)/shard_map/ppermute | solution.py:20
  135.3 10.5 %collective-permute-start.24 = (f32[128,512]{0,1:T(8,128)S(1)}, f32[128,512]{0,1:T(8,128)S(1)}, u32[]{:S(2)}, u32[]{:S(2)}) collective-permute-start(f32[128,512]{0,1:T(8,128)S(1)} %slice.248), channel_id=1, source_target_pairs={{1,0},{2,1},{3,2},{4,3},{5,4},{6,5},{7,6},{8,7},{9,8},{10,9},{11,1... | collective-permute-start | bytes 786440 | tf_op jit(solution)/shard_map/ppermute | solution.py:20
  142.3 8.6 %collective-permute-start.32 = (f32[128,512]{0,1:T(8,128)}, f32[128,512]{0,1:T(8,128)S(1)}, u32[]{:S(2)}, u32[]{:S(2)}) collective-permute-start(f32[128,512]{0,1:T(8,128)} %slice.257), channel_id=1, source_target_pairs={{1,0},{2,1},{3,2},{4,3},{5,4},{6,5},{7,6},{8,7},{9,8},{10,9},{11,1... | collective-permute-start | bytes 786440 | tf_op jit(solution)/shard_map/ppermute | solution.py:20
  146.8 9.0 %collective-permute-start.25 = (f32[128,512]{0,1:T(8,128)S(1)}, f32[128,512]{0,1:T(8,128)S(1)}, u32[]{:S(2)}, u32[]{:S(2)}) collective-permute-start(f32[128,512]{0,1:T(8,128)S(1)} %slice_add_fusion.15), channel_id=1, source_target_pairs={{1,0},{2,1},{3,2},{4,3},{5,4},{6,5},{7,6},{8,7},{9,8},{10,9},{11,1... | collective-permute-start | bytes 786440 | tf_op jit(solution)/shard_map/ppermute | solution.py:20
  151.6 7.9 %collective-permute-start.33 = (f32[128,512]{0,1:T(8,128)}, f32[128,512]{0,1:T(8,128)S(1)}, u32[]{:S(2)}, u32[]{:S(2)}) collective-permute-start(f32[128,512]{0,1:T(8,128)} %slice_add_fusion.7), channel_id=1, source_target_pairs={{1,0},{2,1},{3,2},{4,3},{5,4},{6,5},{7,6},{8,7},{9,8},{10,9},{11,1... | collective-permute-start | bytes 786440 | tf_op jit(solution)/shard_map/ppermute | solution.py:20
  156.7 7.8 %collective-permute-start.26 = (f32[128,512]{0,1:T(8,128)S(1)}, f32[128,512]{0,1:T(8,128)S(1)}, u32[]{:S(2)}, u32[]{:S(2)}) collective-permute-start(f32[128,512]{0,1:T(8,128)S(1)} %slice_add_fusion.14), channel_id=1, source_target_pairs={{1,0},{2,1},{3,2},{4,3},{5,4},{6,5},{7,6},{8,7},{9,8},{10,9},{11,1... | collective-permute-start | bytes 786440 | tf_op jit(solution)/shard_map/ppermute | solution.py:20
  159.5 7.9 %collective-permute-start.34 = (f32[128,512]{0,1:T(8,128)S(1)}, f32[128,512]{0,1:T(8,128)S(1)}, u32[]{:S(2)}, u32[]{:S(2)}) collective-permute-start(f32[128,512]{0,1:T(8,128)S(1)} %slice_add_fusion.6), channel_id=1, source_target_pairs={{1,0},{2,1},{3,2},{4,3},{5,4},{6,5},{7,6},{8,7},{9,8},{10,9},{11,1... | collective-permute-start | bytes 786440 | tf_op jit(solution)/shard_map/ppermute | solution.py:20
  165.5 7.7 %collective-permute-start.27 = (f32[128,512]{0,1:T(8,128)S(1)}, f32[128,512]{0,1:T(8,128)S(1)}, u32[]{:S(2)}, u32[]{:S(2)}) collective-permute-start(f32[128,512]{0,1:T(8,128)S(1)} %slice_add_fusion.13), channel_id=1, source_target_pairs={{1,0},{2,1},{3,2},{4,3},{5,4},{6,5},{7,6},{8,7},{9,8},{10,9},{11,1... | collective-permute-start | bytes 786440 | tf_op jit(solution)/shard_map/ppermute | solution.py:20
  167.5 8.6 %collective-permute-start.35 = (f32[128,512]{0,1:T(8,128)S(1)}, f32[128,512]{0,1:T(8,128)S(1)}, u32[]{:S(2)}, u32[]{:S(2)}) collective-permute-start(f32[128,512]{0,1:T(8,128)S(1)} %slice_add_fusion.5), channel_id=1, source_target_pairs={{1,0},{2,1},{3,2},{4,3},{5,4},{6,5},{7,6},{8,7},{9,8},{10,9},{11,1... | collective-permute-start | bytes 786440 | tf_op jit(solution)/shard_map/ppermute | solution.py:20
  174.2 7.7 %collective-permute-start.28 = (f32[128,512]{0,1:T(8,128)S(1)}, f32[128,512]{0,1:T(8,128)S(1)}, u32[]{:S(2)}, u32[]{:S(2)}) collective-permute-start(f32[128,512]{0,1:T(8,128)S(1)} %slice_add_fusion.12), channel_id=1, source_target_pairs={{1,0},{2,1},{3,2},{4,3},{5,4},{6,5},{7,6},{8,7},{9,8},{10,9},{11,1... | collective-permute-start | bytes 786440 | tf_op jit(solution)/shard_map/ppermute | solution.py:20
  176.1 8.7 %collective-permute-start.36 = (f32[128,512]{0,1:T(8,128)S(1)}, f32[128,512]{0,1:T(8,128)S(1)}, u32[]{:S(2)}, u32[]{:S(2)}) collective-permute-start(f32[128,512]{0,1:T(8,128)S(1)} %slice_add_fusion.4), channel_id=1, source_target_pairs={{1,0},{2,1},{3,2},{4,3},{5,4},{6,5},{7,6},{8,7},{9,8},{10,9},{11,1... | collective-permute-start | bytes 786440 | tf_op jit(solution)/shard_map/ppermute | solution.py:20
  182.8 22.9 %copy-start.17 = (f32[4]{0:T(128)S(1)}, f32[4]{0:T(128)}, u32[]{:S(2)}) copy-start(f32[4]{0:T(128)} %get-tuple-element.48) | copy-start | bytes 52
  182.8 22.9 %copy-start.16 = (f32[4]{0:T(128)S(1)}, f32[4]{0:T(128)}, u32[]{:S(2)}) copy-start(f32[4]{0:T(128)} %get-tuple-element.49) | copy-start | bytes 52
  182.9 22.9 %copy-start.19 = (f32[4]{0:T(128)S(1)}, f32[4]{0:T(128)}, u32[]{:S(2)}) copy-start(f32[4]{0:T(128)} %get-tuple-element.50) | copy-start | bytes 52
  182.9 22.9 %copy-start.18 = (f32[4]{0:T(128)S(1)}, f32[4]{0:T(128)}, u32[]{:S(2)}) copy-start(f32[4]{0:T(128)} %get-tuple-element.51) | copy-start | bytes 52
  182.9 7.7 %collective-permute-start.29 = (f32[128,512]{0,1:T(8,128)S(1)}, f32[128,512]{0,1:T(8,128)S(1)}, u32[]{:S(2)}, u32[]{:S(2)}) collective-permute-start(f32[128,512]{0,1:T(8,128)S(1)} %slice_add_fusion.11), channel_id=1, source_target_pairs={{1,0},{2,1},{3,2},{4,3},{5,4},{6,5},{7,6},{8,7},{9,8},{10,9},{11,1... | collective-permute-start | bytes 786440 | tf_op jit(solution)/shard_map/ppermute | solution.py:20
  184.8 8.6 %collective-permute-start.37 = (f32[128,512]{0,1:T(8,128)S(1)}, f32[128,512]{0,1:T(8,128)S(1)}, u32[]{:S(2)}, u32[]{:S(2)}) collective-permute-start(f32[128,512]{0,1:T(8,128)S(1)} %slice_add_fusion.3), channel_id=1, source_target_pairs={{1,0},{2,1},{3,2},{4,3},{5,4},{6,5},{7,6},{8,7},{9,8},{10,9},{11,1... | collective-permute-start | bytes 786440 | tf_op jit(solution)/shard_map/ppermute | solution.py:20
  191.5 7.7 %collective-permute-start.30 = (f32[128,512]{0,1:T(8,128)S(1)}, f32[128,512]{0,1:T(8,128)S(1)}, u32[]{:S(2)}, u32[]{:S(2)}) collective-permute-start(f32[128,512]{0,1:T(8,128)S(1)} %slice_add_fusion.10), channel_id=1, source_target_pairs={{1,0},{2,1},{3,2},{4,3},{5,4},{6,5},{7,6},{8,7},{9,8},{10,9},{11,1... | collective-permute-start | bytes 786440 | tf_op jit(solution)/shard_map/ppermute | solution.py:20
  193.5 8.6 %collective-permute-start.38 = (f32[128,512]{0,1:T(8,128)S(1)}, f32[128,512]{0,1:T(8,128)}, u32[]{:S(2)}, u32[]{:S(2)}) collective-permute-start(f32[128,512]{0,1:T(8,128)S(1)} %slice_add_fusion.2), channel_id=1, source_target_pairs={{1,0},{2,1},{3,2},{4,3},{5,4},{6,5},{7,6},{8,7},{9,8},{10,9},{11,1... | collective-permute-start | bytes 786440 | tf_op jit(solution)/shard_map/ppermute | solution.py:20
  200.2 109.4 %collective-permute-start.31 = (f32[128,512]{0,1:T(8,128)S(1)}, f32[128,512]{0,1:T(8,128)S(1)}, u32[]{:S(2)}, u32[]{:S(2)}) collective-permute-start(f32[128,512]{0,1:T(8,128)S(1)} %slice_add_fusion.9), channel_id=1, source_target_pairs={{1,0},{2,1},{3,2},{4,3},{5,4},{6,5},{7,6},{8,7},{9,8},{10,9},{11,1... | collective-permute-start | bytes 786440 | tf_op jit(solution)/shard_map/ppermute | solution.py:20
  203.1 108.2 %collective-permute-start.39 = (f32[128,512]{0,1:T(8,128)S(1)}, f32[128,512]{0,1:T(8,128)S(1)}, u32[]{:S(2)}, u32[]{:S(2)}) collective-permute-start(f32[128,512]{0,1:T(8,128)S(1)} %slice_add_fusion.1), channel_id=1, source_target_pairs={{1,0},{2,1},{3,2},{4,3},{5,4},{6,5},{7,6},{8,7},{9,8},{10,9},{11,1... | collective-permute-start | bytes 786440 | tf_op jit(solution)/shard_map/ppermute | solution.py:20
  (13 other events, 38.4 us)
where the time goes:
time: 314 us; the launch traced here: 312 us
  starting transfers between devices  123 us (39%)
  blocking collectives  101 us (32%)
  local copies, waits for them, and re-layouts  26.4 us (8%)
  matrix products  25.9 us (8%)
  other arithmetic  23.3 us (7%)
  waiting for transfers between devices  10.2 us (3%)
    ppermute x40, starting transfers between devices, passed_along(): return lax.ppermute(block, axis, route)  123 us
    psum x4, blocking collectives, by_axis(): return functools.reduce(lax.psum, axes, value)  101 us
    unnamed x77, local copies, waits for them, and re-layouts  12.9 us
    ppermute x40, waiting for transfers between devices, passed_along(): return lax.ppermute(block, axis, route)  10.2 us
    reshape x8, local copies, waits for them, and re-layouts, per_device(): query_list.append(query_part.reshape(tok_rows, groups * HEAD_DIM))  7.35 us
    add x7, other arithmetic, per_device(): moved[0] + block_of(key_partial, distance)  6.85 us
  transfers between devices with their start and end apart: 40, of which 10 were waited for; matrix products, arithmetic and copies ran while one was open for 14% of the time, Pallas kernels for 0%

commit v1 on v0

v1 whole, which is shorter than its diff:
```python
import functools
import math

import jax
import jax.numpy as jnp
from jax import lax
from jax.experimental import pallas as pl
from jax.experimental.pallas import tpu as pltpu
from jax.sharding import PartitionSpec as P

KV_HEADS = 8
HEAD_DIM = 64
WINDOW = 1024
TOK = 128
CHIP = 2 * TOK
HOPS = WINDOW // CHIP
ROW = 4
SPAN = WINDOW + CHIP
HALF_KV = KV_HEADS // 2 * HEAD_DIM
SCALE = 1.0 / math.sqrt(HEAD_DIM)
EXP2_SCALE = SCALE * math.log2(math.e)
MASKED = -1e30
F32 = jnp.float32
BF16 = jnp.bfloat16


NT, NN = ((1,), (1,)), ((1,), (0,))


def dot(a, b, dims):
    return lax.dot_general(a, b, (dims, ((), ())), preferred_element_type=F32)


def mask_bias(place, chunk, own_chunk, hop):
    core, chip = place[0], place[1]
    key_seg = chunk[CHIP : CHIP + 16, :CHIP].astype(F32)[0:1]
    query_seg = own_chunk[CHIP : CHIP + 16, :CHIP].astype(F32)[0:1]
    key_seg = jnp.where(chip >= hop, key_seg, -1.0)
    column = jnp.transpose(jnp.broadcast_to(key_seg, (TOK, CHIP)))
    allowed = jnp.concatenate([column, column], 1) == query_seg
    if hop in (0, HOPS):
        query_pos = lax.broadcasted_iota(jnp.int32, (CHIP, CHIP), 1) ^ (core * TOK)
        key_pos = lax.broadcasted_iota(jnp.int32, (CHIP, CHIP), 0) ^ (core * TOK)
        inside = key_pos <= query_pos if hop == 0 else key_pos > query_pos
        allowed = allowed & inside
    return jnp.where(allowed, 0.0, MASKED)


def two_heads(place, own, peer, tile, p):
    at = tile * 512 + p * 128
    ours = own[:, pl.ds(pl.multiple_of(place[0] * 1024 + at, 128), 128)]
    theirs = peer[:, pl.ds(pl.multiple_of(at, 128), 128)]
    pair = jnp.concatenate([ours, theirs], 0).astype(F32)
    turned = pltpu.roll(pair, HEAD_DIM, 1)
    half = p // 2
    wanted = lax.broadcasted_iota(jnp.int32, (CHIP, 128), 1) // HEAD_DIM == half
    return [
        jnp.where(wanted, pair if half == e else turned, 0.0).astype(BF16) for e in range(2)
    ]


def lane_tile(tile, first_lane=0):
    return pl.ds(pl.multiple_of(first_lane + tile * 128, 128), 128)


def stats_kernel(
    hop, last, place, sinks, q_own, q_peer, g_own, g_peer, chunk, own_chunk, *refs
):
    before, after, bias = refs[:3], refs[3:-1], refs[-1]
    if hop == 0:
        before, after = None, refs[:-1]
    core = place[0]
    bias[...] = mask_bias(place, chunk, own_chunk, hop)

    def of_tile(tile, carry):
        key_tile = chunk[0:CHIP, lane_tile(tile)]
        value_tile = chunk[0:CHIP, lane_tile(tile, HALF_KV)]
        for p in range(4):
            query = two_heads(place, q_own, q_peer, tile, p)
            grad = two_heads(place, g_own, g_peer, tile, p)
            for e in range(2):
                head = tile * 8 + 2 * p + e
                at = pl.ds(head, 1)
                sink = sinks[core * 16 + head] * (1.0 / SCALE)
                s = dot(key_tile, query[e], NT) + bias[...]
                dp = dot(value_tile, grad[e], NT)
                old = jnp.full((1, CHIP), sink, F32) if hop == 0 else before[0][at, :]
                top = jnp.maximum(old, jnp.max(s, 0, keepdims=True))
                ex = jnp.exp2((s - top) * EXP2_SCALE)
                fade = jnp.exp2((old - top) * EXP2_SCALE)
                denom = jnp.sum(ex, 0, keepdims=True)
                weighed = jnp.sum(ex * dp, 0, keepdims=True)
                if hop == 0:
                    denom = denom + fade
                else:
                    denom = denom + before[1][at, :] * fade
                    weighed = weighed + before[2][at, :] * fade
                after[0][at, :] = top
                if last:
                    share = 1.0 / denom
                    delta = weighed * share
                    after[1][at, :] = share
                    after[2][at, :] = delta
                    after[3][at, :] = -jnp.exp2((sink - top) * EXP2_SCALE) * share * delta
                else:
                    after[1][at, :] = denom
                    after[2][at, :] = weighed
        return carry

    lax.fori_loop(0, 2, of_tile, 0)


def parts_kernel(
    hop, tiles, place, q_own, q_peer, g_own, g_peer, chunk, own_chunk, tops, shares, deltas, *refs
):
    bias, keys_t, weight, dscore, query_all, grad_all = refs[-6:]
    dq_in = None if hop == HOPS else refs[0]
    outs = refs[:-6] if hop == HOPS else refs[1:-6]
    kv_out = outs[0]
    base, width = tiles[0], 128 * len(tiles)
    bias[...] = mask_bias(place, chunk, own_chunk, hop)
    keys_t[...] = jnp.transpose(chunk[0:CHIP, 0:CHIP].astype(F32)).astype(BF16)

    def of_tile(tile, carry):
        key_tile = chunk[0:CHIP, lane_tile(tile)]
        value_tile = chunk[0:CHIP, lane_tile(tile, HALF_KV)]
        for p in range(4):
            query = two_heads(place, q_own, q_peer, tile, p)
            grad = two_heads(place, g_own, g_peer, tile, p)
            for e in range(2):
                at = pl.ds(tile * 8 + 2 * p + e, 1)
                span = slice((2 * p + e) * CHIP, (2 * p + e + 1) * CHIP)
                query_all[span, :] = query[e]
                grad_all[span, :] = grad[e]
                s = dot(key_tile, query[e], NT) + bias[...]
                dp = dot(value_tile, grad[e], NT)
                prob = jnp.exp2((s - tops[at, :]) * EXP2_SCALE) * shares[at, :]
                weight[:, span] = prob.astype(BF16)
                dscore[:, span] = (prob * (dp - deltas[at, :])).astype(BF16)
        value_part = dot(weight[...], grad_all[...], NN)
        key_part = dot(dscore[...], query_all[...], NN) * SCALE
        kv_out[:, lane_tile(tile - base)] = key_part.astype(kv_out.dtype)
        kv_out[:, lane_tile(tile - base, width)] = value_part.astype(kv_out.dtype)
        for group in range(2):
            key_rows = pl.ds(
                pl.multiple_of((2 * tile + group) * HEAD_DIM, HEAD_DIM), HEAD_DIM
            )
            g = 2 * (tile - base) + group
            rows = pl.ds(pl.multiple_of(g * HEAD_DIM, HEAD_DIM), HEAD_DIM)
            dq_t = dot(keys_t[key_rows, :], dscore[:, group * 1024 : (group + 1) * 1024], NN)
            if dq_in is not None:
                dq_t = dq_t + dq_in[rows, :]
            if hop > 0:
                outs[1][rows, :] = dq_t
            else:
                for pair in range(2):
                    two = jnp.concatenate(
                        [
                            dq_t[:, (2 * pair + e) * CHIP : (2 * pair + e + 1) * CHIP]
                            for e in range(2)
                        ],
                        0,
                    )
                    dq = (jnp.transpose(two) * SCALE).astype(BF16)
                    lanes = lane_tile(2 * g + pair)
                    outs[1][:, lanes] = dq[:TOK]
                    outs[2][:, lanes] = dq[TOK:]
        return carry

    if len(tiles) == 2:
        lax.fori_loop(0, 2, of_tile, 0)
    else:
        of_tile(base, 0)


def pack_kernel(place, keys, values, segment, queries, grads, own, send, tokens):
    core = place[0]

    def half(ref, which, width):
        return ref[:, pl.ds(pl.multiple_of(which * width, width), width)]

    marks = jnp.broadcast_to(segment[...], (16, TOK)).astype(F32).astype(BF16)
    for out, which in ((own, core), (send, 1 - core)):
        out[:TOK, :HALF_KV] = half(keys, which, HALF_KV)
        out[:TOK, HALF_KV:] = half(values, which, HALF_KV)
        for lane in range(0, 2 * HALF_KV, TOK):
            out[TOK:, lane : lane + TOK] = marks
    tokens[:TOK, :] = half(queries, 1 - core, 1024)
    tokens[TOK:, :] = half(grads, 1 - core, 1024)


def join_kernel(place, mine, theirs, *outs):
    core = place[0]
    width = mine.shape[1] // len(outs)
    for n, out in enumerate(outs):
        for which, part in ((core, mine), (1 - core, theirs)):
            at = pl.ds(pl.multiple_of(which * width, width), width)
            out[:, at] = part[:, n * width : (n + 1) * width]


SMEM = pl.BlockSpec(memory_space=pltpu.SMEM)
VMEM = pl.BlockSpec(memory_space=pltpu.VMEM)
STAT = jax.ShapeDtypeStruct((16, CHIP), F32)


def run(kernel, name, n_scalars, operands, out_shape, scratch, flops, interpret):
    n_arrays = len(operands) - n_scalars
    return pl.pallas_call(
        kernel,
        name=name,
        in_specs=[SMEM] * n_scalars + [VMEM] * n_arrays,
        out_specs=[VMEM] * len(out_shape),
        out_shape=out_shape,
        scratch_shapes=scratch,
        compiler_params=pltpu.CompilerParams(vmem_limit_bytes=32 << 20),
        cost_estimate=pl.CostEstimate(flops=flops, transcendentals=0, bytes_accessed=1 << 20),
        interpret=interpret,
    )(*operands)


def stats_of(hop, last, place, sinks, tokens, chunk, own_chunk, before, interpret):
    return run(
        functools.partial(stats_kernel, hop, last), f"stats_{hop}", 2,
        (place, sinks, *tokens, chunk, own_chunk, *before),
        [STAT] * (4 if last else 3),
        [pltpu.VMEM((CHIP, CHIP), F32)], 2 << 30, interpret,
    )


def parts_of(hop, tiles, place, tokens, chunk, own_chunk, stats, dq, interpret):
    width = 128 * len(tiles)
    kv = jax.ShapeDtypeStruct((CHIP, 2 * width), BF16 if hop else F32)
    if hop:
        dq_shapes = [jax.ShapeDtypeStruct((width, 1024), F32)]
    else:
        dq_shapes = [jax.ShapeDtypeStruct((TOK, 4 * width), BF16)] * 2
    return run(
        functools.partial(parts_kernel, hop, tiles), f"parts_{hop}_{tiles[0]}", 1,
        (place, *tokens, chunk, own_chunk, *stats, *dq),
        [kv] + dq_shapes,
        [
            pltpu.VMEM((CHIP, CHIP), F32),
            pltpu.VMEM((CHIP, CHIP), BF16),
            pltpu.VMEM((CHIP, 8 * CHIP), BF16),
            pltpu.VMEM((CHIP, 8 * CHIP), BF16),
            pltpu.VMEM((8 * CHIP, 128), BF16),
            pltpu.VMEM((8 * CHIP, 128), BF16),
        ],
        3 << 30, interpret,
    )


def packed(place, key_heads, value_heads, segment, queries, out_grad, interpret):
    rows = jax.ShapeDtypeStruct((TOK + 16, 2 * HALF_KV), BF16)
    return run(
        pack_kernel, "pack", 1,
        (place, key_heads, value_heads, segment[None, :], queries, out_grad),
        [rows, rows, jax.ShapeDtypeStruct((2 * TOK, 1024), BF16)], [], 1 << 20, interpret,
    )


def joined(place, mine, theirs, outs, interpret):
    width = mine.shape[1] // outs
    shape = jax.ShapeDtypeStruct((TOK, 2 * width), BF16)
    return run(
        join_kernel, "join", 1, (place, mine, theirs), [shape] * outs, [], 1 << 20, interpret
    )


def per_device(count, interpret, queries, key_heads, value_heads, out_grad, segment, sink_logits):
    index = lax.axis_index("ctx")
    core, chip = index % 2, index // 2
    first = core == 0

    def sent(block, route):
        return lax.ppermute(block, "ctx", route)

    def shifted(block, chips):
        return sent(block, [(i, (i + 2 * chips) % count) for i in range(count)])

    def crossed(block, bit):
        return lax.ppermute(block, "ctx", [(i, i ^ bit) for i in range(count)])

    def in_row(i, hop):
        return i // 8 * 8 + (i // 2 + hop) % ROW * 2 + i % 2

    place = jnp.stack([core, chip]).astype(jnp.int32)
    own, kv_send, tokens_send = packed(
        place, key_heads, value_heads, segment, queries, out_grad, interpret
    )
    came = crossed(kv_send, 1)
    marks = jnp.concatenate(
        [own[TOK:, :TOK], came[TOK:, TOK:CHIP], own[TOK:, CHIP:]], 1
    )
    chunk = jnp.concatenate([own[:TOK], came[:TOK], marks], 0)
    chunks = {0: chunk, HOPS: shifted(chunk, HOPS)}
    both = crossed(tokens_send, 1)
    tokens = (queries, both[:TOK], out_grad, both[TOK:])
    stats = stats_of(
        0, False, place, sink_logits, tokens, chunk, chunk, (), interpret
    )
    *stats, chunks[HOPS] = lax.optimization_barrier((*stats, chunks[HOPS]))
    for hop in range(1, HOPS):
        within = chip % ROW + hop < ROW
        chunks[hop] = sent(
            jnp.where(within, chunk, chunks[HOPS]), [(i, in_row(i, hop)) for i in range(count)]
        )
    for hop in (HOPS, 1, 2, 3):
        stats = stats_of(
            hop, hop == 3, place, sink_logits, tokens, chunks[hop], chunk, stats, interpret
        )
    sink_half = jnp.sum(stats[3], -1)
    zeros = jnp.zeros_like(sink_half)
    sink_grad = jnp.where(
        first, jnp.concatenate([sink_half, zeros]), jnp.concatenate([zeros, sink_half])
    )
    bits = [1 << n for n in range(count.bit_length() - 1)]

    def widened(value):
        return value + crossed(value, bits.pop(0)) if bits else value

    *stats, sink_grad = lax.optimization_barrier((*stats[:3], widened(sink_grad)))
    dq, came_back, totals, dq_parts = {}, {}, [], []
    tile_sets = {4: ((0, 1),), 3: ((0, 1),), 2: ((0, 1),), 1: ((0,), (1,)), 0: ((0,), (1,))}
    for hop in range(HOPS, -1, -1):
        pieces = []
        for tiles in tile_sets[hop]:
            if len(tiles) == 1 and len(dq) == 1:
                whole = dq[(0, 1)]
                dq = {(0,): whole[:128], (1,): whole[128:]}
            before = [dq[tiles]] if tiles in dq else []
            piece, *after = parts_of(
                hop, tiles, place, tokens, chunks[hop], chunk, stats, before, interpret
            )
            pieces.append(piece)
            if hop == 0:
                dq_parts.append(after)
                if tiles == (0,):
                    sink_grad, dq[(1,)] = lax.optimization_barrier(
                        (widened(sink_grad), dq[(1,)])
                    )
                continue
            dq[tiles] = after[0]
            if tiles == tile_sets[hop][-1]:
                if len(pieces) == 2:
                    piece = jnp.concatenate(
                        [x[:, :128] for x in pieces] + [x[:, 128:] for x in pieces], 1
                    )
                came_back[hop] = shifted(piece, -hop)
            sink_grad = widened(sink_grad)
            tied = [n for n in came_back if n == hop + 1]
            keys = list(dq)
            flat = lax.optimization_barrier(
                (sink_grad, *[dq[n] for n in keys], *[came_back[n] for n in tied])
            )
            sink_grad = flat[0]
            dq = dict(zip(keys, flat[1:]))
            came_back.update(zip(tied, flat[1 + len(keys) :]))
        if hop == 0:
            totals = pieces
    dq_own = jnp.concatenate([x[0] for x in dq_parts], 1)
    dq_peer = jnp.concatenate([x[1] for x in dq_parts], 1)
    (query_grad,) = joined(place, dq_own, crossed(dq_peer, 1), 1, interpret)
    total = jnp.concatenate([x[:, :128] for x in totals] + [x[:, 128:] for x in totals], 1)
    for part in came_back.values():
        total = total + part.astype(F32)
    total = total.astype(BF16)
    key_grad, value_grad = joined(place, total[:TOK], crossed(total[TOK:], 1), 2, interpret)
    while bits:
        sink_grad = widened(sink_grad)
    return query_grad, key_grad, value_grad, sink_grad


def solution(mesh, interpret=False):
    rows = P("ctx", None)
    return jax.shard_map(
        functools.partial(per_device, mesh.size, interpret),
        mesh=mesh,
        in_specs=(rows, rows, rows, rows, P("ctx"), P()),
        out_specs=(rows, rows, rows, P()),
        check_vma=False,
    )
```

time: 314 us -> 103 us (0.33)
  blocking collectives: 101 us -> 0 us
  starting transfers between devices: 123 us -> 33.4 us
  Pallas kernels: 0 us -> 37.1 us
  matrix products: 25.9 us -> 0 us
  other arithmetic: 23.3 us -> 2.1 us
  local copies, waits for them, and re-layouts: 26.4 us -> 5.84 us
  waiting for transfers between devices: 10.2 us -> 23.1 us
    psum x4 -> x0, blocking collectives: 101 us -> none  [by_axis(): return functools.reduce(lax.psum, axes, value)]
    ppermute x40 -> x20, starting transfers between devices: 123 us -> 33.4 us  [the longest x8 19.7 us: sent(): return lax.ppermute(block, 'ctx', route)]
    pallas_call x0 -> x15, Pallas kernels: none -> 37.1 us  [run(): pl.pallas_call(kernel, name=name, in_specs=[SMEM] * n_scalars + [VMEM] *...]
    dot_general x40 -> x0, matrix products: 23.2 us -> none  [the longest x8 5.96 us: group_grads(): jnp.einsum('gbl,ld->bgd', dscore, key_group, preferred_element_type=jnp.f...]
    ppermute x40 -> x20, waiting for transfers between devices: 10.2 us -> 23.1 us  [the longest x8 15.2 us: sent(): return lax.ppermute(block, 'ctx', route)]
    add x24 -> x8, other arithmetic: 9.97 us -> 0.61 us  [widened(): return value + crossed(value, bits.pop(0)) if bits else value]
    reshape x8 -> x0, local copies, waits for them, and re-layouts: 7.35 us -> none  [per_device(): query_list.append(query_part.reshape(tok_rows, groups * HEAD_DIM))]
    unnamed x77 -> x16, local copies, waits for them, and re-layouts: 12.9 us -> 5.58 us
  transfers between devices with their start and end apart: 40 -> 20, of which waited for: 10 -> 9; matrix products, arithmetic and copies ran while one was open for 14% -> 1% of each run, Pallas kernels for 0% -> 32%
where the time goes in v1:
time: 103 us
  Pallas kernels  37.1 us (36%)
  starting transfers between devices  33.4 us (32%)
  waiting for transfers between devices  23.1 us (22%)
  local copies, waits for them, and re-layouts  5.84 us (6%)
  other arithmetic  2.1 us (2%)
    pallas_call x15, Pallas kernels, run(): pl.pallas_call(kernel, name=name, in_specs=[SMEM] * n_scalars + [VMEM] *...  37.1 us
    ppermute x8, starting transfers between devices, sent(): return lax.ppermute(block, 'ctx', route)  19.7 us
    ppermute x8, waiting for transfers between devices, sent(): return lax.ppermute(block, 'ctx', route)  15.2 us
    ppermute x12, starting transfers between devices, crossed(): return lax.ppermute(block, 'ctx', [(i, i ^ bit) for i in range(count)])  13.8 us
    ppermute x12, waiting for transfers between devices, crossed(): return lax.ppermute(block, 'ctx', [(i, i ^ bit) for i in range(count)])  7.91 us
    unnamed x16, local copies, waits for them, and re-layouts  5.58 us
  transfers between devices with their start and end apart: 20, of which 9 were waited for; matrix products, arithmetic and copies ran while one was open for 1% of the time, Pallas kernels for 32%

profile of v1, /device:TPU:1, one launch (start us, length us, event | category | flops | bytes accessed | tf_op | source)
XLA Modules:
  0.0 102.6 jit_solution(15132267114213721332)
XLA Ops:
  0.7 0.7 copy-done.6
  1.4 1.0 %copy-done = bf16[128,2048]{1,0:T(8,128)(2,1)S(1)} copy-done((bf16[128,2048]{1,0:T(8,128)(2,1)S(1)}, bf16[128,2048]{1,0:T(8,128)(2,1)}, u32[]{:S(2)}) %copy-start) | copy-done | bytes 524312
  2.4 1.0 %copy-done.2 = bf16[128,2048]{1,0:T(8,128)(2,1)S(1)} copy-done((bf16[128,2048]{1,0:T(8,128)(2,1)S(1)}, bf16[128,2048]{1,0:T(8,128)(2,1)}, u32[]{:S(2)}) %copy-start.2) | copy-done | bytes 524312
  3.5 0.9 copy-done.4
  4.4 0.9 copy-done.5
  5.3 0.6 pack.1
  5.9 3.3 %collective-permute-start = (bf16[256,1024]{1,0:T(8,128)(2,1)S(1)}, bf16[256,1024]{1,0:T(8,128)(2,1)S(1)}, u32[]{:S(2)}, u32[]{:S(2)}) collective-permute-start(bf16[256,1024]{1,0:T(8,128)(2,1)S(1)} %get-tuple-element.67), channel_id=1, source_target_pairs={{0,1},{1,0},{2,3},{3,2},{4,5},{5,4},{6,7},{7,6},{8,9},{9,8},{10,11... | collective-permute-start | bytes 1572872 | tf_op jit(solution)/shard_map/ppermute | solution.py:282
  9.3 1.6 %collective-permute-done.1 = bf16[144,512]{1,0:T(8,128)(2,1)S(1)} collective-permute-done((bf16[144,512]{1,0:T(8,128)(2,1)S(1)}, bf16[144,512]{1,0:T(8,128)(2,1)S(1)}, u32[]{:S(2)}, u32[]{:S(2)}) %collective-permute-start.1) | collective-permute-done | bytes 147488 | tf_op jit(solution)/shard_map/ppermute | solution.py:282
  11.2 0.9 copy-done.1
  12.0 0.2 copy-done.3
  12.2 2.6 %stats_0.1 = (f32[16,256]{1,0:T(8,128)S(1)}, f32[16,256]{1,0:T(8,128)S(1)}, f32[16,256]{1,0:T(8,128)S(1)}) custom-call(s32[2]{0:T(128)S(1)} %pad_add_fusion.place, f32[32]{0:T(128)S(1)} %copy-done.7, bf16[128,2048]{1,0:T(8,128)(2,1)S(1)} %copy-done.1, bf16[128,1024]{1,0:T(8,128)(2,1)S(1)} %get-tuple-element.136.q_peer, bf16[128,2048]{1,0:T(8,128)(2,1)S(1)} %copy-done.3, ...), custom_call_target="tpu_custom_call" | custom-call | flops 2147483648 | bytes 1048576 | tf_op jit(solution)/shard_map/stats_0/pallas_call | solution.py:208
  14.8 9.0 %collective-permute-done.2.chunk = bf16[272,512]{1,0:T(8,128)(2,1)S(1)} collective-permute-done((bf16[272,512]{1,0:T(8,128)(2,1)S(1)}, bf16[272,512]{1,0:T(8,128)(2,1)S(1)}, u32[]{:S(2)}, u32[]{:S(2)}) %collective-permute-start.2) | collective-permute-done | bytes 278560 | tf_op jit(solution)/shard_map/ppermute | solution.py:276
  23.9 1.0 broadcast_select_fusion
  24.8 1.3 %collective-permute-start.5 = (bf16[272,512]{1,0:T(8,128)(2,1)}, bf16[272,512]{1,0:T(8,128)(2,1)S(1)}, u32[]{:S(2)}, u32[]{:S(2)}) collective-permute-start(bf16[272,512]{1,0:T(8,128)(2,1)} %get-tuple-element.132), channel_id=1, source_target_pairs={{0,2},{1,3},{2,4},{3,5},{4,6},{5,7},{6,0},{7,1},{8,10},{9,11},{10,... | collective-permute-start | bytes 835592 | tf_op jit(solution)/shard_map/ppermute | solution.py:276
  26.1 2.6 %collective-permute-start.4 = (bf16[272,512]{1,0:T(8,128)(2,1)}, bf16[272,512]{1,0:T(8,128)(2,1)S(1)}, u32[]{:S(2)}, u32[]{:S(2)}) collective-permute-start(bf16[272,512]{1,0:T(8,128)(2,1)} %get-tuple-element.133), channel_id=1, source_target_pairs={{0,4},{1,5},{2,6},{3,7},{4,0},{5,1},{6,2},{7,3},{8,12},{9,13},{10,... | collective-permute-start | bytes 835592 | tf_op jit(solution)/shard_map/ppermute | solution.py:276
  28.7 1.1 %collective-permute-start.3 = (bf16[272,512]{1,0:T(8,128)(2,1)S(1)}, bf16[272,512]{1,0:T(8,128)(2,1)S(1)}, u32[]{:S(2)}, u32[]{:S(2)}) collective-permute-start(bf16[272,512]{1,0:T(8,128)(2,1)S(1)} %get-tuple-element.134), channel_id=1, source_target_pairs={{0,6},{1,7},{2,0},{3,1},{4,2},{5,3},{6,4},{7,5},{8,14},{9,15},{10,... | collective-permute-start | bytes 835592 | tf_op jit(solution)/shard_map/ppermute | solution.py:276
  29.8 2.7 %stats_4.1 = (f32[16,256]{1,0:T(8,128)S(1)}, f32[16,256]{1,0:T(8,128)S(1)}, f32[16,256]{1,0:T(8,128)S(1)}) custom-call(s32[2]{0:T(128)S(1)} %pad_add_fusion.place, f32[32]{0:T(128)S(1)} %copy-done.7, bf16[128,2048]{1,0:T(8,128)(2,1)S(1)} %copy-done.1, bf16[128,1024]{1,0:T(8,128)(2,1)S(1)} %get-tuple-element.136.q_peer, bf16[128,2048]{1,0:T(8,128)(2,1)S(1)} %copy-done.3, ...), custom_call_target="tpu_custom_call" | custom-call | flops 2147483648 | bytes 1048576 | tf_op jit(solution)/shard_map/stats_4/pallas_call | solution.py:208
  32.5 1.2 %collective-permute-done.5.chunk = bf16[272,512]{1,0:T(8,128)(2,1)S(1)} collective-permute-done((bf16[272,512]{1,0:T(8,128)(2,1)}, bf16[272,512]{1,0:T(8,128)(2,1)S(1)}, u32[]{:S(2)}, u32[]{:S(2)}) %collective-permute-start.5) | collective-permute-done | bytes 278560 | tf_op jit(solution)/shard_map/ppermute | solution.py:276
  33.7 2.7 %stats_1.1 = (f32[16,256]{1,0:T(8,128)S(1)}, f32[16,256]{1,0:T(8,128)S(1)}, f32[16,256]{1,0:T(8,128)S(1)}) custom-call(s32[2]{0:T(128)S(1)} %pad_add_fusion.place, f32[32]{0:T(128)S(1)} %copy-done.7, bf16[128,2048]{1,0:T(8,128)(2,1)S(1)} %copy-done.1, bf16[128,1024]{1,0:T(8,128)(2,1)S(1)} %get-tuple-element.136.q_peer, bf16[128,2048]{1,0:T(8,128)(2,1)S(1)} %copy-done.3, ...), custom_call_target="tpu_custom_call" | custom-call | flops 2147483648 | bytes 1048576 | tf_op jit(solution)/shard_map/stats_1/pallas_call | solution.py:208
  36.3 4.4 %collective-permute-done.4.chunk = bf16[272,512]{1,0:T(8,128)(2,1)S(1)} collective-permute-done((bf16[272,512]{1,0:T(8,128)(2,1)}, bf16[272,512]{1,0:T(8,128)(2,1)S(1)}, u32[]{:S(2)}, u32[]{:S(2)}) %collective-permute-start.4) | collective-permute-done | bytes 278560 | tf_op jit(solution)/shard_map/ppermute | solution.py:276
  40.7 2.7 %stats_2.1 = (f32[16,256]{1,0:T(8,128)S(1)}, f32[16,256]{1,0:T(8,128)S(1)}, f32[16,256]{1,0:T(8,128)S(1)}) custom-call(s32[2]{0:T(128)S(1)} %pad_add_fusion.place, f32[32]{0:T(128)S(1)} %copy-done.7, bf16[128,2048]{1,0:T(8,128)(2,1)S(1)} %copy-done.1, bf16[128,1024]{1,0:T(8,128)(2,1)S(1)} %get-tuple-element.136.q_peer, bf16[128,2048]{1,0:T(8,128)(2,1)S(1)} %copy-done.3, ...), custom_call_target="tpu_custom_call" | custom-call | flops 2147483648 | bytes 1048576 | tf_op jit(solution)/shard_map/stats_2/pallas_call | solution.py:208
  43.4 2.7 %stats_3.1 = (f32[16,256]{1,0:T(8,128)S(1)}, f32[16,256]{1,0:T(8,128)S(1)}, f32[16,256]{1,0:T(8,128)S(1)}, f32[16,256]{1,0:T(8,128)S(1)}) custom-call(s32[2]{0:T(128)S(1)} %pad_add_fusion.place, f32[32]{0:T(128)S(1)} %copy-done.7, bf16[128,2048]{1,0:T(8,128)(2,1)S(1)} %copy-done.1, bf16[128,1024]{1,0:T(8,128)(2,1)S(1)} %get-tuple-element.136.q_peer, ...), custom_call_target="tpu_custom_call" | custom-call | flops 2147483648 | bytes 1048576 | tf_op jit(solution)/shard_map/stats_3/pallas_call | solution.py:208
  46.3 1.8 %collective-permute-start.6 = (f32[32]{0:T(128)S(1)}, f32[32]{0:T(128)S(1)}, u32[]{:S(2)}, u32[]{:S(2)}) collective-permute-start(f32[32]{0:T(128)S(1)} %broadcast_select_fusion.3), channel_id=1, source_target_pairs={{0,1},{1,0},{2,3},{3,2},{4,5},{5,4},{6,7},{7,6},{8,9},{9,8},{10,11... | collective-permute-start | bytes 392 | tf_op jit(solution)/shard_map/ppermute | solution.py:282
  48.1 0.8 collective-permute-done.6
  49.0 0.2 collective-permute-start.7
  49.2 3.9 %parts_4_0.1 = (bf16[256,512]{1,0:T(8,128)(2,1)S(1)}, f32[256,1024]{1,0:T(8,128)S(1)}) custom-call(s32[2]{0:T(128)S(1)} %pad_add_fusion.place, bf16[128,2048]{1,0:T(8,128)(2,1)S(1)} %copy-done.1, bf16[128,1024]{1,0:T(8,128)(2,1)S(1)} %get-tuple-element.136.q_peer, bf16[128,2048]{1,0:T(8,128)(2,1)S(1)} %copy-done.3, ...), custom_call_target="tpu_custom_call" | custom-call | flops 3221225472 | bytes 1048576 | tf_op jit(solution)/shard_map/parts_4_0/pallas_call | solution.py:208
  53.2 1.2 %collective-permute-start.9 = (bf16[256,512]{1,0:T(8,128)(2,1)S(1)}, bf16[256,512]{1,0:T(8,128)(2,1)S(1)}, u32[]{:S(2)}, u32[]{:S(2)}) collective-permute-start(bf16[256,512]{1,0:T(8,128)(2,1)S(1)} %get-tuple-element.98), channel_id=1, source_target_pairs={{0,248},{1,249},{2,250},{3,251},{4,252},{5,253},{6,254},{7,255},{8... | collective-permute-start | bytes 786440 | tf_op jit(solution)/shard_map/ppermute | solution.py:276
  54.4 3.2 %collective-permute-start.8 = (f32[32]{0:T(128)S(1)}, f32[32]{0:T(128)S(1)}, u32[]{:S(2)}, u32[]{:S(2)}) collective-permute-start(f32[32]{0:T(128)S(1)} %add.65), channel_id=1, source_target_pairs={{0,4},{1,5},{2,6},{3,7},{4,0},{5,1},{6,2},{7,3},{8,12},{9,13},{10,... | collective-permute-start | bytes 392 | tf_op jit(solution)/shard_map/ppermute | solution.py:282
  57.5 3.9 %parts_3_0.1 = (bf16[256,512]{1,0:T(8,128)(2,1)S(1)}, f32[256,1024]{1,0:T(8,128)S(1)}) custom-call(s32[2]{0:T(128)S(1)} %pad_add_fusion.place, bf16[128,2048]{1,0:T(8,128)(2,1)S(1)} %copy-done.1, bf16[128,1024]{1,0:T(8,128)(2,1)S(1)} %get-tuple-element.136.q_peer, bf16[128,2048]{1,0:T(8,128)(2,1)S(1)} %copy-done.3, ...), custom_call_target="tpu_custom_call" | custom-call | flops 3221225472 | bytes 1048576 | tf_op jit(solution)/shard_map/parts_3_0/pallas_call | solution.py:208
  61.4 1.4 %collective-permute-start.11 = (bf16[256,512]{1,0:T(8,128)(2,1)S(1)}, bf16[256,512]{1,0:T(8,128)(2,1)S(1)}, u32[]{:S(2)}, u32[]{:S(2)}) collective-permute-start(bf16[256,512]{1,0:T(8,128)(2,1)S(1)} %get-tuple-element.102), channel_id=1, source_target_pairs={{0,250},{1,251},{2,252},{3,253},{4,254},{5,255},{6,0},{7,1},{8,2},... | collective-permute-start | bytes 786440 | tf_op jit(solution)/shard_map/ppermute | solution.py:276
  62.8 0.8 collective-permute-start.10
  63.6 3.9 %parts_2_0.1 = (bf16[256,512]{1,0:T(8,128)(2,1)S(1)}, f32[256,1024]{1,0:T(8,128)S(1)}) custom-call(s32[2]{0:T(128)S(1)} %pad_add_fusion.place, bf16[128,2048]{1,0:T(8,128)(2,1)S(1)} %copy-done.1, bf16[128,1024]{1,0:T(8,128)(2,1)S(1)} %get-tuple-element.136.q_peer, bf16[128,2048]{1,0:T(8,128)(2,1)S(1)} %copy-done.3, ...), custom_call_target="tpu_custom_call" | custom-call | flops 3221225472 | bytes 1048576 | tf_op jit(solution)/shard_map/parts_2_0/pallas_call | solution.py:208
  67.5 4.6 %collective-permute-start.13 = (bf16[256,512]{1,0:T(8,128)(2,1)S(1)}, bf16[256,512]{1,0:T(8,128)(2,1)S(1)}, u32[]{:S(2)}, u32[]{:S(2)}) collective-permute-start(bf16[256,512]{1,0:T(8,128)(2,1)S(1)} %get-tuple-element.106), channel_id=1, source_target_pairs={{0,252},{1,253},{2,254},{3,255},{4,0},{5,1},{6,2},{7,3},{8,4},{9,5... | collective-permute-start | bytes 786440 | tf_op jit(solution)/shard_map/ppermute | solution.py:276
  72.3 2.2 %parts_1_0.1 = (bf16[256,256]{1,0:T(8,128)(2,1)S(1)}, f32[128,1024]{1,0:T(8,128)S(1)}) custom-call(s32[2]{0:T(128)S(1)} %pad_add_fusion.place, bf16[128,2048]{1,0:T(8,128)(2,1)S(1)} %copy-done.1, bf16[128,1024]{1,0:T(8,128)(2,1)S(1)} %get-tuple-element.136.q_peer, bf16[128,2048]{1,0:T(8,128)(2,1)S(1)} %copy-done.3, ...), custom_call_target="tpu_custom_call" | custom-call | flops 3221225472 | bytes 1048576 | tf_op jit(solution)/shard_map/parts_1_0/pallas_call | solution.py:208
  74.5 1.5 %collective-permute-done.12 = f32[32]{0:T(128)S(1)} collective-permute-done((f32[32]{0:T(128)S(1)}, f32[32]{0:T(128)S(1)}, u32[]{:S(2)}, u32[]{:S(2)}) %collective-permute-start.12) | collective-permute-done | bytes 160 | tf_op jit(solution)/shard_map/ppermute | solution.py:282
  76.0 0.6 collective-permute-done.13
  76.6 0.1 collective-permute-start.14
  76.7 2.2 %parts_1_1.1 = (bf16[256,256]{1,0:T(8,128)(2,1)S(1)}, f32[128,1024]{1,0:T(8,128)S(1)}) custom-call(s32[2]{0:T(128)S(1)} %pad_add_fusion.place, bf16[128,2048]{1,0:T(8,128)(2,1)S(1)} %copy-done.1, bf16[128,1024]{1,0:T(8,128)(2,1)S(1)} %get-tuple-element.136.q_peer, bf16[128,2048]{1,0:T(8,128)(2,1)S(1)} %copy-done.3, ...), custom_call_target="tpu_custom_call" | custom-call | flops 3221225472 | bytes 1048576 | tf_op jit(solution)/shard_map/parts_1_1/pallas_call | solution.py:208
  79.0 7.5 %collective-permute-start.17 = (bf16[256,512]{1,0:T(8,128)(2,1)S(1)}, bf16[256,512]{1,0:T(8,128)(2,1)S(1)}, u32[]{:S(2)}, u32[]{:S(2)}) collective-permute-start(bf16[256,512]{1,0:T(8,128)(2,1)S(1)} %pad_maximum_fusion.2), channel_id=1, source_target_pairs={{0,254},{1,255},{2,0},{3,1},{4,2},{5,3},{6,4},{7,5},{8,6},{9,7},{1... | collective-permute-start | bytes 786440 | tf_op jit(solution)/shard_map/ppermute | solution.py:276
  86.5 2.3 %parts_0_0.1 = (f32[256,256]{1,0:T(8,128)S(1)}, bf16[128,512]{1,0:T(8,128)(2,1)S(1)}, bf16[128,512]{1,0:T(8,128)(2,1)S(1)}) custom-call(s32[2]{0:T(128)S(1)} %pad_add_fusion.place, bf16[128,2048]{1,0:T(8,128)(2,1)S(1)} %copy-done.1, bf16[128,1024]{1,0:T(8,128)(2,1)S(1)} %get-tuple-element.136.q_peer, bf16[128,2048]{1,0:T(8,128)(2,1)S(1)} %copy-done.3, ...), custom_call_target="tpu_custom_call" | custom-call | flops 3221225472 | bytes 1048576 | tf_op jit(solution)/shard_map/parts_0_0/pallas_call | solution.py:208
  88.7 0.1 collective-permute-done.15
  88.9 2.2 %parts_0_1.1 = (f32[256,256]{1,0:T(8,128)S(1)}, bf16[128,512]{1,0:T(8,128)(2,1)S(1)}, bf16[128,512]{1,0:T(8,128)(2,1)S(1)}) custom-call(s32[2]{0:T(128)S(1)} %pad_add_fusion.place, bf16[128,2048]{1,0:T(8,128)(2,1)S(1)} %copy-done.1, bf16[128,1024]{1,0:T(8,128)(2,1)S(1)} %get-tuple-element.136.q_peer, bf16[128,2048]{1,0:T(8,128)(2,1)S(1)} %copy-done.3, ...), custom_call_target="tpu_custom_call" | custom-call | flops 3221225472 | bytes 1048576 | tf_op jit(solution)/shard_map/parts_0_1/pallas_call | solution.py:208
  91.1 3.9 %collective-permute-start.16 = (bf16[128,1024]{1,0:T(8,128)(2,1)S(1)}, bf16[128,1024]{1,0:T(8,128)(2,1)S(1)}, u32[]{:S(2)}, u32[]{:S(2)}) collective-permute-start(bf16[128,1024]{1,0:T(8,128)(2,1)S(1)} %pad_maximum_fusion.1), channel_id=1, source_target_pairs={{0,1},{1,0},{2,3},{3,2},{4,5},{5,4},{6,7},{7,6},{8,9},{9,8},{10,11... | collective-permute-start | bytes 786440 | tf_op jit(solution)/shard_map/ppermute | solution.py:282
  95.1 0.2 fusion.3
  95.6 3.9 %collective-permute-done.19 = f32[32]{0:T(128)S(1)} collective-permute-done((f32[32]{0:T(128)S(1)}, f32[32]{0:T(128)S(1)}, u32[]{:S(2)}, u32[]{:S(2)}) %collective-permute-start.19) | collective-permute-done | bytes 160 | tf_op jit(solution)/shard_map/ppermute | solution.py:282
  99.4 0.5 add.75
  99.9 1.4 %join.2 = bf16[128,2048]{1,0:T(8,128)(2,1)} custom-call(s32[2]{0:T(128)S(1)} %pad_add_fusion.place, bf16[128,1024]{1,0:T(8,128)(2,1)S(1)} %pad_maximum_fusion.mine, bf16[128,1024]{1,0:T(8,128)(2,1)S(1)} %collective-permute-done.16.theirs), custom_call_target="tpu_custom_call" | custom-call | flops 1048576 | bytes 1048576 | tf_op jit(solution)/shard_map/join/pallas_call | solution.py:208
  101.3 1.3 %join.3 = (bf16[128,512]{1,0:T(8,128)(2,1)}, bf16[128,512]{1,0:T(8,128)(2,1)}) custom-call(s32[2]{0:T(128)S(1)} %pad_add_fusion.place, bf16[128,512]{1,0:T(8,128)(2,1)S(1)} %get-tuple-element.138.mine, bf16[128,512]{1,0:T(8,128)(2,1)S(1)} %collective-permute-done.18.theirs), custom_call_target="tpu_custom_call" | custom-call | flops 1048576 | bytes 1048576 | tf_op jit(solution)/shard_map/join/pallas_call | solution.py:208
  (50 shorter events, 1.2 us)
Async XLA Ops:
  0.7 0.7 copy-start.6
  1.4 1.0 %copy-start = (bf16[128,2048]{1,0:T(8,128)(2,1)S(1)}, bf16[128,2048]{1,0:T(8,128)(2,1)}, u32[]{:S(2)}) copy-start(bf16[128,2048]{1,0:T(8,128)(2,1)} %q_own.23) | copy-start | bytes 1572868
  2.4 1.0 %copy-start.2 = (bf16[128,2048]{1,0:T(8,128)(2,1)S(1)}, bf16[128,2048]{1,0:T(8,128)(2,1)}, u32[]{:S(2)}) copy-start(bf16[128,2048]{1,0:T(8,128)(2,1)} %g_own.23) | copy-start | bytes 1572868
  3.5 0.9 copy-start.4
  4.4 0.9 copy-start.5
  5.9 5.2 %collective-permute-start = (bf16[256,1024]{1,0:T(8,128)(2,1)S(1)}, bf16[256,1024]{1,0:T(8,128)(2,1)S(1)}, u32[]{:S(2)}, u32[]{:S(2)}) collective-permute-start(bf16[256,1024]{1,0:T(8,128)(2,1)S(1)} %get-tuple-element.67), channel_id=1, source_target_pairs={{0,1},{1,0},{2,3},{3,2},{4,5},{5,4},{6,7},{7,6},{8,9},{9,8},{10,11... | collective-permute-start | bytes 1572872 | tf_op jit(solution)/shard_map/ppermute | solution.py:282
  9.2 1.7 %collective-permute-start.1 = (bf16[144,512]{1,0:T(8,128)(2,1)S(1)}, bf16[144,512]{1,0:T(8,128)(2,1)S(1)}, u32[]{:S(2)}, u32[]{:S(2)}) collective-permute-start(bf16[144,512]{1,0:T(8,128)(2,1)S(1)} %get-tuple-element.69), channel_id=1, source_target_pairs={{0,1},{1,0},{2,3},{3,2},{4,5},{5,4},{6,7},{7,6},{8,9},{9,8},{10,11... | collective-permute-start | bytes 442376 | tf_op jit(solution)/shard_map/ppermute | solution.py:282
  11.0 1.0 %copy-start.1 = (bf16[128,2048]{1,0:T(8,128)(2,1)S(1)}, bf16[128,2048]{1,0:T(8,128)(2,1)}, u32[]{:S(2)}) copy-start(bf16[128,2048]{1,0:T(8,128)(2,1)} %q_own.23) | copy-start | bytes 1572868
  11.0 1.2 %copy-start.3 = (bf16[128,2048]{1,0:T(8,128)(2,1)S(1)}, bf16[128,2048]{1,0:T(8,128)(2,1)}, u32[]{:S(2)}) copy-start(bf16[128,2048]{1,0:T(8,128)(2,1)} %g_own.23) | copy-start | bytes 1572868
  11.0 12.8 %collective-permute-start.2 = (bf16[272,512]{1,0:T(8,128)(2,1)S(1)}, bf16[272,512]{1,0:T(8,128)(2,1)S(1)}, u32[]{:S(2)}, u32[]{:S(2)}) collective-permute-start(bf16[272,512]{1,0:T(8,128)(2,1)S(1)} %maximum_maximum_fusion.chunk.own_chunk), channel_id=1, source_target_pairs={{0,8},{1,9},{2,10},{3,11},{4,12},{5,13},{6,14},{7,15},{8,16},{9,17... | collective-permute-start | bytes 835592 | tf_op jit(solution)/shard_map/ppermute | solution.py:276
  11.2 1.0 %copy-start.7 = (f32[32]{0:T(128)S(1)}, f32[32]{0:T(128)}, u32[]{:S(2)}) copy-start(f32[32]{0:T(128)} %sinks.9) | copy-start | bytes 388
  24.8 8.8 %collective-permute-start.5 = (bf16[272,512]{1,0:T(8,128)(2,1)}, bf16[272,512]{1,0:T(8,128)(2,1)S(1)}, u32[]{:S(2)}, u32[]{:S(2)}) collective-permute-start(bf16[272,512]{1,0:T(8,128)(2,1)} %get-tuple-element.132), channel_id=1, source_target_pairs={{0,2},{1,3},{2,4},{3,5},{4,6},{5,7},{6,0},{7,1},{8,10},{9,11},{10,... | collective-permute-start | bytes 835592 | tf_op jit(solution)/shard_map/ppermute | solution.py:276
  26.1 14.6 %collective-permute-start.4 = (bf16[272,512]{1,0:T(8,128)(2,1)}, bf16[272,512]{1,0:T(8,128)(2,1)S(1)}, u32[]{:S(2)}, u32[]{:S(2)}) collective-permute-start(bf16[272,512]{1,0:T(8,128)(2,1)} %get-tuple-element.133), channel_id=1, source_target_pairs={{0,4},{1,5},{2,6},{3,7},{4,0},{5,1},{6,2},{7,3},{8,12},{9,13},{10,... | collective-permute-start | bytes 835592 | tf_op jit(solution)/shard_map/ppermute | solution.py:276
  28.7 14.7 %collective-permute-start.3 = (bf16[272,512]{1,0:T(8,128)(2,1)S(1)}, bf16[272,512]{1,0:T(8,128)(2,1)S(1)}, u32[]{:S(2)}, u32[]{:S(2)}) collective-permute-start(bf16[272,512]{1,0:T(8,128)(2,1)S(1)} %get-tuple-element.134), channel_id=1, source_target_pairs={{0,6},{1,7},{2,0},{3,1},{4,2},{5,3},{6,4},{7,5},{8,14},{9,15},{10,... | collective-permute-start | bytes 835592 | tf_op jit(solution)/shard_map/ppermute | solution.py:276
  46.3 2.6 %collective-permute-start.6 = (f32[32]{0:T(128)S(1)}, f32[32]{0:T(128)S(1)}, u32[]{:S(2)}, u32[]{:S(2)}) collective-permute-start(f32[32]{0:T(128)S(1)} %broadcast_select_fusion.3), channel_id=1, source_target_pairs={{0,1},{1,0},{2,3},{3,2},{4,5},{5,4},{6,7},{7,6},{8,9},{9,8},{10,11... | collective-permute-start | bytes 392 | tf_op jit(solution)/shard_map/ppermute | solution.py:282
  49.0 5.3 %collective-permute-start.7 = (f32[32]{0:T(128)S(1)}, f32[32]{0:T(128)S(1)}, u32[]{:S(2)}, u32[]{:S(2)}) collective-permute-start(f32[32]{0:T(128)S(1)} %fusion.11), channel_id=1, source_target_pairs={{0,2},{1,3},{2,0},{3,1},{4,6},{5,7},{6,4},{7,5},{8,10},{9,11},{10,... | collective-permute-start | bytes 392 | tf_op jit(solution)/shard_map/ppermute | solution.py:282
  53.2 9.7 %collective-permute-start.9 = (bf16[256,512]{1,0:T(8,128)(2,1)S(1)}, bf16[256,512]{1,0:T(8,128)(2,1)S(1)}, u32[]{:S(2)}, u32[]{:S(2)}) collective-permute-start(bf16[256,512]{1,0:T(8,128)(2,1)S(1)} %get-tuple-element.98), channel_id=1, source_target_pairs={{0,248},{1,249},{2,250},{3,251},{4,252},{5,253},{6,254},{7,255},{8... | collective-permute-start | bytes 786440 | tf_op jit(solution)/shard_map/ppermute | solution.py:276
  54.4 8.4 %collective-permute-start.8 = (f32[32]{0:T(128)S(1)}, f32[32]{0:T(128)S(1)}, u32[]{:S(2)}, u32[]{:S(2)}) collective-permute-start(f32[32]{0:T(128)S(1)} %add.65), channel_id=1, source_target_pairs={{0,4},{1,5},{2,6},{3,7},{4,0},{5,1},{6,2},{7,3},{8,12},{9,13},{10,... | collective-permute-start | bytes 392 | tf_op jit(solution)/shard_map/ppermute | solution.py:282
  61.4 10.7 %collective-permute-start.11 = (bf16[256,512]{1,0:T(8,128)(2,1)S(1)}, bf16[256,512]{1,0:T(8,128)(2,1)S(1)}, u32[]{:S(2)}, u32[]{:S(2)}) collective-permute-start(bf16[256,512]{1,0:T(8,128)(2,1)S(1)} %get-tuple-element.102), channel_id=1, source_target_pairs={{0,250},{1,251},{2,252},{3,253},{4,254},{5,255},{6,0},{7,1},{8,2},... | collective-permute-start | bytes 786440 | tf_op jit(solution)/shard_map/ppermute | solution.py:276
  62.8 9.3 %collective-permute-start.10 = (f32[32]{0:T(128)S(1)}, f32[32]{0:T(128)S(1)}, u32[]{:S(2)}, u32[]{:S(2)}) collective-permute-start(f32[32]{0:T(128)S(1)} %add.66), channel_id=1, source_target_pairs={{0,8},{1,9},{2,10},{3,11},{4,12},{5,13},{6,14},{7,15},{8,0},{9,1},... | collective-permute-start | bytes 392 | tf_op jit(solution)/shard_map/ppermute | solution.py:282
  67.5 9.0 %collective-permute-start.13 = (bf16[256,512]{1,0:T(8,128)(2,1)S(1)}, bf16[256,512]{1,0:T(8,128)(2,1)S(1)}, u32[]{:S(2)}, u32[]{:S(2)}) collective-permute-start(bf16[256,512]{1,0:T(8,128)(2,1)S(1)} %get-tuple-element.106), channel_id=1, source_target_pairs={{0,252},{1,253},{2,254},{3,255},{4,0},{5,1},{6,2},{7,3},{8,4},{9,5... | collective-permute-start | bytes 786440 | tf_op jit(solution)/shard_map/ppermute | solution.py:276
  72.2 3.7 %collective-permute-start.12 = (f32[32]{0:T(128)S(1)}, f32[32]{0:T(128)S(1)}, u32[]{:S(2)}, u32[]{:S(2)}) collective-permute-start(f32[32]{0:T(128)S(1)} %add.67), channel_id=1, source_target_pairs={{0,16},{1,17},{2,18},{3,19},{4,20},{5,21},{6,22},{7,23},{8,24},{9,... | collective-permute-start | bytes 392 | tf_op jit(solution)/shard_map/ppermute | solution.py:282
  76.6 9.9 %collective-permute-start.14 = (f32[32]{0:T(128)S(1)}, f32[32]{0:T(128)S(1)}, u32[]{:S(2)}, u32[]{:S(2)}) collective-permute-start(f32[32]{0:T(128)S(1)} %add.68), channel_id=1, source_target_pairs={{0,32},{1,33},{2,34},{3,35},{4,36},{5,37},{6,38},{7,39},{8,40},{9,... | collective-permute-start | bytes 392 | tf_op jit(solution)/shard_map/ppermute | solution.py:282
  79.0 16.1 %collective-permute-start.17 = (bf16[256,512]{1,0:T(8,128)(2,1)S(1)}, bf16[256,512]{1,0:T(8,128)(2,1)S(1)}, u32[]{:S(2)}, u32[]{:S(2)}) collective-permute-start(bf16[256,512]{1,0:T(8,128)(2,1)S(1)} %pad_maximum_fusion.2), channel_id=1, source_target_pairs={{0,254},{1,255},{2,0},{3,1},{4,2},{5,3},{6,4},{7,5},{8,6},{9,7},{1... | collective-permute-start | bytes 786440 | tf_op jit(solution)/shard_map/ppermute | solution.py:276
  86.5 2.4 %collective-permute-start.15 = (f32[32]{0:T(128)S(1)}, f32[32]{0:T(128)S(1)}, u32[]{:S(2)}, u32[]{:S(2)}) collective-permute-start(f32[32]{0:T(128)S(1)} %add.69), channel_id=1, source_target_pairs={{0,64},{1,65},{2,66},{3,67},{4,68},{5,69},{6,70},{7,71},{8,72},{9,... | collective-permute-start | bytes 392 | tf_op jit(solution)/shard_map/ppermute | solution.py:282
  91.1 8.8 %collective-permute-start.16 = (bf16[128,1024]{1,0:T(8,128)(2,1)S(1)}, bf16[128,1024]{1,0:T(8,128)(2,1)S(1)}, u32[]{:S(2)}, u32[]{:S(2)}) collective-permute-start(bf16[128,1024]{1,0:T(8,128)(2,1)S(1)} %pad_maximum_fusion.1), channel_id=1, source_target_pairs={{0,1},{1,0},{2,3},{3,2},{4,5},{5,4},{6,7},{7,6},{8,9},{9,8},{10,11... | collective-permute-start | bytes 786440 | tf_op jit(solution)/shard_map/ppermute | solution.py:282
  95.3 6.0 %collective-permute-start.18 = (bf16[128,512]{1,0:T(8,128)(2,1)S(1)}, bf16[128,512]{1,0:T(8,128)(2,1)S(1)}, u32[]{:S(2)}, u32[]{:S(2)}) collective-permute-start(bf16[128,512]{1,0:T(8,128)(2,1)S(1)} %get-tuple-element.137), channel_id=1, source_target_pairs={{0,1},{1,0},{2,3},{3,2},{4,5},{5,4},{6,7},{7,6},{8,9},{9,8},{10,11... | collective-permute-start | bytes 393224 | tf_op jit(solution)/shard_map/ppermute | solution.py:282
  95.4 4.0 %collective-permute-start.19 = (f32[32]{0:T(128)S(1)}, f32[32]{0:T(128)S(1)}, u32[]{:S(2)}, u32[]{:S(2)}) collective-permute-start(f32[32]{0:T(128)S(1)} %add.70), channel_id=1, source_target_pairs={{0,128},{1,129},{2,130},{3,131},{4,132},{5,133},{6,134},{7,135},{8... | collective-permute-start | bytes 392 | tf_op jit(solution)/shard_map/ppermute | solution.py:282

commit v2 on v1

v2 whole, which is shorter than its diff:
```python
import functools
import math

import jax
import jax.numpy as jnp
from jax import lax
from jax.experimental import pallas as pl
from jax.experimental.pallas import tpu as pltpu
from jax.sharding import PartitionSpec as P

KV_HEADS = 8
HEAD_DIM = 64
WINDOW = 1024
TOK = 128
CHIP = 2 * TOK
HOPS = WINDOW // CHIP
ROW = 4
SPAN = WINDOW + CHIP
HALF_KV = KV_HEADS // 2 * HEAD_DIM
SCALE = 1.0 / math.sqrt(HEAD_DIM)
EXP2_SCALE = SCALE * math.log2(math.e)
MASKED = -1e30
F32 = jnp.float32
BF16 = jnp.bfloat16


NT, NN = ((1,), (1,)), ((1,), (0,))


def dot(a, b, dims):
    return lax.dot_general(a, b, (dims, ((), ())), preferred_element_type=F32)


def mask_bias(place, chunk, own_chunk, hop):
    core, chip = place[0], place[1]
    key_seg = chunk[CHIP : CHIP + 16, :CHIP].astype(F32)[0:1]
    query_seg = own_chunk[CHIP : CHIP + 16, :CHIP].astype(F32)[0:1]
    key_seg = jnp.where(chip >= hop, key_seg, -1.0)
    column = jnp.transpose(jnp.broadcast_to(key_seg, (TOK, CHIP)))
    allowed = jnp.concatenate([column, column], 1) == query_seg
    if hop in (0, HOPS):
        query_pos = lax.broadcasted_iota(jnp.int32, (CHIP, CHIP), 1) ^ (core * TOK)
        key_pos = lax.broadcasted_iota(jnp.int32, (CHIP, CHIP), 0) ^ (core * TOK)
        inside = key_pos <= query_pos if hop == 0 else key_pos > query_pos
        allowed = allowed & inside
    return jnp.where(allowed, 0.0, MASKED)


def prep_kernel(place, q_own, g_own, both_peer, query_all, grad_all):
    core = place[0]
    q_peer, g_peer = both_peer.at[:TOK, :], both_peer.at[TOK:, :]
    lane_half = lax.broadcasted_iota(jnp.int32, (CHIP, 128), 1) // HEAD_DIM
    for own, peer, out in ((q_own, q_peer, query_all), (g_own, g_peer, grad_all)):
        for pair in range(8):
            at = pl.ds(pl.multiple_of(core * 1024 + pair * 128, 128), 128)
            theirs = peer[:, pair * 128 : (pair + 1) * 128]
            rows = jnp.concatenate([own[:, at], theirs], 0).astype(F32)
            turned = pltpu.roll(rows, HEAD_DIM, 1)
            half = pair // 2 % 2
            for e in range(2):
                chosen = jnp.where(lane_half == half, rows if half == e else turned, 0.0)
                out[head_rows(2 * pair + e), :] = chosen.astype(BF16)


def head_rows(head):
    return slice(head * CHIP, (head + 1) * CHIP)


def lane_tile(tile, first_lane=0):
    return slice(first_lane + tile * 128, first_lane + tile * 128 + 128)


def stats_kernel(hop, last, place, sinks, query_all, grad_all, chunk, own_chunk, *refs):
    before, after = refs[:3], refs[3:]
    if hop == 0:
        before, after = None, refs
    (top_out, second, third), bias = after[:3], after[-1]
    core = place[0]
    bias[...] = mask_bias(place, chunk, own_chunk, hop)
    for head in range(16):
        tile, at = head // 8, slice(head, head + 1)
        sink = sinks[core * 16 + head] * (1.0 / SCALE)
        s = dot(chunk[0:CHIP, lane_tile(tile)], query_all[head_rows(head), :], NT) + bias[...]
        dp = dot(chunk[0:CHIP, lane_tile(tile, HALF_KV)], grad_all[head_rows(head), :], NT)
        old = jnp.full((1, CHIP), sink, F32) if hop == 0 else before[0][at, :]
        top = jnp.maximum(old, jnp.max(s, 0, keepdims=True))
        ex = jnp.exp2((s - top) * EXP2_SCALE)
        fade = jnp.exp2((old - top) * EXP2_SCALE)
        denom = jnp.sum(ex, 0, keepdims=True)
        weighed = jnp.sum(ex * dp, 0, keepdims=True)
        if hop == 0:
            denom = denom + fade
        else:
            denom = denom + before[1][at, :] * fade
            weighed = weighed + before[2][at, :] * fade
        top_out[at, :] = top
        if last:
            share = 1.0 / denom
            delta = weighed * share
            second[at, :] = share
            third[at, :] = delta
            after[3][at, :] = -jnp.exp2((sink - top) * EXP2_SCALE) * share * delta
        else:
            second[at, :] = denom
            third[at, :] = weighed


def parts_kernel(
    hop, place, query_all, grad_all, chunk, own_chunk, tops, shares, deltas, *refs
):
    weight, dscore, bias = refs[-3:]
    dq_in = None if hop == HOPS else refs[0]
    outs = refs[:-3] if hop == HOPS else refs[1:-3]
    kv_out = outs[0]
    bias[...] = mask_bias(place, chunk, own_chunk, hop)
    keys_t = jnp.transpose(chunk[0:CHIP, 0:CHIP].astype(F32)).astype(BF16)
    for tile in range(2):
        for n in range(8):
            head, span = 8 * tile + n, head_rows(n)
            at = slice(head, head + 1)
            s = dot(chunk[0:CHIP, lane_tile(tile)], query_all[head_rows(head), :], NT)
            dp = dot(
                chunk[0:CHIP, lane_tile(tile, HALF_KV)], grad_all[head_rows(head), :], NT
            )
            prob = jnp.exp2((s + bias[...] - tops[at, :]) * EXP2_SCALE) * shares[at, :]
            weight[tile, :, span] = prob.astype(BF16)
            dscore[tile, :, span] = (prob * (dp - deltas[at, :])).astype(BF16)
        rows = slice(8 * tile * CHIP, 8 * (tile + 1) * CHIP)
        value_part = dot(weight[tile], grad_all[rows, :], NN)
        key_part = dot(dscore[tile], query_all[rows, :], NN) * SCALE
        kv_out[:, lane_tile(tile)] = key_part.astype(kv_out.dtype)
        kv_out[:, lane_tile(tile, HALF_KV)] = value_part.astype(kv_out.dtype)
        for group in range(2):
            g = 2 * tile + group
            rows = slice(g * HEAD_DIM, (g + 1) * HEAD_DIM)
            dq_t = dot(
                keys_t[rows, :], dscore[tile, :, group * 1024 : (group + 1) * 1024], NN
            )
            if dq_in is not None:
                dq_t = dq_t + dq_in[rows, :]
            if hop > 0:
                outs[1][rows, :] = dq_t
                continue
            for pair in range(2):
                two = jnp.concatenate(
                    [dq_t[:, head_rows(2 * pair)], dq_t[:, head_rows(2 * pair + 1)]], 0
                )
                dq = (jnp.transpose(two) * SCALE).astype(BF16)
                outs[1][:, lane_tile(2 * g + pair)] = dq[:TOK]
                outs[2][:, lane_tile(2 * g + pair)] = dq[TOK:]


def pack_kernel(place, segment, keys, values, queries, grads, own, send, tokens, sems):
    core = place[0]

    def half(ref, which, width):
        return ref.at[:, pl.ds(pl.multiple_of(which * width, width), width)]

    moves = []
    for out, which in ((send, 1 - core), (own, core)):
        moves.append((half(keys, which, HALF_KV), out.at[:TOK, :HALF_KV]))
        moves.append((half(values, which, HALF_KV), out.at[:TOK, HALF_KV:]))
    moves.append((half(queries, 1 - core, 1024), tokens.at[:TOK, :]))
    moves.append((half(grads, 1 - core, 1024), tokens.at[TOK:, :]))
    copies = [
        pltpu.make_async_copy(source, target, sems.at[n])
        for n, (source, target) in enumerate(moves)
    ]
    for copy in copies:
        copy.start()
    marks = jnp.broadcast_to(segment[...], (16, TOK)).astype(F32).astype(BF16)
    for out in (own, send):
        for lane in range(0, 2 * HALF_KV, TOK):
            out[TOK:, lane : lane + TOK] = marks
    for copy in copies:
        copy.wait()


def join_kernel(place, mine, theirs, *outs):
    core = place[0]
    width = mine.shape[1] // len(outs)
    for n, out in enumerate(outs):
        for which, part in ((core, mine), (1 - core, theirs)):
            at = pl.ds(pl.multiple_of(which * width, width), width)
            out[:, at] = part[:, n * width : (n + 1) * width]


SMEM = pl.BlockSpec(memory_space=pltpu.SMEM)
VMEM = pl.BlockSpec(memory_space=pltpu.VMEM)
STAT = jax.ShapeDtypeStruct((16, CHIP), F32)


def run(
    kernel, name, n_scalars, operands, out_shape, scratch, flops, interpret, n_far=0, vmem=16
):
    n_arrays = len(operands) - n_scalars - n_far
    return pl.pallas_call(
        kernel,
        name=name,
        in_specs=[SMEM] * n_scalars
        + [VMEM] * n_arrays
        + [pl.BlockSpec(memory_space=pltpu.HBM)] * n_far,
        out_specs=[VMEM] * len(out_shape),
        out_shape=out_shape,
        scratch_shapes=scratch,
        compiler_params=pltpu.CompilerParams(vmem_limit_bytes=vmem << 20),
        cost_estimate=pl.CostEstimate(flops=flops, transcendentals=0, bytes_accessed=1 << 20),
        interpret=interpret,
    )(*operands)


def prepared(place, queries, out_grad, both_peer, interpret):
    rows = jax.ShapeDtypeStruct((16 * CHIP, 128), BF16)
    return run(
        prep_kernel, "prep", 1, (place, queries, out_grad, both_peer),
        [rows, rows], [], 1 << 30, interpret,
    )


def stats_of(hop, last, place, sinks, tokens, chunk, own_chunk, before, interpret):
    return run(
        functools.partial(stats_kernel, hop, last), f"stats_{hop}", 2,
        (place, sinks, *tokens, chunk, own_chunk, *before),
        [STAT] * (4 if last else 3),
        [pltpu.VMEM((CHIP, CHIP), F32)], 2 << 30, interpret,
    )


def parts_of(hop, place, tokens, chunk, own_chunk, stats, dq, interpret):
    kv = jax.ShapeDtypeStruct((CHIP, 2 * HALF_KV), BF16 if hop else F32)
    if hop:
        dq_shapes = [jax.ShapeDtypeStruct((CHIP, 1024), F32)]
    else:
        dq_shapes = [jax.ShapeDtypeStruct((TOK, 1024), BF16)] * 2
    return run(
        functools.partial(parts_kernel, hop), f"parts_{hop}", 1,
        (place, *tokens, chunk, own_chunk, *stats, *dq),
        [kv] + dq_shapes,
        [pltpu.VMEM((2, CHIP, 8 * CHIP), BF16)] * 2 + [pltpu.VMEM((CHIP, CHIP), F32)],
        3 << 30, interpret,
    )


def packed(place, key_heads, value_heads, segment, queries, out_grad, interpret):
    rows = jax.ShapeDtypeStruct((TOK + 16, 2 * HALF_KV), BF16)
    return run(
        pack_kernel, "pack", 1,
        (place, segment[None, :], key_heads, value_heads, queries, out_grad),
        [rows, rows, jax.ShapeDtypeStruct((2 * TOK, 1024), BF16)],
        [pltpu.SemaphoreType.DMA((6,))], 1 << 20, interpret, n_far=4, vmem=62,
    )


def joined(place, mine, theirs, outs, interpret):
    width = mine.shape[1] // outs
    shape = jax.ShapeDtypeStruct((TOK, 2 * width), BF16)
    return run(
        join_kernel, "join", 1, (place, mine, theirs), [shape] * outs, [], 1 << 20, interpret
    )


def per_device(count, interpret, queries, key_heads, value_heads, out_grad, segment, sink_logits):
    index = lax.axis_index("ctx")
    core, chip = index % 2, index // 2
    first = core == 0

    def sent(block, route):
        return lax.ppermute(block, "ctx", route)

    def shifted(block, chips):
        return sent(block, [(i, (i + 2 * chips) % count) for i in range(count)])

    def crossed(block, bit):
        return lax.ppermute(block, "ctx", [(i, i ^ bit) for i in range(count)])

    def in_row(i, hop):
        return i // 8 * 8 + (i // 2 + hop) % ROW * 2 + i % 2

    place = jnp.stack([core, chip]).astype(jnp.int32)
    own, kv_send, tokens_send = packed(
        place, key_heads, value_heads, segment, queries, out_grad, interpret
    )
    came, tokens_send = lax.optimization_barrier((crossed(kv_send, 1), tokens_send))
    marks = jnp.concatenate(
        [own[TOK:, :TOK], came[TOK:, TOK:CHIP], own[TOK:, CHIP:]], 1
    )
    chunk = jnp.concatenate([own[:TOK], came[:TOK], marks], 0)
    chunks = {0: chunk, HOPS: shifted(chunk, HOPS)}
    both = crossed(tokens_send, 1)
    tokens = prepared(place, queries, out_grad, both, interpret)
    stats = stats_of(
        0, False, place, sink_logits, tokens, chunk, chunk, (), interpret
    )
    *stats, chunks[HOPS] = lax.optimization_barrier((*stats, chunks[HOPS]))
    for hop in range(1, HOPS):
        within = chip % ROW + hop < ROW
        chunks[hop] = sent(
            jnp.where(within, chunk, chunks[HOPS]), [(i, in_row(i, hop)) for i in range(count)]
        )
    for hop in (HOPS, 1, 2, 3):
        stats = stats_of(
            hop, hop == 3, place, sink_logits, tokens, chunks[hop], chunk, stats, interpret
        )
    *stats, sink_rows = stats
    sink_grad = jnp.sum(sink_rows, -1)
    bits = [1 << n for n in range(1, count.bit_length() - 1)]

    def widened(value):
        return value + crossed(value, bits.pop(0)) if bits else value

    dq, came_back = (), {}
    for hop in range(HOPS, 0, -1):
        part, *dq = parts_of(hop, place, tokens, chunks[hop], chunk, stats, dq, interpret)
        came_back[hop] = shifted(part, -hop)
        sink_grad = widened(sink_grad)
        if hop + 1 in came_back:
            dq[0], sink_grad, came_back[hop + 1] = lax.optimization_barrier(
                (dq[0], sink_grad, came_back[hop + 1])
            )
        else:
            dq[0], sink_grad = lax.optimization_barrier((dq[0], sink_grad))
    total, dq_own, dq_peer = parts_of(0, place, tokens, chunk, chunk, stats, dq, interpret)
    dq_own, dq_peer, sink_grad = lax.optimization_barrier(
        (dq_own, dq_peer, widened(sink_grad))
    )
    dq_came = crossed(dq_peer, 1)
    query_grad = jnp.where(
        first,
        jnp.concatenate([dq_own, dq_came], 1),
        jnp.concatenate([dq_came, dq_own], 1),
    )
    for part in came_back.values():
        total = total + part.astype(F32)
    total = total.astype(BF16)
    key_grad, value_grad = joined(place, total[:TOK], crossed(total[TOK:], 1), 2, interpret)
    while bits:
        sink_grad = widened(sink_grad)
    other = crossed(sink_grad, 1)
    sink_grad = jnp.where(
        first, jnp.concatenate([sink_grad, other]), jnp.concatenate([other, sink_grad])
    )
    return query_grad, key_grad, value_grad, sink_grad


def solution(mesh, interpret=False):
    rows = P("ctx", None)
    return jax.shard_map(
        functools.partial(per_device, mesh.size, interpret),
        mesh=mesh,
        in_specs=(rows, rows, rows, rows, P("ctx"), P()),
        out_specs=(rows, rows, rows, P()),
        check_vma=False,
    )
```

time: 103 us -> 96.9 us (0.941)
  Pallas kernels: 37.1 us -> 33.4 us
  starting transfers between devices: 33.4 us -> 30 us
  waiting for transfers between devices: 23.1 us -> 24.8 us
    ppermute x8, starting transfers between devices: 19.7 us -> 13.9 us  [sent(): return lax.ppermute(block, 'ctx', route)]
    pallas_call x15 -> x13, Pallas kernels: 37.1 us -> 33.4 us  [run(): pl.pallas_call(kernel, name=name, in_specs=[SMEM] * n_scalars + [VMEM] *...]
    unnamed x16 -> x12, local copies, waits for them, and re-layouts: 5.58 us -> 2.46 us
    ppermute x12, starting transfers between devices: 13.8 us -> 16.2 us  [crossed(): return lax.ppermute(block, 'ctx', [(i, i ^ bit) for i in range(count)])]
    ppermute x12, waiting for transfers between devices: 7.91 us -> 10.1 us  [crossed(): return lax.ppermute(block, 'ctx', [(i, i ^ bit) for i in range(count)])]
    select_n x1 -> x2, other arithmetic: 0.08 us -> 1.51 us  [the longest x1 0.92 us: per_device(): jnp.where(first, jnp.concatenate([dq_own, dq_came], 1), jnp.concatenate([...]
  transfers between devices with their start and end apart: 20 -> 20, of which waited for: 9 -> 8; matrix products, arithmetic and copies ran while one was open for 1% -> 3% of each run, Pallas kernels for 32% -> 29%
where the time goes in v2:
time: 96.9 us; the launch traced here: 96.6 us
  Pallas kernels  33.4 us (34%)
  starting transfers between devices  30 us (31%)
  waiting for transfers between devices  24.8 us (26%)
  local copies, waits for them, and re-layouts  4.87 us (5%)
  other arithmetic  2.57 us (3%)
    pallas_call x13, Pallas kernels, run(): pl.pallas_call(kernel, name=name, in_specs=[SMEM] * n_scalars + [VMEM] *...  33.4 us
    ppermute x12, starting transfers between devices, crossed(): return lax.ppermute(block, 'ctx', [(i, i ^ bit) for i in range(count)])  16.2 us
    ppermute x8, waiting for transfers between devices, sent(): return lax.ppermute(block, 'ctx', route)  14.7 us
    ppermute x8, starting transfers between devices, sent(): return lax.ppermute(block, 'ctx', route)  13.9 us
    ppermute x12, waiting for transfers between devices, crossed(): return lax.ppermute(block, 'ctx', [(i, i ^ bit) for i in range(count)])  10.1 us
    unnamed x12, local copies, waits for them, and re-layouts  2.46 us
  transfers between devices with their start and end apart: 20, of which 8 were waited for; matrix products, arithmetic and copies ran while one was open for 3% of the time, Pallas kernels for 29%

profile of v2, /device:TPU:1, one launch (start us, length us, event | category | flops | bytes accessed | tf_op | source)
XLA Modules:
  0.0 96.6 jit_solution(4458514656461370579)
XLA Ops:
  0.6 0.6 pad_add_fusion.place
  1.2 2.8 %pack.1 = (bf16[144,512]{1,0:T(8,128)(2,1)}, bf16[144,512]{1,0:T(8,128)(2,1)}, bf16[256,1024]{1,0:T(8,128)(2,1)}) custom-call(s32[2]{0:T(128)} %pad_add_fusion.place, s32[1,128]{1,0:T(1,128)} %bitcast.3, bf16[128,512]{1,0:T(8,128)(2,1)} %keys.1, bf16[128,512]{1,0:T(8,128)(2,1)} %values.1, bf16[128,2048]{1,0:T(8,128)(2,1)} %q_own.1, bf16[128,2048]{1,0:T(8,128)(2,1)} %g_own.1), custom_call_target="tpu_custom_call" | custom-call | flops 1048576 | bytes 1048576 | tf_op jit(solution)/shard_map/pack/pallas_call | solution.py:197
  4.0 3.3 %collective-permute-start = (bf16[144,512]{1,0:T(8,128)(2,1)}, bf16[144,512]{1,0:T(8,128)(2,1)S(1)}, u32[]{:S(2)}, u32[]{:S(2)}) collective-permute-start(bf16[144,512]{1,0:T(8,128)(2,1)} %get-tuple-element.58), channel_id=1, source_target_pairs={{0,1},{1,0},{2,3},{3,2},{4,5},{5,4},{6,7},{7,6},{8,9},{9,8},{10,11... | collective-permute-start | bytes 442376 | tf_op jit(solution)/shard_map/ppermute | solution.py:274
  7.4 1.2 %collective-permute-done = bf16[144,512]{1,0:T(8,128)(2,1)S(1)} collective-permute-done((bf16[144,512]{1,0:T(8,128)(2,1)}, bf16[144,512]{1,0:T(8,128)(2,1)S(1)}, u32[]{:S(2)}, u32[]{:S(2)}) %collective-permute-start) | collective-permute-done | bytes 147488 | tf_op jit(solution)/shard_map/ppermute | solution.py:274
  8.6 0.4 collective-permute-start.1
  8.9 0.7 slice.23
  9.6 0.7 slice.25
  10.3 1.0 %slice.21 = bf16[128,512]{1,0:T(8,128)(2,1)S(1)} slice(bf16[144,512]{1,0:T(8,128)(2,1)} %get-tuple-element.63), slice={[0:128], [0:512]} | slice | bytes 262144 | tf_op jit(solution)/shard_map/slice | solution.py:287
  11.6 0.5 copy-done.2
  12.1 1.0 %prep.1 = (bf16[4096,128]{1,0:T(8,128)(2,1)S(1)}, bf16[4096,128]{1,0:T(8,128)(2,1)S(1)}) custom-call(s32[2]{0:T(128)S(1)} %copy-done.2, bf16[128,2048]{1,0:T(8,128)(2,1)S(1)} %copy-done, bf16[128,2048]{1,0:T(8,128)(2,1)S(1)} %copy-done.1, bf16[256,1024]{1,0:T(8,128)(2,1)S(1)} %collective-permute-done.1.both_peer), custom_call_target="tpu_custom_call" | custom-call | flops 1073741824 | bytes 1048576 | tf_op jit(solution)/shard_map/prep/pallas_call | solution.py:197
  13.1 0.7 copy-done.3
  13.7 2.2 %stats_0.1 = (f32[16,256]{1,0:T(8,128)S(1)}, f32[16,256]{1,0:T(8,128)S(1)}, f32[16,256]{1,0:T(8,128)S(1)}) custom-call(s32[2]{0:T(128)S(1)} %copy-done.2, f32[32]{0:T(128)S(1)} %copy-done.3, bf16[4096,128]{1,0:T(8,128)(2,1)S(1)} %get-tuple-element.61.query_all, bf16[4096,128]{1,0:T(8,128)(2,1)S(1)} %get-tuple-element.62.grad_all, ...), custom_call_target="tpu_custom_call" | custom-call | flops 2147483648 | bytes 1048576 | tf_op jit(solution)/shard_map/stats_0/pallas_call | solution.py:197
  16.0 8.4 %collective-permute-done.2.chunk = bf16[272,512]{1,0:T(8,128)(2,1)S(1)} collective-permute-done((bf16[272,512]{1,0:T(8,128)(2,1)S(1)}, bf16[272,512]{1,0:T(8,128)(2,1)S(1)}, u32[]{:S(2)}, u32[]{:S(2)}) %collective-permute-start.2) | collective-permute-done | bytes 278560 | tf_op jit(solution)/shard_map/ppermute | solution.py:268
  24.4 0.1 broadcast_select_fusion
  24.5 1.4 %collective-permute-start.5 = (bf16[272,512]{1,0:T(8,128)(2,1)S(1)}, bf16[272,512]{1,0:T(8,128)(2,1)S(1)}, u32[]{:S(2)}, u32[]{:S(2)}) collective-permute-start(bf16[272,512]{1,0:T(8,128)(2,1)S(1)} %get-tuple-element.112), channel_id=1, source_target_pairs={{0,2},{1,3},{2,4},{3,5},{4,6},{5,7},{6,0},{7,1},{8,10},{9,11},{10,... | collective-permute-start | bytes 835592 | tf_op jit(solution)/shard_map/ppermute | solution.py:268
  25.9 2.6 %collective-permute-start.4 = (bf16[272,512]{1,0:T(8,128)(2,1)S(1)}, bf16[272,512]{1,0:T(8,128)(2,1)S(1)}, u32[]{:S(2)}, u32[]{:S(2)}) collective-permute-start(bf16[272,512]{1,0:T(8,128)(2,1)S(1)} %get-tuple-element.113), channel_id=1, source_target_pairs={{0,4},{1,5},{2,6},{3,7},{4,0},{5,1},{6,2},{7,3},{8,12},{9,13},{10,... | collective-permute-start | bytes 835592 | tf_op jit(solution)/shard_map/ppermute | solution.py:268
  28.5 1.1 %collective-permute-start.3 = (bf16[272,512]{1,0:T(8,128)(2,1)S(1)}, bf16[272,512]{1,0:T(8,128)(2,1)S(1)}, u32[]{:S(2)}, u32[]{:S(2)}) collective-permute-start(bf16[272,512]{1,0:T(8,128)(2,1)S(1)} %get-tuple-element.114), channel_id=1, source_target_pairs={{0,6},{1,7},{2,0},{3,1},{4,2},{5,3},{6,4},{7,5},{8,14},{9,15},{10,... | collective-permute-start | bytes 835592 | tf_op jit(solution)/shard_map/ppermute | solution.py:268
  29.6 2.3 %stats_4.1 = (f32[16,256]{1,0:T(8,128)S(1)}, f32[16,256]{1,0:T(8,128)S(1)}, f32[16,256]{1,0:T(8,128)S(1)}) custom-call(s32[2]{0:T(128)S(1)} %copy-done.2, f32[32]{0:T(128)S(1)} %copy-done.3, bf16[4096,128]{1,0:T(8,128)(2,1)S(1)} %get-tuple-element.61.query_all, bf16[4096,128]{1,0:T(8,128)(2,1)S(1)} %get-tuple-element.62.grad_all, ...), custom_call_target="tpu_custom_call" | custom-call | flops 2147483648 | bytes 1048576 | tf_op jit(solution)/shard_map/stats_4/pallas_call | solution.py:197
  31.9 1.5 %collective-permute-done.5.chunk = bf16[272,512]{1,0:T(8,128)(2,1)S(1)} collective-permute-done((bf16[272,512]{1,0:T(8,128)(2,1)S(1)}, bf16[272,512]{1,0:T(8,128)(2,1)S(1)}, u32[]{:S(2)}, u32[]{:S(2)}) %collective-permute-start.5) | collective-permute-done | bytes 278560 | tf_op jit(solution)/shard_map/ppermute | solution.py:268
  33.4 2.3 %stats_1.1 = (f32[16,256]{1,0:T(8,128)S(1)}, f32[16,256]{1,0:T(8,128)S(1)}, f32[16,256]{1,0:T(8,128)S(1)}) custom-call(s32[2]{0:T(128)S(1)} %copy-done.2, f32[32]{0:T(128)S(1)} %copy-done.3, bf16[4096,128]{1,0:T(8,128)(2,1)S(1)} %get-tuple-element.61.query_all, bf16[4096,128]{1,0:T(8,128)(2,1)S(1)} %get-tuple-element.62.grad_all, ...), custom_call_target="tpu_custom_call" | custom-call | flops 2147483648 | bytes 1048576 | tf_op jit(solution)/shard_map/stats_1/pallas_call | solution.py:197
  35.8 4.7 %collective-permute-done.4.chunk = bf16[272,512]{1,0:T(8,128)(2,1)S(1)} collective-permute-done((bf16[272,512]{1,0:T(8,128)(2,1)S(1)}, bf16[272,512]{1,0:T(8,128)(2,1)S(1)}, u32[]{:S(2)}, u32[]{:S(2)}) %collective-permute-start.4) | collective-permute-done | bytes 278560 | tf_op jit(solution)/shard_map/ppermute | solution.py:268
  40.5 2.3 %stats_2.1 = (f32[16,256]{1,0:T(8,128)S(1)}, f32[16,256]{1,0:T(8,128)S(1)}, f32[16,256]{1,0:T(8,128)S(1)}) custom-call(s32[2]{0:T(128)S(1)} %copy-done.2, f32[32]{0:T(128)S(1)} %copy-done.3, bf16[4096,128]{1,0:T(8,128)(2,1)S(1)} %get-tuple-element.61.query_all, bf16[4096,128]{1,0:T(8,128)(2,1)S(1)} %get-tuple-element.62.grad_all, ...), custom_call_target="tpu_custom_call" | custom-call | flops 2147483648 | bytes 1048576 | tf_op jit(solution)/shard_map/stats_2/pallas_call | solution.py:197
  42.9 2.3 %stats_3.1 = (f32[16,256]{1,0:T(8,128)S(1)}, f32[16,256]{1,0:T(8,128)S(1)}, f32[16,256]{1,0:T(8,128)S(1)}, f32[16,256]{1,0:T(8,128)S(1)}) custom-call(s32[2]{0:T(128)S(1)} %copy-done.2, f32[32]{0:T(128)S(1)} %copy-done.3, bf16[4096,128]{1,0:T(8,128)(2,1)S(1)} %get-tuple-element.61.query_all, bf16[4096,128]{1,0:T(8,128)(2,1)S(1)} %get-tuple-element.62.grad_all, ...), custom_call_target="tpu_custom_call" | custom-call | flops 2147483648 | bytes 1048576 | tf_op jit(solution)/shard_map/stats_3/pallas_call | solution.py:197
  45.2 0.1 reduce_sum.9
  45.4 1.2 %copy-done.5 = bf16[4096,128]{1,0:T(8,128)(2,1)S(1)} copy-done((bf16[4096,128]{1,0:T(8,128)(2,1)S(1)}, bf16[4096,128]{1,0:T(8,128)(2,1)}, u32[]{:S(2)}) %copy-start.5) | copy-done | bytes 1048600
  46.6 3.4 %parts_4.1 = (bf16[256,512]{1,0:T(8,128)(2,1)S(1)}, f32[256,1024]{1,0:T(8,128)S(1)}) custom-call(s32[2]{0:T(128)S(1)} %copy-done.2, bf16[4096,128]{1,0:T(8,128)(2,1)S(1)} %get-tuple-element.61.query_all, bf16[4096,128]{1,0:T(8,128)(2,1)S(1)} %copy-done.5, bf16[272,512]{1,0:T(8,128)(2,1)S(1)} %collective-permute-done.2.chunk, ...), custom_call_target="tpu_custom_call" | custom-call | flops 3221225472 | bytes 1048576 | tf_op jit(solution)/shard_map/parts_4/pallas_call | solution.py:197
  50.0 1.0 %collective-permute-start.8 = (bf16[256,512]{1,0:T(8,128)(2,1)S(1)}, bf16[256,512]{1,0:T(8,128)(2,1)S(1)}, u32[]{:S(2)}, u32[]{:S(2)}) collective-permute-start(bf16[256,512]{1,0:T(8,128)(2,1)S(1)} %get-tuple-element.89), channel_id=1, source_target_pairs={{0,248},{1,249},{2,250},{3,251},{4,252},{5,253},{6,254},{7,255},{8... | collective-permute-start | bytes 786440 | tf_op jit(solution)/shard_map/ppermute | solution.py:268
  51.0 2.1 %collective-permute-start.7 = (f32[16]{0:T(128)S(1)}, f32[16]{0:T(128)S(1)}, u32[]{:S(2)}, u32[]{:S(2)}) collective-permute-start(f32[16]{0:T(128)S(1)} %add.57), channel_id=1, source_target_pairs={{0,4},{1,5},{2,6},{3,7},{4,0},{5,1},{6,2},{7,3},{8,12},{9,13},{10,... | collective-permute-start | bytes 200 | tf_op jit(solution)/shard_map/ppermute | solution.py:274
  53.1 3.4 %parts_3.1 = (bf16[256,512]{1,0:T(8,128)(2,1)S(1)}, f32[256,1024]{1,0:T(8,128)S(1)}) custom-call(s32[2]{0:T(128)S(1)} %copy-done.2, bf16[4096,128]{1,0:T(8,128)(2,1)S(1)} %get-tuple-element.61.query_all, bf16[4096,128]{1,0:T(8,128)(2,1)S(1)} %copy-done.5, bf16[272,512]{1,0:T(8,128)(2,1)S(1)} %collective-permute-done.3.chunk, ...), custom_call_target="tpu_custom_call" | custom-call | flops 3221225472 | bytes 1048576 | tf_op jit(solution)/shard_map/parts_3/pallas_call | solution.py:197
  56.6 0.6 collective-permute-start.9
  57.3 3.3 %parts_2.1 = (bf16[256,512]{1,0:T(8,128)(2,1)S(1)}, f32[256,1024]{1,0:T(8,128)S(1)}) custom-call(s32[2]{0:T(128)S(1)} %copy-done.2, bf16[4096,128]{1,0:T(8,128)(2,1)S(1)} %get-tuple-element.61.query_all, bf16[4096,128]{1,0:T(8,128)(2,1)S(1)} %copy-done.5, bf16[272,512]{1,0:T(8,128)(2,1)S(1)} %collective-permute-done.4.chunk, ...), custom_call_target="tpu_custom_call" | custom-call | flops 3221225472 | bytes 1048576 | tf_op jit(solution)/shard_map/parts_2/pallas_call | solution.py:197
  60.6 5.2 %collective-permute-start.12 = (bf16[256,512]{1,0:T(8,128)(2,1)S(1)}, bf16[256,512]{1,0:T(8,128)(2,1)S(1)}, u32[]{:S(2)}, u32[]{:S(2)}) collective-permute-start(bf16[256,512]{1,0:T(8,128)(2,1)S(1)} %get-tuple-element.97), channel_id=1, source_target_pairs={{0,252},{1,253},{2,254},{3,255},{4,0},{5,1},{6,2},{7,3},{8,4},{9,5... | collective-permute-start | bytes 786440 | tf_op jit(solution)/shard_map/ppermute | solution.py:268
  65.9 0.1 collective-permute-start.11
  66.0 3.4 %parts_1.1 = (bf16[256,512]{1,0:T(8,128)(2,1)S(1)}, f32[256,1024]{1,0:T(8,128)S(1)}) custom-call(s32[2]{0:T(128)S(1)} %copy-done.2, bf16[4096,128]{1,0:T(8,128)(2,1)S(1)} %get-tuple-element.61.query_all, bf16[4096,128]{1,0:T(8,128)(2,1)S(1)} %copy-done.5, bf16[272,512]{1,0:T(8,128)(2,1)S(1)} %collective-permute-done.5.chunk, ...), custom_call_target="tpu_custom_call" | custom-call | flops 3221225472 | bytes 1048576 | tf_op jit(solution)/shard_map/parts_1/pallas_call | solution.py:197
  69.3 2.4 %collective-permute-start.15 = (bf16[256,512]{1,0:T(8,128)(2,1)S(1)}, bf16[256,512]{1,0:T(8,128)(2,1)S(1)}, u32[]{:S(2)}, u32[]{:S(2)}) collective-permute-start(bf16[256,512]{1,0:T(8,128)(2,1)S(1)} %get-tuple-element.108), channel_id=1, source_target_pairs={{0,254},{1,255},{2,0},{3,1},{4,2},{5,3},{6,4},{7,5},{8,6},{9,7},{1... | collective-permute-start | bytes 786440 | tf_op jit(solution)/shard_map/ppermute | solution.py:268
  71.7 1.3 %collective-permute-start.13 = (f32[16]{0:T(128)S(1)}, f32[16]{0:T(128)S(1)}, u32[]{:S(2)}, u32[]{:S(2)}) collective-permute-start(f32[16]{0:T(128)S(1)} %add.60), channel_id=1, source_target_pairs={{0,32},{1,33},{2,34},{3,35},{4,36},{5,37},{6,38},{7,39},{8,40},{9,... | collective-permute-start | bytes 200 | tf_op jit(solution)/shard_map/ppermute | solution.py:274
  73.1 3.5 %parts_0.1 = (f32[256,512]{1,0:T(8,128)S(1)}, bf16[128,1024]{1,0:T(8,128)(2,1)S(1)}, bf16[128,1024]{1,0:T(8,128)(2,1)S(1)}) custom-call(s32[2]{0:T(128)S(1)} %copy-done.2, bf16[4096,128]{1,0:T(8,128)(2,1)S(1)} %get-tuple-element.61.query_all, bf16[4096,128]{1,0:T(8,128)(2,1)S(1)} %copy-done.5, bf16[272,512]{1,0:T(8,128)(2,1)S(1)} %maximum_maximum_fusion.chunk.own_chunk, ...), custom_call_target="tpu_custom_call" | custom-call | flops 3221225472 | bytes 1048576 | tf_op jit(solution)/shard_map/parts_0/pallas_call | solution.py:197
  76.6 1.8 %collective-permute-done.13 = f32[16]{0:T(128)S(1)} collective-permute-done((f32[16]{0:T(128)S(1)}, f32[16]{0:T(128)S(1)}, u32[]{:S(2)}, u32[]{:S(2)}) %collective-permute-start.13) | collective-permute-done | bytes 96 | tf_op jit(solution)/shard_map/ppermute | solution.py:274
  78.4 5.2 %collective-permute-start.14 = (bf16[128,1024]{1,0:T(8,128)(2,1)S(1)}, bf16[128,1024]{1,0:T(8,128)(2,1)S(1)}, u32[]{:S(2)}, u32[]{:S(2)}) collective-permute-start(bf16[128,1024]{1,0:T(8,128)(2,1)S(1)} %get-tuple-element.103), channel_id=1, source_target_pairs={{0,1},{1,0},{2,3},{3,2},{4,5},{5,4},{6,7},{7,6},{8,9},{9,8},{10,11... | collective-permute-start | bytes 786440 | tf_op jit(solution)/shard_map/ppermute | solution.py:274
  83.6 0.2 add_convert_fusion
  83.8 0.1 collective-permute-start.16
  84.0 2.4 %collective-permute-done.17 = f32[16]{0:T(128)S(1)} collective-permute-done((f32[16]{0:T(128)S(1)}, f32[16]{0:T(128)S(1)}, u32[]{:S(2)}, u32[]{:S(2)}) %collective-permute-start.17) | collective-permute-done | bytes 96 | tf_op jit(solution)/shard_map/ppermute | solution.py:274
  86.5 3.8 %collective-permute-done.18 = f32[16]{0:T(128)S(1)} collective-permute-done((f32[16]{0:T(128)S(1)}, f32[16]{0:T(128)S(1)}, u32[]{:S(2)}, u32[]{:S(2)}) %collective-permute-start.18) | collective-permute-done | bytes 96 | tf_op jit(solution)/shard_map/ppermute | solution.py:274
  90.3 2.7 %collective-permute-start.19 = (f32[16]{0:T(128)S(1)}, f32[16]{0:T(128)S(1)}, u32[]{:S(2)}, u32[]{:S(2)}) collective-permute-start(f32[16]{0:T(128)S(1)} %add.67), channel_id=1, source_target_pairs={{0,1},{1,0},{2,3},{3,2},{4,5},{5,4},{6,7},{7,6},{8,9},{9,8},{10,11... | collective-permute-start | bytes 200 | tf_op jit(solution)/shard_map/ppermute | solution.py:274
  93.0 0.8 collective-permute-done.19
  93.8 0.6 broadcast_select_fusion.3
  94.4 1.3 %join.1 = (bf16[128,512]{1,0:T(8,128)(2,1)}, bf16[128,512]{1,0:T(8,128)(2,1)}) custom-call(s32[2]{0:T(128)S(1)} %copy-done.2, bf16[128,512]{1,0:T(8,128)(2,1)S(1)} %get-tuple-element.116.mine, bf16[128,512]{1,0:T(8,128)(2,1)S(1)} %collective-permute-done.16.theirs), custom_call_target="tpu_custom_call" | custom-call | flops 1048576 | bytes 1048576 | tf_op jit(solution)/shard_map/join/pallas_call | solution.py:197
  95.7 0.9 maximum_select_fusion
  (37 shorter events, 0.6 us)
Async XLA Ops:
  4.0 4.5 %collective-permute-start = (bf16[144,512]{1,0:T(8,128)(2,1)}, bf16[144,512]{1,0:T(8,128)(2,1)S(1)}, u32[]{:S(2)}, u32[]{:S(2)}) collective-permute-start(bf16[144,512]{1,0:T(8,128)(2,1)} %get-tuple-element.58), channel_id=1, source_target_pairs={{0,1},{1,0},{2,3},{3,2},{4,5},{5,4},{6,7},{7,6},{8,9},{9,8},{10,11... | collective-permute-start | bytes 442376 | tf_op jit(solution)/shard_map/ppermute | solution.py:274
  8.6 2.9 %collective-permute-start.1 = (bf16[256,1024]{1,0:T(8,128)(2,1)}, bf16[256,1024]{1,0:T(8,128)(2,1)S(1)}, u32[]{:S(2)}, u32[]{:S(2)}) collective-permute-start(bf16[256,1024]{1,0:T(8,128)(2,1)} %get-tuple-element.60), channel_id=1, source_target_pairs={{0,1},{1,0},{2,3},{3,2},{4,5},{5,4},{6,7},{7,6},{8,9},{9,8},{10,11... | collective-permute-start | bytes 1572872 | tf_op jit(solution)/shard_map/ppermute | solution.py:274
  10.3 1.2 %copy-start = (bf16[128,2048]{1,0:T(8,128)(2,1)S(1)}, bf16[128,2048]{1,0:T(8,128)(2,1)}, u32[]{:S(2)}) copy-start(bf16[128,2048]{1,0:T(8,128)(2,1)} %q_own.1) | copy-start | bytes 1572868
  10.3 1.3 %copy-start.1 = (bf16[128,2048]{1,0:T(8,128)(2,1)S(1)}, bf16[128,2048]{1,0:T(8,128)(2,1)}, u32[]{:S(2)}) copy-start(bf16[128,2048]{1,0:T(8,128)(2,1)} %g_own.1) | copy-start | bytes 1572868
  11.4 0.7 copy-start.2
  11.4 13.0 %collective-permute-start.2 = (bf16[272,512]{1,0:T(8,128)(2,1)S(1)}, bf16[272,512]{1,0:T(8,128)(2,1)S(1)}, u32[]{:S(2)}, u32[]{:S(2)}) collective-permute-start(bf16[272,512]{1,0:T(8,128)(2,1)S(1)} %maximum_maximum_fusion.chunk.own_chunk), channel_id=1, source_target_pairs={{0,8},{1,9},{2,10},{3,11},{4,12},{5,13},{6,14},{7,15},{8,16},{9,17... | collective-permute-start | bytes 835592 | tf_op jit(solution)/shard_map/ppermute | solution.py:268
  13.1 29.8 %copy-start.4 = (bf16[4096,128]{1,0:T(8,128)(2,1)}, bf16[4096,128]{1,0:T(8,128)(2,1)S(1)}, u32[]{:S(2)}) copy-start(bf16[4096,128]{1,0:T(8,128)(2,1)S(1)} %get-tuple-element.62.grad_all) | copy-start | bytes 3145732
  13.1 0.7 copy-start.3
  24.5 8.9 %collective-permute-start.5 = (bf16[272,512]{1,0:T(8,128)(2,1)S(1)}, bf16[272,512]{1,0:T(8,128)(2,1)S(1)}, u32[]{:S(2)}, u32[]{:S(2)}) collective-permute-start(bf16[272,512]{1,0:T(8,128)(2,1)S(1)} %get-tuple-element.112), channel_id=1, source_target_pairs={{0,2},{1,3},{2,4},{3,5},{4,6},{5,7},{6,0},{7,1},{8,10},{9,11},{10,... | collective-permute-start | bytes 835592 | tf_op jit(solution)/shard_map/ppermute | solution.py:268
  25.9 14.6 %collective-permute-start.4 = (bf16[272,512]{1,0:T(8,128)(2,1)S(1)}, bf16[272,512]{1,0:T(8,128)(2,1)S(1)}, u32[]{:S(2)}, u32[]{:S(2)}) collective-permute-start(bf16[272,512]{1,0:T(8,128)(2,1)S(1)} %get-tuple-element.113), channel_id=1, source_target_pairs={{0,4},{1,5},{2,6},{3,7},{4,0},{5,1},{6,2},{7,3},{8,12},{9,13},{10,... | collective-permute-start | bytes 835592 | tf_op jit(solution)/shard_map/ppermute | solution.py:268
  28.5 14.3 %collective-permute-start.3 = (bf16[272,512]{1,0:T(8,128)(2,1)S(1)}, bf16[272,512]{1,0:T(8,128)(2,1)S(1)}, u32[]{:S(2)}, u32[]{:S(2)}) collective-permute-start(bf16[272,512]{1,0:T(8,128)(2,1)S(1)} %get-tuple-element.114), channel_id=1, source_target_pairs={{0,6},{1,7},{2,0},{3,1},{4,2},{5,3},{6,4},{7,5},{8,14},{9,15},{10,... | collective-permute-start | bytes 835592 | tf_op jit(solution)/shard_map/ppermute | solution.py:268
  45.3 5.7 %collective-permute-start.6 = (f32[16]{0:T(128)S(1)}, f32[16]{0:T(128)S(1)}, u32[]{:S(2)}, u32[]{:S(2)}) collective-permute-start(f32[16]{0:T(128)S(1)} %reduce_sum.9), channel_id=1, source_target_pairs={{0,2},{1,3},{2,0},{3,1},{4,6},{5,7},{6,4},{7,5},{8,10},{9,11},{10,... | collective-permute-start | bytes 200 | tf_op jit(solution)/shard_map/ppermute | solution.py:274
  45.4 1.2 %copy-start.5 = (bf16[4096,128]{1,0:T(8,128)(2,1)S(1)}, bf16[4096,128]{1,0:T(8,128)(2,1)}, u32[]{:S(2)}) copy-start(bf16[4096,128]{1,0:T(8,128)(2,1)} %copy-done.4) | copy-start | bytes 3145732
  50.0 6.6 %collective-permute-start.8 = (bf16[256,512]{1,0:T(8,128)(2,1)S(1)}, bf16[256,512]{1,0:T(8,128)(2,1)S(1)}, u32[]{:S(2)}, u32[]{:S(2)}) collective-permute-start(bf16[256,512]{1,0:T(8,128)(2,1)S(1)} %get-tuple-element.89), channel_id=1, source_target_pairs={{0,248},{1,249},{2,250},{3,251},{4,252},{5,253},{6,254},{7,255},{8... | collective-permute-start | bytes 786440 | tf_op jit(solution)/shard_map/ppermute | solution.py:268
  51.0 5.5 %collective-permute-start.7 = (f32[16]{0:T(128)S(1)}, f32[16]{0:T(128)S(1)}, u32[]{:S(2)}, u32[]{:S(2)}) collective-permute-start(f32[16]{0:T(128)S(1)} %add.57), channel_id=1, source_target_pairs={{0,4},{1,5},{2,6},{3,7},{4,0},{5,1},{6,2},{7,3},{8,12},{9,13},{10,... | collective-permute-start | bytes 200 | tf_op jit(solution)/shard_map/ppermute | solution.py:274
  56.5 9.4 %collective-permute-start.10 = (bf16[256,512]{1,0:T(8,128)(2,1)S(1)}, bf16[256,512]{1,0:T(8,128)(2,1)S(1)}, u32[]{:S(2)}, u32[]{:S(2)}) collective-permute-start(bf16[256,512]{1,0:T(8,128)(2,1)S(1)} %get-tuple-element.93), channel_id=1, source_target_pairs={{0,250},{1,251},{2,252},{3,253},{4,254},{5,255},{6,0},{7,1},{8,2},... | collective-permute-start | bytes 786440 | tf_op jit(solution)/shard_map/ppermute | solution.py:268
  56.6 9.3 %collective-permute-start.9 = (f32[16]{0:T(128)S(1)}, f32[16]{0:T(128)S(1)}, u32[]{:S(2)}, u32[]{:S(2)}) collective-permute-start(f32[16]{0:T(128)S(1)} %add.58), channel_id=1, source_target_pairs={{0,8},{1,9},{2,10},{3,11},{4,12},{5,13},{6,14},{7,15},{8,0},{9,1},... | collective-permute-start | bytes 200 | tf_op jit(solution)/shard_map/ppermute | solution.py:274
  60.6 11.1 %collective-permute-start.12 = (bf16[256,512]{1,0:T(8,128)(2,1)S(1)}, bf16[256,512]{1,0:T(8,128)(2,1)S(1)}, u32[]{:S(2)}, u32[]{:S(2)}) collective-permute-start(bf16[256,512]{1,0:T(8,128)(2,1)S(1)} %get-tuple-element.97), channel_id=1, source_target_pairs={{0,252},{1,253},{2,254},{3,255},{4,0},{5,1},{6,2},{7,3},{8,4},{9,5... | collective-permute-start | bytes 786440 | tf_op jit(solution)/shard_map/ppermute | solution.py:268
  65.9 5.8 %collective-permute-start.11 = (f32[16]{0:T(128)S(1)}, f32[16]{0:T(128)S(1)}, u32[]{:S(2)}, u32[]{:S(2)}) collective-permute-start(f32[16]{0:T(128)S(1)} %add.59), channel_id=1, source_target_pairs={{0,16},{1,17},{2,18},{3,19},{4,20},{5,21},{6,22},{7,23},{8,24},{9,... | collective-permute-start | bytes 200 | tf_op jit(solution)/shard_map/ppermute | solution.py:274
  69.3 14.3 %collective-permute-start.15 = (bf16[256,512]{1,0:T(8,128)(2,1)S(1)}, bf16[256,512]{1,0:T(8,128)(2,1)S(1)}, u32[]{:S(2)}, u32[]{:S(2)}) collective-permute-start(bf16[256,512]{1,0:T(8,128)(2,1)S(1)} %get-tuple-element.108), channel_id=1, source_target_pairs={{0,254},{1,255},{2,0},{3,1},{4,2},{5,3},{6,4},{7,5},{8,6},{9,7},{1... | collective-permute-start | bytes 786440 | tf_op jit(solution)/shard_map/ppermute | solution.py:268
  71.7 6.6 %collective-permute-start.13 = (f32[16]{0:T(128)S(1)}, f32[16]{0:T(128)S(1)}, u32[]{:S(2)}, u32[]{:S(2)}) collective-permute-start(f32[16]{0:T(128)S(1)} %add.60), channel_id=1, source_target_pairs={{0,32},{1,33},{2,34},{3,35},{4,36},{5,37},{6,38},{7,39},{8,40},{9,... | collective-permute-start | bytes 200 | tf_op jit(solution)/shard_map/ppermute | solution.py:274
  78.4 17.3 %collective-permute-start.14 = (bf16[128,1024]{1,0:T(8,128)(2,1)S(1)}, bf16[128,1024]{1,0:T(8,128)(2,1)S(1)}, u32[]{:S(2)}, u32[]{:S(2)}) collective-permute-start(bf16[128,1024]{1,0:T(8,128)(2,1)S(1)} %get-tuple-element.103), channel_id=1, source_target_pairs={{0,1},{1,0},{2,3},{3,2},{4,5},{5,4},{6,7},{7,6},{8,9},{9,8},{10,11... | collective-permute-start | bytes 786440 | tf_op jit(solution)/shard_map/ppermute | solution.py:274
  83.8 10.6 %collective-permute-start.16 = (bf16[128,512]{1,0:T(8,128)(2,1)S(1)}, bf16[128,512]{1,0:T(8,128)(2,1)S(1)}, u32[]{:S(2)}, u32[]{:S(2)}) collective-permute-start(bf16[128,512]{1,0:T(8,128)(2,1)S(1)} %get-tuple-element.115), channel_id=1, source_target_pairs={{0,1},{1,0},{2,3},{3,2},{4,5},{5,4},{6,7},{7,6},{8,9},{9,8},{10,11... | collective-permute-start | bytes 393224 | tf_op jit(solution)/shard_map/ppermute | solution.py:274
  83.9 2.5 %collective-permute-start.17 = (f32[16]{0:T(128)S(1)}, f32[16]{0:T(128)S(1)}, u32[]{:S(2)}, u32[]{:S(2)}) collective-permute-start(f32[16]{0:T(128)S(1)} %add.61), channel_id=1, source_target_pairs={{0,64},{1,65},{2,66},{3,67},{4,68},{5,69},{6,70},{7,71},{8,72},{9,... | collective-permute-start | bytes 200 | tf_op jit(solution)/shard_map/ppermute | solution.py:274
  86.4 3.9 %collective-permute-start.18 = (f32[16]{0:T(128)S(1)}, f32[16]{0:T(128)S(1)}, u32[]{:S(2)}, u32[]{:S(2)}) collective-permute-start(f32[16]{0:T(128)S(1)} %add.66), channel_id=1, source_target_pairs={{0,128},{1,129},{2,130},{3,131},{4,132},{5,133},{6,134},{7,135},{8... | collective-permute-start | bytes 200 | tf_op jit(solution)/shard_map/ppermute | solution.py:274
  90.3 3.5 %collective-permute-start.19 = (f32[16]{0:T(128)S(1)}, f32[16]{0:T(128)S(1)}, u32[]{:S(2)}, u32[]{:S(2)}) collective-permute-start(f32[16]{0:T(128)S(1)} %add.67), channel_id=1, source_target_pairs={{0,1},{1,0},{2,3},{3,2},{4,5},{5,4},{6,7},{7,6},{8,9},{9,8},{10,11... | collective-permute-start | bytes 200 | tf_op jit(solution)/shard_map/ppermute | solution.py:274

commit v3 on v2

--- a/solution.py
+++ b/solution.py
@@ -46,7 +46,8 @@
     return jnp.where(allowed, 0.0, MASKED)
 
 
-def prep_kernel(place, q_own, g_own, both_peer, query_all, grad_all):
+def prep_kernel(place, q_own, g_own, both_peer, rows_all):
+    query_all, grad_all = split_rows(rows_all)
     core = place[0]
     q_peer, g_peer = both_peer.at[:TOK, :], both_peer.at[TOK:, :]
     lane_half = lax.broadcasted_iota(jnp.int32, (CHIP, 128), 1) // HEAD_DIM
@@ -62,6 +63,10 @@
                 out[head_rows(2 * pair + e), :] = chosen.astype(BF16)
 
 
+def split_rows(rows_all):
+    return rows_all.at[: 16 * CHIP, :], rows_all.at[16 * CHIP :, :]
+
+
 def head_rows(head):
     return slice(head * CHIP, (head + 1) * CHIP)
 
@@ -70,11 +75,13 @@
     return slice(first_lane + tile * 128, first_lane + tile * 128 + 128)
 
 
-def stats_kernel(hop, last, place, sinks, query_all, grad_all, chunk, own_chunk, *refs):
+def stats_kernel(hop, last, place, sinks, rows_all, chunk, own_chunk, *refs):
+    query_all, grad_all = split_rows(rows_all)
     before, after = refs[:3], refs[3:]
     if hop == 0:
         before, after = None, refs
-    (top_out, second, third), bias = after[:3], after[-1]
+    top_out, second, third = after[:3]
+    bias, sink_rows = after[-2:]
     core = place[0]
     bias[...] = mask_bias(place, chunk, own_chunk, hop)
     for head in range(16):
@@ -99,15 +106,19 @@
             delta = weighed * share
             second[at, :] = share
             third[at, :] = delta
-            after[3][at, :] = -jnp.exp2((sink - top) * EXP2_SCALE) * share * delta
+            sink_rows[at, :] = -jnp.exp2((sink - top) * EXP2_SCALE) * share * delta
         else:
             second[at, :] = denom
             third[at, :] = weighed
+    if last:
+        sums = jnp.sum(sink_rows[...], 1, keepdims=True)
+        after[3][...] = jnp.transpose(jnp.broadcast_to(sums, (16, 128)))[0:1, :]
 
 
 def parts_kernel(
-    hop, place, query_all, grad_all, chunk, own_chunk, tops, shares, deltas, *refs
+    hop, place, rows_all, chunk, own_chunk, tops, shares, deltas, *refs
 ):
+    query_all, grad_all = split_rows(rows_all)
     weight, dscore, bias = refs[-3:]
     dq_in = None if hop == HOPS else refs[0]
     outs = refs[:-3] if hop == HOPS else refs[1:-3]
@@ -150,70 +161,31 @@
                 outs[2][:, lane_tile(2 * g + pair)] = dq[TOK:]
 
 
-def pack_kernel(place, segment, keys, values, queries, grads, own, send, tokens, sems):
-    core = place[0]
-
-    def half(ref, which, width):
-        return ref.at[:, pl.ds(pl.multiple_of(which * width, width), width)]
-
-    moves = []
-    for out, which in ((send, 1 - core), (own, core)):
-        moves.append((half(keys, which, HALF_KV), out.at[:TOK, :HALF_KV]))
-        moves.append((half(values, which, HALF_KV), out.at[:TOK, HALF_KV:]))
-    moves.append((half(queries, 1 - core, 1024), tokens.at[:TOK, :]))
-    moves.append((half(grads, 1 - core, 1024), tokens.at[TOK:, :]))
-    copies = [
-        pltpu.make_async_copy(source, target, sems.at[n])
-        for n, (source, target) in enumerate(moves)
-    ]
-    for copy in copies:
-        copy.start()
-    marks = jnp.broadcast_to(segment[...], (16, TOK)).astype(F32).astype(BF16)
-    for out in (own, send):
-        for lane in range(0, 2 * HALF_KV, TOK):
-            out[TOK:, lane : lane + TOK] = marks
-    for copy in copies:
-        copy.wait()
-
-
-def join_kernel(place, mine, theirs, *outs):
-    core = place[0]
-    width = mine.shape[1] // len(outs)
-    for n, out in enumerate(outs):
-        for which, part in ((core, mine), (1 - core, theirs)):
-            at = pl.ds(pl.multiple_of(which * width, width), width)
-            out[:, at] = part[:, n * width : (n + 1) * width]
-
-
 SMEM = pl.BlockSpec(memory_space=pltpu.SMEM)
 VMEM = pl.BlockSpec(memory_space=pltpu.VMEM)
 STAT = jax.ShapeDtypeStruct((16, CHIP), F32)
 
 
-def run(
-    kernel, name, n_scalars, operands, out_shape, scratch, flops, interpret, n_far=0, vmem=16
-):
-    n_arrays = len(operands) - n_scalars - n_far
+def run(kernel, name, n_scalars, operands, out_shape, scratch, flops, interpret):
+    n_arrays = len(operands) - n_scalars
     return pl.pallas_call(
         kernel,
         name=name,
-        in_specs=[SMEM] * n_scalars
-        + [VMEM] * n_arrays
-        + [pl.BlockSpec(memory_space=pltpu.HBM)] * n_far,
+        in_specs=[SMEM] * n_scalars + [VMEM] * n_arrays,
         out_specs=[VMEM] * len(out_shape),
         out_shape=out_shape,
         scratch_shapes=scratch,
-        compiler_params=pltpu.CompilerParams(vmem_limit_bytes=vmem << 20),
+        compiler_params=pltpu.CompilerParams(vmem_limit_bytes=16 << 20),
         cost_estimate=pl.CostEstimate(flops=flops, transcendentals=0, bytes_accessed=1 << 20),
         interpret=interpret,
     )(*operands)
 
 
 def prepared(place, queries, out_grad, both_peer, interpret):
-    rows = jax.ShapeDtypeStruct((16 * CHIP, 128), BF16)
+    rows = jax.ShapeDtypeStruct((32 * CHIP, 128), BF16)
     return run(
         prep_kernel, "prep", 1, (place, queries, out_grad, both_peer),
-        [rows, rows], [], 1 << 30, interpret,
+        [rows], [], 1 << 30, interpret,
     )
 
 
@@ -221,8 +193,8 @@
     return run(
         functools.partial(stats_kernel, hop, last), f"stats_{hop}", 2,
         (place, sinks, *tokens, chunk, own_chunk, *before),
-        [STAT] * (4 if last else 3),
-        [pltpu.VMEM((CHIP, CHIP), F32)], 2 << 30, interpret,
+        [STAT] * 3 + [jax.ShapeDtypeStruct((1, 16), F32)] * last,
+        [pltpu.VMEM((CHIP, CHIP), F32), pltpu.VMEM((16, CHIP), F32)], 2 << 30, interpret,
     )
 
 
@@ -241,24 +213,6 @@
     )
 
 
-def packed(place, key_heads, value_heads, segment, queries, out_grad, interpret):
-    rows = jax.ShapeDtypeStruct((TOK + 16, 2 * HALF_KV), BF16)
-    return run(
-        pack_kernel, "pack", 1,
-        (place, segment[None, :], key_heads, value_heads, queries, out_grad),
-        [rows, rows, jax.ShapeDtypeStruct((2 * TOK, 1024), BF16)],
-        [pltpu.SemaphoreType.DMA((6,))], 1 << 20, interpret, n_far=4, vmem=62,
-    )
-
-
-def joined(place, mine, theirs, outs, interpret):
-    width = mine.shape[1] // outs
-    shape = jax.ShapeDtypeStruct((TOK, 2 * width), BF16)
-    return run(
-        join_kernel, "join", 1, (place, mine, theirs), [shape] * outs, [], 1 << 20, interpret
-    )
-
-
 def per_device(count, interpret, queries, key_heads, value_heads, out_grad, segment, sink_logits):
     index = lax.axis_index("ctx")
     core, chip = index % 2, index // 2
@@ -277,14 +231,25 @@
         return i // 8 * 8 + (i // 2 + hop) % ROW * 2 + i % 2
 
     place = jnp.stack([core, chip]).astype(jnp.int32)
-    own, kv_send, tokens_send = packed(
-        place, key_heads, value_heads, segment, queries, out_grad, interpret
+    def either(array, middle):
+        return array[:, :middle], array[:, middle:]
+
+    k_low, k_high = either(key_heads, HALF_KV)
+    v_low, v_high = either(value_heads, HALF_KV)
+    kv_low = jnp.concatenate([k_low, v_low], 1)
+    kv_high = jnp.concatenate([k_high, v_high], 1)
+    own, send = jnp.where(first, kv_low, kv_high), jnp.where(first, kv_high, kv_low)
+    marks = jnp.pad(segment.astype(BF16)[None, :], ((0, 15), (0, 2 * HALF_KV - TOK)))
+    kv_send = jnp.concatenate([send, marks], 0)
+    queries, out_grad, kv_send = lax.optimization_barrier((queries, out_grad, kv_send))
+    q_low, q_high = either(queries, 1024)
+    g_low, g_high = either(out_grad, 1024)
+    tokens_send = jnp.concatenate(
+        [jnp.where(first, q_high, q_low), jnp.where(first, g_high, g_low)], 0
     )
     came, tokens_send = lax.optimization_barrier((crossed(kv_send, 1), tokens_send))
-    marks = jnp.concatenate(
-        [own[TOK:, :TOK], came[TOK:, TOK:CHIP], own[TOK:, CHIP:]], 1
-    )
-    chunk = jnp.concatenate([own[:TOK], came[:TOK], marks], 0)
+    marks_both = jnp.concatenate([marks[:, :TOK], came[TOK:, :TOK], marks[:, CHIP:]], 1)
+    chunk = jnp.concatenate([own, came[:TOK], marks_both], 0)
     chunks = {0: chunk, HOPS: shifted(chunk, HOPS)}
     both = crossed(tokens_send, 1)
     tokens = prepared(place, queries, out_grad, both, interpret)
@@ -301,9 +266,9 @@
         stats = stats_of(
             hop, hop == 3, place, sink_logits, tokens, chunks[hop], chunk, stats, interpret
         )
-    *stats, sink_rows = stats
-    sink_grad = jnp.sum(sink_rows, -1)
-    bits = [1 << n for n in range(1, count.bit_length() - 1)]
+    *stats, sink_row = stats
+    sink_grad = sink_row.reshape(16)
+    bits = [bit for bit in (4, 16, 32, 128, 8, 64, 2) if bit < count]
 
     def widened(value):
         return value + crossed(value, bits.pop(0)) if bits else value
@@ -311,34 +276,37 @@
     dq, came_back = (), {}
     for hop in range(HOPS, 0, -1):
         part, *dq = parts_of(hop, place, tokens, chunks[hop], chunk, stats, dq, interpret)
+        part, sink_grad = lax.optimization_barrier((part, widened(sink_grad)))
         came_back[hop] = shifted(part, -hop)
-        sink_grad = widened(sink_grad)
-        if hop + 1 in came_back:
+        if hop > 1:
+            sink_grad = widened(sink_grad)
+        else:
+            sink_half, sink_grad = sink_grad, crossed(sink_grad, 1)
+        if hop < HOPS:
             dq[0], sink_grad, came_back[hop + 1] = lax.optimization_barrier(
                 (dq[0], sink_grad, came_back[hop + 1])
             )
         else:
             dq[0], sink_grad = lax.optimization_barrier((dq[0], sink_grad))
     total, dq_own, dq_peer = parts_of(0, place, tokens, chunk, chunk, stats, dq, interpret)
-    dq_own, dq_peer, sink_grad = lax.optimization_barrier(
-        (dq_own, dq_peer, widened(sink_grad))
-    )
-    dq_came = crossed(dq_peer, 1)
-    query_grad = jnp.where(
+
+    def joined(mine, theirs):
+        return jnp.where(
+            first, jnp.concatenate([mine, theirs], 1), jnp.concatenate([theirs, mine], 1)
+        )
+
+    sink_grad = jnp.where(
         first,
-        jnp.concatenate([dq_own, dq_came], 1),
-        jnp.concatenate([dq_came, dq_own], 1),
-    )
+        jnp.concatenate([sink_half, sink_grad]),
+        jnp.concatenate([sink_grad, sink_half]),
+    )
+    query_grad = joined(dq_own, crossed(dq_peer, 1))
     for part in came_back.values():
         total = total + part.astype(F32)
     total = total.astype(BF16)
-    key_grad, value_grad = joined(place, total[:TOK], crossed(total[TOK:], 1), 2, interpret)
-    while bits:
-        sink_grad = widened(sink_grad)
-    other = crossed(sink_grad, 1)
-    sink_grad = jnp.where(
-        first, jnp.concatenate([sink_grad, other]), jnp.concatenate([other, sink_grad])
-    )
+    came, query_grad = lax.optimization_barrier((crossed(total[TOK:], 1), query_grad))
+    key_grad = joined(total[:TOK, :HALF_KV], came[:, :HALF_KV])
+    value_grad = joined(total[:TOK, HALF_KV:], came[:, HALF_KV:])
     return query_grad, key_grad, value_grad, sink_grad
 
 

time: 96.9 us -> 93.1 us (0.961)
  waiting for transfers between devices: 24.8 us -> 20.1 us
  starting transfers between devices: 30 us -> 34 us
  local copies, waits for them, and re-layouts: 4.87 us -> 1.84 us
  other arithmetic: 2.57 us -> 5.32 us
  Pallas kernels: 33.4 us -> 30.7 us
    ppermute x12, waiting for transfers between devices: 10.1 us -> 5.42 us  [crossed(): return lax.ppermute(block, 'ctx', [(i, i ^ bit) for i in range(count)])]
    pallas_call x13 -> x11, Pallas kernels: 33.4 us -> 30.7 us  [run(): pl.pallas_call(kernel, name=name, in_specs=[SMEM] * n_scalars + [VMEM] *...]
    select_n x2 -> x6, other arithmetic: 1.51 us -> 4.17 us  [the longest x3 2.29 us: joined(): jnp.where(first, jnp.concatenate([mine, theirs], 1), jnp.concatenate([the...]
    unnamed x12 -> x6, local copies, waits for them, and re-layouts: 2.46 us -> 0.02 us
    ppermute x8, starting transfers between devices: 13.9 us -> 16.3 us  [sent(): return lax.ppermute(block, 'ctx', route)]
    ppermute x12, starting transfers between devices: 16.2 us -> 17.8 us  [crossed(): return lax.ppermute(block, 'ctx', [(i, i ^ bit) for i in range(count)])]
    slice x5 -> x8, local copies, waits for them, and re-layouts: 2.39 us -> 1.81 us  [the longest x2 1.77 us: either(): return (array[:, :middle], array[:, middle:])]
  transfers between devices with their start and end apart: 20 -> 20, of which waited for: 8 -> 8; matrix products, arithmetic and copies ran while one was open for 3% -> 3% of each run, Pallas kernels for 29% -> 30%
where the time goes in v3:
time: 93.1 us; the launch traced here: 92.9 us
  starting transfers between devices  34 us (37%)
  Pallas kernels  30.7 us (33%)
  waiting for transfers between devices  20.1 us (22%)
  other arithmetic  5.32 us (6%)
  local copies, waits for them, and re-layouts  1.84 us (2%)
    pallas_call x11, Pallas kernels, run(): pl.pallas_call(kernel, name=name, in_specs=[SMEM] * n_scalars + [VMEM] *...  30.7 us
    ppermute x12, starting transfers between devices, crossed(): return lax.ppermute(block, 'ctx', [(i, i ^ bit) for i in range(count)])  17.8 us
    ppermute x8, starting transfers between devices, sent(): return lax.ppermute(block, 'ctx', route)  16.3 us
    ppermute x8, waiting for transfers between devices, sent(): return lax.ppermute(block, 'ctx', route)  14.7 us
    ppermute x12, waiting for transfers between devices, crossed(): return lax.ppermute(block, 'ctx', [(i, i ^ bit) for i in range(count)])  5.42 us
    select_n x3, other arithmetic, joined(): jnp.where(first, jnp.concatenate([mine, theirs], 1), jnp.concatenate([the...  2.29 us
  transfers between devices with their start and end apart: 20, of which 8 were waited for; matrix products, arithmetic and copies ran while one was open for 3% of the time, Pallas kernels for 30%

profile of v3, /device:TPU:1, one launch (start us, length us, event | category | flops | bytes accessed | tf_op | source)
XLA Modules:
  0.0 92.9 jit_solution(2901800359225513496)
XLA Ops:
  0.6 0.7 convert_bitcast_fusion
  1.3 0.9 fusion.2
  2.2 0.9 fusion.3
  3.2 3.3 %collective-permute-start = (bf16[144,512]{1,0:T(8,128)(2,1)S(1)}, bf16[144,512]{1,0:T(8,128)(2,1)S(1)}, u32[]{:S(2)}, u32[]{:S(2)}) collective-permute-start(bf16[144,512]{1,0:T(8,128)(2,1)S(1)} %pad_maximum_fusion.1), channel_id=1, source_target_pairs={{0,1},{1,0},{2,3},{3,2},{4,5},{5,4},{6,7},{7,6},{8,9},{9,8},{10,11... | collective-permute-start | bytes 442376 | tf_op jit(solution)/shard_map/ppermute | solution.py:228
  6.5 1.2 %slice_select_fusion = (bf16[128,1024]{1,0:T(8,128)(2,1)S(1)}, bf16[128,1024]{1,0:T(8,128)(2,1)S(1)}) fusion(bf16[128,2048]{1,0:T(8,128)(2,1)} %g_own, pred[]{:T(512)S(6)} %eq.8, bf16[128,2048]{1,0:T(8,128)(2,1)} %q_own), kind=kLoop, calls=%fused_computation.7 | loop fusion | flops 262144 | bytes 1572865 | tf_op jit(solution)/shard_map/jit(_where)/select_n | solution.py:248
  7.8 0.2 collective-permute-start.1
  8.2 0.1 collective-permute-start.2
  8.3 1.6 %collective-permute-done.1.both_peer = bf16[256,1024]{1,0:T(8,128)(2,1)S(1)} collective-permute-done((bf16[256,1024]{1,0:T(8,128)(2,1)S(1)}, bf16[256,1024]{1,0:T(8,128)(2,1)S(1)}, u32[]{:S(2)}, u32[]{:S(2)}) %collective-permute-start.1) | collective-permute-done | bytes 524320 | tf_op jit(solution)/shard_map/ppermute | solution.py:228
  9.8 1.0 %prep.1.rows_all = bf16[8192,128]{1,0:T(8,128)(2,1)S(1)} custom-call(s32[2]{0:T(128)S(1)} %pad_add_fusion.place, bf16[128,2048]{1,0:T(8,128)(2,1)S(1)} %copy-done, bf16[128,2048]{1,0:T(8,128)(2,1)S(1)} %copy-done.1, bf16[256,1024]{1,0:T(8,128)(2,1)S(1)} %collective-permute-done.1.both_peer), custom_call_target="tpu_custom_call" | custom-call | flops 1073741824 | bytes 1048576 | tf_op jit(solution)/shard_map/prep/pallas_call | solution.py:171
  10.8 2.3 %stats_0.1 = (f32[16,256]{1,0:T(8,128)S(1)}, f32[16,256]{1,0:T(8,128)S(1)}, f32[16,256]{1,0:T(8,128)S(1)}) custom-call(s32[2]{0:T(128)S(1)} %pad_add_fusion.place, f32[32]{0:T(128)S(1)} %copy-done.2, bf16[8192,128]{1,0:T(8,128)(2,1)S(1)} %prep.1.rows_all, bf16[272,512]{1,0:T(8,128)(2,1)S(1)} %maximum_maximum_fusion.chunk.own_chunk, ...), custom_call_target="tpu_custom_call" | custom-call | flops 2147483648 | bytes 1048576 | tf_op jit(solution)/shard_map/stats_0/pallas_call | solution.py:171
  13.2 7.8 %collective-permute-done.2.chunk = bf16[272,512]{1,0:T(8,128)(2,1)S(1)} collective-permute-done((bf16[272,512]{1,0:T(8,128)(2,1)S(1)}, bf16[272,512]{1,0:T(8,128)(2,1)S(1)}, u32[]{:S(2)}, u32[]{:S(2)}) %collective-permute-start.2) | collective-permute-done | bytes 278560 | tf_op jit(solution)/shard_map/ppermute | solution.py:222
  21.0 0.1 broadcast_select_fusion.1
  21.1 1.4 %collective-permute-start.5 = (bf16[272,512]{1,0:T(8,128)(2,1)S(1)}, bf16[272,512]{1,0:T(8,128)(2,1)S(1)}, u32[]{:S(2)}, u32[]{:S(2)}) collective-permute-start(bf16[272,512]{1,0:T(8,128)(2,1)S(1)} %get-tuple-element.119), channel_id=1, source_target_pairs={{0,2},{1,3},{2,4},{3,5},{4,6},{5,7},{6,0},{7,1},{8,10},{9,11},{10,... | collective-permute-start | bytes 835592 | tf_op jit(solution)/shard_map/ppermute | solution.py:222
  22.5 2.6 %collective-permute-start.4 = (bf16[272,512]{1,0:T(8,128)(2,1)S(1)}, bf16[272,512]{1,0:T(8,128)(2,1)S(1)}, u32[]{:S(2)}, u32[]{:S(2)}) collective-permute-start(bf16[272,512]{1,0:T(8,128)(2,1)S(1)} %get-tuple-element.118), channel_id=1, source_target_pairs={{0,4},{1,5},{2,6},{3,7},{4,0},{5,1},{6,2},{7,3},{8,12},{9,13},{10,... | collective-permute-start | bytes 835592 | tf_op jit(solution)/shard_map/ppermute | solution.py:222
  25.1 1.1 %collective-permute-start.3 = (bf16[272,512]{1,0:T(8,128)(2,1)S(1)}, bf16[272,512]{1,0:T(8,128)(2,1)S(1)}, u32[]{:S(2)}, u32[]{:S(2)}) collective-permute-start(bf16[272,512]{1,0:T(8,128)(2,1)S(1)} %get-tuple-element.120), channel_id=1, source_target_pairs={{0,6},{1,7},{2,0},{3,1},{4,2},{5,3},{6,4},{7,5},{8,14},{9,15},{10,... | collective-permute-start | bytes 835592 | tf_op jit(solution)/shard_map/ppermute | solution.py:222
  26.2 2.4 %stats_4.1 = (f32[16,256]{1,0:T(8,128)S(1)}, f32[16,256]{1,0:T(8,128)S(1)}, f32[16,256]{1,0:T(8,128)S(1)}) custom-call(s32[2]{0:T(128)S(1)} %pad_add_fusion.place, f32[32]{0:T(128)S(1)} %copy-done.2, bf16[8192,128]{1,0:T(8,128)(2,1)S(1)} %prep.1.rows_all, bf16[272,512]{1,0:T(8,128)(2,1)S(1)} %collective-permute-done.2.chunk, ...), custom_call_target="tpu_custom_call" | custom-call | flops 2147483648 | bytes 1048576 | tf_op jit(solution)/shard_map/stats_4/pallas_call | solution.py:171
  28.6 1.2 %collective-permute-done.5.chunk = bf16[272,512]{1,0:T(8,128)(2,1)S(1)} collective-permute-done((bf16[272,512]{1,0:T(8,128)(2,1)S(1)}, bf16[272,512]{1,0:T(8,128)(2,1)S(1)}, u32[]{:S(2)}, u32[]{:S(2)}) %collective-permute-start.5) | collective-permute-done | bytes 278560 | tf_op jit(solution)/shard_map/ppermute | solution.py:222
  29.8 2.4 %stats_1.1 = (f32[16,256]{1,0:T(8,128)S(1)}, f32[16,256]{1,0:T(8,128)S(1)}, f32[16,256]{1,0:T(8,128)S(1)}) custom-call(s32[2]{0:T(128)S(1)} %pad_add_fusion.place, f32[32]{0:T(128)S(1)} %copy-done.2, bf16[8192,128]{1,0:T(8,128)(2,1)S(1)} %prep.1.rows_all, bf16[272,512]{1,0:T(8,128)(2,1)S(1)} %collective-permute-done.5.chunk, ...), custom_call_target="tpu_custom_call" | custom-call | flops 2147483648 | bytes 1048576 | tf_op jit(solution)/shard_map/stats_1/pallas_call | solution.py:171
  32.2 4.7 %collective-permute-done.4.chunk = bf16[272,512]{1,0:T(8,128)(2,1)S(1)} collective-permute-done((bf16[272,512]{1,0:T(8,128)(2,1)S(1)}, bf16[272,512]{1,0:T(8,128)(2,1)S(1)}, u32[]{:S(2)}, u32[]{:S(2)}) %collective-permute-start.4) | collective-permute-done | bytes 278560 | tf_op jit(solution)/shard_map/ppermute | solution.py:222
  36.9 2.4 %stats_2.1 = (f32[16,256]{1,0:T(8,128)S(1)}, f32[16,256]{1,0:T(8,128)S(1)}, f32[16,256]{1,0:T(8,128)S(1)}) custom-call(s32[2]{0:T(128)S(1)} %pad_add_fusion.place, f32[32]{0:T(128)S(1)} %copy-done.2, bf16[8192,128]{1,0:T(8,128)(2,1)S(1)} %prep.1.rows_all, bf16[272,512]{1,0:T(8,128)(2,1)S(1)} %collective-permute-done.4.chunk, ...), custom_call_target="tpu_custom_call" | custom-call | flops 2147483648 | bytes 1048576 | tf_op jit(solution)/shard_map/stats_2/pallas_call | solution.py:171
  39.3 2.6 %stats_3.1 = (f32[16,256]{1,0:T(8,128)S(1)}, f32[16,256]{1,0:T(8,128)S(1)}, f32[16,256]{1,0:T(8,128)S(1)}, f32[1,16]{1,0:T(1,128)S(1)}) custom-call(s32[2]{0:T(128)S(1)} %pad_add_fusion.place, f32[32]{0:T(128)S(1)} %copy-done.2, bf16[8192,128]{1,0:T(8,128)(2,1)S(1)} %prep.1.rows_all, bf16[272,512]{1,0:T(8,128)(2,1)S(1)} %collective-permute-done.3.chunk, ...), custom_call_target="tpu_custom_call" | custom-call | flops 2147483648 | bytes 1048576 | tf_op jit(solution)/shard_map/stats_3/pallas_call | solution.py:171
  41.9 0.4 collective-permute-start.6
  42.4 3.5 %parts_4.1 = (bf16[256,512]{1,0:T(8,128)(2,1)S(1)}, f32[256,1024]{1,0:T(8,128)S(1)}) custom-call(s32[2]{0:T(128)S(1)} %pad_add_fusion.place, bf16[8192,128]{1,0:T(8,128)(2,1)S(1)} %prep.1.rows_all, bf16[272,512]{1,0:T(8,128)(2,1)S(1)} %collective-permute-done.2.chunk, bf16[272,512]{1,0:T(8,128)(2,1)S(1)} %maximum_maximum_fusion.chunk.own_chunk, ...), custom_call_target="tpu_custom_call" | custom-call | flops 3221225472 | bytes 1048576 | tf_op jit(solution)/shard_map/parts_4/pallas_call | solution.py:171
  45.9 0.1 collective-permute-start.7
  46.0 2.0 %collective-permute-start.10 = (bf16[256,512]{1,0:T(8,128)(2,1)S(1)}, bf16[256,512]{1,0:T(8,128)(2,1)S(1)}, u32[]{:S(2)}, u32[]{:S(2)}) collective-permute-start(bf16[256,512]{1,0:T(8,128)(2,1)S(1)} %get-tuple-element.94), channel_id=1, source_target_pairs={{0,248},{1,249},{2,250},{3,251},{4,252},{5,253},{6,254},{7,255},{8... | collective-permute-start | bytes 786440 | tf_op jit(solution)/shard_map/ppermute | solution.py:222
  47.9 1.3 %collective-permute-done.7 = f32[16]{0:T(128)S(1)} collective-permute-done((f32[16]{0:T(128)S(1)}, f32[16]{0:T(128)S(1)}, u32[]{:S(2)}, u32[]{:S(2)}) %collective-permute-start.7) | collective-permute-done | bytes 96 | tf_op jit(solution)/shard_map/ppermute | solution.py:228
  49.3 1.2 %collective-permute-start.8 = (f32[16]{0:T(128)S(1)}, f32[16]{0:T(128)S(1)}, u32[]{:S(2)}, u32[]{:S(2)}) collective-permute-start(f32[16]{0:T(128)S(1)} %add.60), channel_id=1, source_target_pairs={{0,32},{1,33},{2,34},{3,35},{4,36},{5,37},{6,38},{7,39},{8,40},{9,... | collective-permute-start | bytes 200 | tf_op jit(solution)/shard_map/ppermute | solution.py:228
  50.4 3.5 %parts_3.1 = (bf16[256,512]{1,0:T(8,128)(2,1)S(1)}, f32[256,1024]{1,0:T(8,128)S(1)}) custom-call(s32[2]{0:T(128)S(1)} %pad_add_fusion.place, bf16[8192,128]{1,0:T(8,128)(2,1)S(1)} %prep.1.rows_all, bf16[272,512]{1,0:T(8,128)(2,1)S(1)} %collective-permute-done.3.chunk, bf16[272,512]{1,0:T(8,128)(2,1)S(1)} %maximum_maximum_fusion.chunk.own_chunk, ...), custom_call_target="tpu_custom_call" | custom-call | flops 3221225472 | bytes 1048576 | tf_op jit(solution)/shard_map/parts_3/pallas_call | solution.py:171
  53.9 1.7 %collective-permute-done.8 = f32[16]{0:T(128)S(1)} collective-permute-done((f32[16]{0:T(128)S(1)}, f32[16]{0:T(128)S(1)}, u32[]{:S(2)}, u32[]{:S(2)}) %collective-permute-start.8) | collective-permute-done | bytes 96 | tf_op jit(solution)/shard_map/ppermute | solution.py:228
  55.6 1.2 %collective-permute-start.9 = (f32[16]{0:T(128)S(1)}, f32[16]{0:T(128)S(1)}, u32[]{:S(2)}, u32[]{:S(2)}) collective-permute-start(f32[16]{0:T(128)S(1)} %add.61), channel_id=1, source_target_pairs={{0,128},{1,129},{2,130},{3,131},{4,132},{5,133},{6,134},{7,135},{8... | collective-permute-start | bytes 200 | tf_op jit(solution)/shard_map/ppermute | solution.py:228
  56.8 1.9 %collective-permute-start.13 = (bf16[256,512]{1,0:T(8,128)(2,1)S(1)}, bf16[256,512]{1,0:T(8,128)(2,1)S(1)}, u32[]{:S(2)}, u32[]{:S(2)}) collective-permute-start(bf16[256,512]{1,0:T(8,128)(2,1)S(1)} %get-tuple-element.100), channel_id=1, source_target_pairs={{0,250},{1,251},{2,252},{3,253},{4,254},{5,255},{6,0},{7,1},{8,2},... | collective-permute-start | bytes 786440 | tf_op jit(solution)/shard_map/ppermute | solution.py:222
  58.6 0.8 collective-permute-done.9
  59.5 3.5 %parts_2.1 = (bf16[256,512]{1,0:T(8,128)(2,1)S(1)}, f32[256,1024]{1,0:T(8,128)S(1)}) custom-call(s32[2]{0:T(128)S(1)} %pad_add_fusion.place, bf16[8192,128]{1,0:T(8,128)(2,1)S(1)} %prep.1.rows_all, bf16[272,512]{1,0:T(8,128)(2,1)S(1)} %collective-permute-done.4.chunk, bf16[272,512]{1,0:T(8,128)(2,1)S(1)} %maximum_maximum_fusion.chunk.own_chunk, ...), custom_call_target="tpu_custom_call" | custom-call | flops 3221225472 | bytes 1048576 | tf_op jit(solution)/shard_map/parts_2/pallas_call | solution.py:171
  63.0 0.3 collective-permute-start.12
  63.3 4.2 %collective-permute-start.16 = (bf16[256,512]{1,0:T(8,128)(2,1)S(1)}, bf16[256,512]{1,0:T(8,128)(2,1)S(1)}, u32[]{:S(2)}, u32[]{:S(2)}) collective-permute-start(bf16[256,512]{1,0:T(8,128)(2,1)S(1)} %get-tuple-element.106), channel_id=1, source_target_pairs={{0,252},{1,253},{2,254},{3,255},{4,0},{5,1},{6,2},{7,3},{8,4},{9,5... | collective-permute-start | bytes 786440 | tf_op jit(solution)/shard_map/ppermute | solution.py:222
  67.5 0.1 collective-permute-start.14
  67.6 3.5 %parts_1.1 = (bf16[256,512]{1,0:T(8,128)(2,1)S(1)}, f32[256,1024]{1,0:T(8,128)S(1)}) custom-call(s32[2]{0:T(128)S(1)} %pad_add_fusion.place, bf16[8192,128]{1,0:T(8,128)(2,1)S(1)} %prep.1.rows_all, bf16[272,512]{1,0:T(8,128)(2,1)S(1)} %collective-permute-done.5.chunk, bf16[272,512]{1,0:T(8,128)(2,1)S(1)} %maximum_maximum_fusion.chunk.own_chunk, ...), custom_call_target="tpu_custom_call" | custom-call | flops 3221225472 | bytes 1048576 | tf_op jit(solution)/shard_map/parts_1/pallas_call | solution.py:171
  71.1 9.6 %collective-permute-start.15 = (f32[16]{0:T(128)S(1)}, f32[16]{0:T(128)S(1)}, u32[]{:S(2)}, u32[]{:S(2)}) collective-permute-start(f32[16]{0:T(128)S(1)} %add.65), channel_id=1, source_target_pairs={{0,1},{1,0},{2,3},{3,2},{4,5},{5,4},{6,7},{7,6},{8,9},{9,8},{10,11... | collective-permute-start | bytes 200 | tf_op jit(solution)/shard_map/ppermute | solution.py:228
  80.7 3.1 %collective-permute-start.17 = (bf16[256,512]{1,0:T(8,128)(2,1)S(1)}, bf16[256,512]{1,0:T(8,128)(2,1)S(1)}, u32[]{:S(2)}, u32[]{:S(2)}) collective-permute-start(bf16[256,512]{1,0:T(8,128)(2,1)S(1)} %get-tuple-element.112), channel_id=1, source_target_pairs={{0,254},{1,255},{2,0},{3,1},{4,2},{5,3},{6,4},{7,5},{8,6},{9,7},{1... | collective-permute-start | bytes 786440 | tf_op jit(solution)/shard_map/ppermute | solution.py:222
  83.8 3.6 %parts_0.1 = (f32[256,512]{1,0:T(8,128)S(1)}, bf16[128,1024]{1,0:T(8,128)(2,1)S(1)}, bf16[128,1024]{1,0:T(8,128)(2,1)S(1)}) custom-call(s32[2]{0:T(128)S(1)} %pad_add_fusion.place, bf16[8192,128]{1,0:T(8,128)(2,1)S(1)} %prep.1.rows_all, bf16[272,512]{1,0:T(8,128)(2,1)S(1)} %maximum_maximum_fusion.chunk.own_chunk, ...), custom_call_target="tpu_custom_call" | custom-call | flops 3221225472 | bytes 1048576 | tf_op jit(solution)/shard_map/parts_0/pallas_call | solution.py:171
  87.4 0.4 collective-permute-start.19
  87.8 0.6 broadcast_select_fusion.5
  88.4 1.0 %collective-permute-done.17 = bf16[256,512]{1,0:T(8,128)(2,1)S(1)} collective-permute-done((bf16[256,512]{1,0:T(8,128)(2,1)S(1)}, bf16[256,512]{1,0:T(8,128)(2,1)S(1)}, u32[]{:S(2)}, u32[]{:S(2)}) %collective-permute-start.17) | collective-permute-done | bytes 262176 | tf_op jit(solution)/shard_map/ppermute | solution.py:222
  89.4 0.2 add_convert_fusion
  89.6 1.0 %collective-permute-start.18 = (bf16[128,512]{1,0:T(8,128)(2,1)S(1)}, bf16[128,512]{1,0:T(8,128)(2,1)S(1)}, u32[]{:S(2)}, u32[]{:S(2)}) collective-permute-start(bf16[128,512]{1,0:T(8,128)(2,1)S(1)} %slice.68), channel_id=1, source_target_pairs={{0,1},{1,0},{2,3},{3,2},{4,5},{5,4},{6,7},{7,6},{8,9},{9,8},{10,11... | collective-permute-start | bytes 393224 | tf_op jit(solution)/shard_map/ppermute | solution.py:228
  90.6 0.9 maximum_select_fusion
  91.5 0.7 maximum_select_fusion.2
  92.2 0.7 maximum_select_fusion.1
  (39 shorter events, 0.4 us)
Async XLA Ops:
  3.1 6.7 %copy-start = (bf16[128,2048]{1,0:T(8,128)(2,1)S(1)}, bf16[128,2048]{1,0:T(8,128)(2,1)}, u32[]{:S(2)}) copy-start(bf16[128,2048]{1,0:T(8,128)(2,1)} %q_own) | copy-start | bytes 1572868
  3.1 6.7 %copy-start.1 = (bf16[128,2048]{1,0:T(8,128)(2,1)S(1)}, bf16[128,2048]{1,0:T(8,128)(2,1)}, u32[]{:S(2)}) copy-start(bf16[128,2048]{1,0:T(8,128)(2,1)} %g_own) | copy-start | bytes 1572868
  3.2 4.6 %collective-permute-start = (bf16[144,512]{1,0:T(8,128)(2,1)S(1)}, bf16[144,512]{1,0:T(8,128)(2,1)S(1)}, u32[]{:S(2)}, u32[]{:S(2)}) collective-permute-start(bf16[144,512]{1,0:T(8,128)(2,1)S(1)} %pad_maximum_fusion.1), channel_id=1, source_target_pairs={{0,1},{1,0},{2,3},{3,2},{4,5},{5,4},{6,7},{7,6},{8,9},{9,8},{10,11... | collective-permute-start | bytes 442376 | tf_op jit(solution)/shard_map/ppermute | solution.py:228
  7.8 2.0 %collective-permute-start.1 = (bf16[256,1024]{1,0:T(8,128)(2,1)S(1)}, bf16[256,1024]{1,0:T(8,128)(2,1)S(1)}, u32[]{:S(2)}, u32[]{:S(2)}) collective-permute-start(bf16[256,1024]{1,0:T(8,128)(2,1)S(1)} %pad_maximum_fusion), channel_id=1, source_target_pairs={{0,1},{1,0},{2,3},{3,2},{4,5},{5,4},{6,7},{7,6},{8,9},{9,8},{10,11... | collective-permute-start | bytes 1572872 | tf_op jit(solution)/shard_map/ppermute | solution.py:228
  8.2 2.7 %copy-start.2 = (f32[32]{0:T(128)S(1)}, f32[32]{0:T(128)}, u32[]{:S(2)}) copy-start(f32[32]{0:T(128)} %sinks.9) | copy-start | bytes 388
  8.2 12.8 %collective-permute-start.2 = (bf16[272,512]{1,0:T(8,128)(2,1)S(1)}, bf16[272,512]{1,0:T(8,128)(2,1)S(1)}, u32[]{:S(2)}, u32[]{:S(2)}) collective-permute-start(bf16[272,512]{1,0:T(8,128)(2,1)S(1)} %maximum_maximum_fusion.chunk.own_chunk), channel_id=1, source_target_pairs={{0,8},{1,9},{2,10},{3,11},{4,12},{5,13},{6,14},{7,15},{8,16},{9,17... | collective-permute-start | bytes 835592 | tf_op jit(solution)/shard_map/ppermute | solution.py:222
  21.1 8.7 %collective-permute-start.5 = (bf16[272,512]{1,0:T(8,128)(2,1)S(1)}, bf16[272,512]{1,0:T(8,128)(2,1)S(1)}, u32[]{:S(2)}, u32[]{:S(2)}) collective-permute-start(bf16[272,512]{1,0:T(8,128)(2,1)S(1)} %get-tuple-element.119), channel_id=1, source_target_pairs={{0,2},{1,3},{2,4},{3,5},{4,6},{5,7},{6,0},{7,1},{8,10},{9,11},{10,... | collective-permute-start | bytes 835592 | tf_op jit(solution)/shard_map/ppermute | solution.py:222
  22.5 14.4 %collective-permute-start.4 = (bf16[272,512]{1,0:T(8,128)(2,1)S(1)}, bf16[272,512]{1,0:T(8,128)(2,1)S(1)}, u32[]{:S(2)}, u32[]{:S(2)}) collective-permute-start(bf16[272,512]{1,0:T(8,128)(2,1)S(1)} %get-tuple-element.118), channel_id=1, source_target_pairs={{0,4},{1,5},{2,6},{3,7},{4,0},{5,1},{6,2},{7,3},{8,12},{9,13},{10,... | collective-permute-start | bytes 835592 | tf_op jit(solution)/shard_map/ppermute | solution.py:222
  25.1 14.2 %collective-permute-start.3 = (bf16[272,512]{1,0:T(8,128)(2,1)S(1)}, bf16[272,512]{1,0:T(8,128)(2,1)S(1)}, u32[]{:S(2)}, u32[]{:S(2)}) collective-permute-start(bf16[272,512]{1,0:T(8,128)(2,1)S(1)} %get-tuple-element.120), channel_id=1, source_target_pairs={{0,6},{1,7},{2,0},{3,1},{4,2},{5,3},{6,4},{7,5},{8,14},{9,15},{10,... | collective-permute-start | bytes 835592 | tf_op jit(solution)/shard_map/ppermute | solution.py:222
  41.9 3.9 %collective-permute-start.6 = (f32[16]{0:T(128)S(1)}, f32[16]{0:T(128)S(1)}, u32[]{:S(2)}, u32[]{:S(2)}) collective-permute-start(f32[16]{0:T(128)S(1)} %bitcast.6), channel_id=1, source_target_pairs={{0,4},{1,5},{2,6},{3,7},{4,0},{5,1},{6,2},{7,3},{8,12},{9,13},{10,... | collective-permute-start | bytes 200 | tf_op jit(solution)/shard_map/ppermute | solution.py:228
  45.9 3.4 %collective-permute-start.7 = (f32[16]{0:T(128)S(1)}, f32[16]{0:T(128)S(1)}, u32[]{:S(2)}, u32[]{:S(2)}) collective-permute-start(f32[16]{0:T(128)S(1)} %bitcast_add_fusion), channel_id=1, source_target_pairs={{0,16},{1,17},{2,18},{3,19},{4,20},{5,21},{6,22},{7,23},{8,24},{9,... | collective-permute-start | bytes 200 | tf_op jit(solution)/shard_map/ppermute | solution.py:228
  46.0 13.5 %collective-permute-start.10 = (bf16[256,512]{1,0:T(8,128)(2,1)S(1)}, bf16[256,512]{1,0:T(8,128)(2,1)S(1)}, u32[]{:S(2)}, u32[]{:S(2)}) collective-permute-start(bf16[256,512]{1,0:T(8,128)(2,1)S(1)} %get-tuple-element.94), channel_id=1, source_target_pairs={{0,248},{1,249},{2,250},{3,251},{4,252},{5,253},{6,254},{7,255},{8... | collective-permute-start | bytes 786440 | tf_op jit(solution)/shard_map/ppermute | solution.py:222
  49.3 6.3 %collective-permute-start.8 = (f32[16]{0:T(128)S(1)}, f32[16]{0:T(128)S(1)}, u32[]{:S(2)}, u32[]{:S(2)}) collective-permute-start(f32[16]{0:T(128)S(1)} %add.60), channel_id=1, source_target_pairs={{0,32},{1,33},{2,34},{3,35},{4,36},{5,37},{6,38},{7,39},{8,40},{9,... | collective-permute-start | bytes 200 | tf_op jit(solution)/shard_map/ppermute | solution.py:228
  55.6 3.9 %collective-permute-start.9 = (f32[16]{0:T(128)S(1)}, f32[16]{0:T(128)S(1)}, u32[]{:S(2)}, u32[]{:S(2)}) collective-permute-start(f32[16]{0:T(128)S(1)} %add.61), channel_id=1, source_target_pairs={{0,128},{1,129},{2,130},{3,131},{4,132},{5,133},{6,134},{7,135},{8... | collective-permute-start | bytes 200 | tf_op jit(solution)/shard_map/ppermute | solution.py:228
  56.8 10.7 %collective-permute-start.13 = (bf16[256,512]{1,0:T(8,128)(2,1)S(1)}, bf16[256,512]{1,0:T(8,128)(2,1)S(1)}, u32[]{:S(2)}, u32[]{:S(2)}) collective-permute-start(bf16[256,512]{1,0:T(8,128)(2,1)S(1)} %get-tuple-element.100), channel_id=1, source_target_pairs={{0,250},{1,251},{2,252},{3,253},{4,254},{5,255},{6,0},{7,1},{8,2},... | collective-permute-start | bytes 786440 | tf_op jit(solution)/shard_map/ppermute | solution.py:222
  59.5 3.5 %collective-permute-start.11 = (f32[16]{0:T(128)S(1)}, f32[16]{0:T(128)S(1)}, u32[]{:S(2)}, u32[]{:S(2)}) collective-permute-start(f32[16]{0:T(128)S(1)} %add.62), channel_id=1, source_target_pairs={{0,8},{1,9},{2,10},{3,11},{4,12},{5,13},{6,14},{7,15},{8,0},{9,1},... | collective-permute-start | bytes 200 | tf_op jit(solution)/shard_map/ppermute | solution.py:228
  63.0 4.5 %collective-permute-start.12 = (f32[16]{0:T(128)S(1)}, f32[16]{0:T(128)S(1)}, u32[]{:S(2)}, u32[]{:S(2)}) collective-permute-start(f32[16]{0:T(128)S(1)} %add.63), channel_id=1, source_target_pairs={{0,64},{1,65},{2,66},{3,67},{4,68},{5,69},{6,70},{7,71},{8,72},{9,... | collective-permute-start | bytes 200 | tf_op jit(solution)/shard_map/ppermute | solution.py:228
  63.3 20.5 %collective-permute-start.16 = (bf16[256,512]{1,0:T(8,128)(2,1)S(1)}, bf16[256,512]{1,0:T(8,128)(2,1)S(1)}, u32[]{:S(2)}, u32[]{:S(2)}) collective-permute-start(bf16[256,512]{1,0:T(8,128)(2,1)S(1)} %get-tuple-element.106), channel_id=1, source_target_pairs={{0,252},{1,253},{2,254},{3,255},{4,0},{5,1},{6,2},{7,3},{8,4},{9,5... | collective-permute-start | bytes 786440 | tf_op jit(solution)/shard_map/ppermute | solution.py:222
  67.5 3.6 %collective-permute-start.14 = (f32[16]{0:T(128)S(1)}, f32[16]{0:T(128)S(1)}, u32[]{:S(2)}, u32[]{:S(2)}) collective-permute-start(f32[16]{0:T(128)S(1)} %add.64), channel_id=1, source_target_pairs={{0,2},{1,3},{2,0},{3,1},{4,6},{5,7},{6,4},{7,5},{8,10},{9,11},{10,... | collective-permute-start | bytes 200 | tf_op jit(solution)/shard_map/ppermute | solution.py:228
  71.1 12.7 %collective-permute-start.15 = (f32[16]{0:T(128)S(1)}, f32[16]{0:T(128)S(1)}, u32[]{:S(2)}, u32[]{:S(2)}) collective-permute-start(f32[16]{0:T(128)S(1)} %add.65), channel_id=1, source_target_pairs={{0,1},{1,0},{2,3},{3,2},{4,5},{5,4},{6,7},{7,6},{8,9},{9,8},{10,11... | collective-permute-start | bytes 200 | tf_op jit(solution)/shard_map/ppermute | solution.py:228
  80.7 8.7 %collective-permute-start.17 = (bf16[256,512]{1,0:T(8,128)(2,1)S(1)}, bf16[256,512]{1,0:T(8,128)(2,1)S(1)}, u32[]{:S(2)}, u32[]{:S(2)}) collective-permute-start(bf16[256,512]{1,0:T(8,128)(2,1)S(1)} %get-tuple-element.112), channel_id=1, source_target_pairs={{0,254},{1,255},{2,0},{3,1},{4,2},{5,3},{6,4},{7,5},{8,6},{9,7},{1... | collective-permute-start | bytes 786440 | tf_op jit(solution)/shard_map/ppermute | solution.py:222
  87.4 3.2 %collective-permute-start.19 = (bf16[128,1024]{1,0:T(8,128)(2,1)S(1)}, bf16[128,1024]{1,0:T(8,128)(2,1)S(1)}, u32[]{:S(2)}, u32[]{:S(2)}) collective-permute-start(bf16[128,1024]{1,0:T(8,128)(2,1)S(1)} %get-tuple-element.114), channel_id=1, source_target_pairs={{0,1},{1,0},{2,3},{3,2},{4,5},{5,4},{6,7},{7,6},{8,9},{9,8},{10,11... | collective-permute-start | bytes 786440 | tf_op jit(solution)/shard_map/ppermute | solution.py:228
  89.6 1.9 %collective-permute-start.18 = (bf16[128,512]{1,0:T(8,128)(2,1)S(1)}, bf16[128,512]{1,0:T(8,128)(2,1)S(1)}, u32[]{:S(2)}, u32[]{:S(2)}) collective-permute-start(bf16[128,512]{1,0:T(8,128)(2,1)S(1)} %slice.68), channel_id=1, source_target_pairs={{0,1},{1,0},{2,3},{3,2},{4,5},{5,4},{6,7},{7,6},{8,9},{9,8},{10,11... | collective-permute-start | bytes 393224 | tf_op jit(solution)/shard_map/ppermute | solution.py:228

commit v4 on v3

--- a/solution.py
+++ b/solution.py
@@ -6,6 +6,7 @@
 from jax import lax
 from jax.experimental import pallas as pl
 from jax.experimental.pallas import tpu as pltpu
+from jax.sharding import Mesh
 from jax.sharding import PartitionSpec as P
 
 KV_HEADS = 8
@@ -15,6 +16,8 @@
 CHIP = 2 * TOK
 HOPS = WINDOW // CHIP
 ROW = 4
+SINK_ROWS = 256
+AXES = ("far", "y", "core")
 SPAN = WINDOW + CHIP
 HALF_KV = KV_HEADS // 2 * HEAD_DIM
 SCALE = 1.0 / math.sqrt(HEAD_DIM)
@@ -84,69 +87,77 @@
     bias, sink_rows = after[-2:]
     core = place[0]
     bias[...] = mask_bias(place, chunk, own_chunk, hop)
-    for head in range(16):
-        tile, at = head // 8, slice(head, head + 1)
-        sink = sinks[core * 16 + head] * (1.0 / SCALE)
-        s = dot(chunk[0:CHIP, lane_tile(tile)], query_all[head_rows(head), :], NT) + bias[...]
-        dp = dot(chunk[0:CHIP, lane_tile(tile, HALF_KV)], grad_all[head_rows(head), :], NT)
-        old = jnp.full((1, CHIP), sink, F32) if hop == 0 else before[0][at, :]
-        top = jnp.maximum(old, jnp.max(s, 0, keepdims=True))
-        ex = jnp.exp2((s - top) * EXP2_SCALE)
-        fade = jnp.exp2((old - top) * EXP2_SCALE)
-        denom = jnp.sum(ex, 0, keepdims=True)
-        weighed = jnp.sum(ex * dp, 0, keepdims=True)
-        if hop == 0:
-            denom = denom + fade
-        else:
-            denom = denom + before[1][at, :] * fade
-            weighed = weighed + before[2][at, :] * fade
-        top_out[at, :] = top
-        if last:
-            share = 1.0 / denom
-            delta = weighed * share
-            second[at, :] = share
-            third[at, :] = delta
-            sink_rows[at, :] = -jnp.exp2((sink - top) * EXP2_SCALE) * share * delta
-        else:
-            second[at, :] = denom
-            third[at, :] = weighed
+    def of_tile(tile, carry):
+        lanes = pl.ds(pl.multiple_of(tile * 128, 128), 128)
+        value_lanes = pl.ds(pl.multiple_of(HALF_KV + tile * 128, 128), 128)
+        for n in range(8):
+            head = tile * 8 + n
+            at, rows = pl.ds(head, 1), pl.ds(pl.multiple_of(head * CHIP, CHIP), CHIP)
+            sink = sinks[core * 16 + head] * (1.0 / SCALE)
+            s = dot(chunk[0:CHIP, lanes], query_all[rows, :], NT) + bias[...]
+            dp = dot(chunk[0:CHIP, value_lanes], grad_all[rows, :], NT)
+            old = jnp.full((1, CHIP), sink, F32) if hop == 0 else before[0][at, :]
+            top = jnp.maximum(old, jnp.max(s, 0, keepdims=True))
+            ex = jnp.exp2((s - top) * EXP2_SCALE)
+            fade = jnp.exp2((old - top) * EXP2_SCALE)
+            denom = jnp.sum(ex, 0, keepdims=True)
+            weighed = jnp.sum(ex * dp, 0, keepdims=True)
+            if hop == 0:
+                denom = denom + fade
+            else:
+                denom = denom + before[1][at, :] * fade
+                weighed = weighed + before[2][at, :] * fade
+            top_out[at, :] = top
+            if last:
+                share = 1.0 / denom
+                delta = weighed * share
+                second[at, :] = share
+                third[at, :] = delta
+                sink_rows[at, :] = -jnp.exp2((sink - top) * EXP2_SCALE) * share * delta
+            else:
+                second[at, :] = denom
+                third[at, :] = weighed
+        return carry
+
+    lax.fori_loop(0, 2, of_tile, 0)
     if last:
         sums = jnp.sum(sink_rows[...], 1, keepdims=True)
-        after[3][...] = jnp.transpose(jnp.broadcast_to(sums, (16, 128)))[0:1, :]
+        for row in range(0, SINK_ROWS, 16):
+            after[3][row : row + 16, :] = jnp.broadcast_to(sums, (16, 128))
 
 
 def parts_kernel(
     hop, place, rows_all, chunk, own_chunk, tops, shares, deltas, *refs
 ):
     query_all, grad_all = split_rows(rows_all)
-    weight, dscore, bias = refs[-3:]
+    weight, dscore, bias, keys_t = refs[-4:]
     dq_in = None if hop == HOPS else refs[0]
-    outs = refs[:-3] if hop == HOPS else refs[1:-3]
+    outs = refs[:-4] if hop == HOPS else refs[1:-4]
     kv_out = outs[0]
     bias[...] = mask_bias(place, chunk, own_chunk, hop)
-    keys_t = jnp.transpose(chunk[0:CHIP, 0:CHIP].astype(F32)).astype(BF16)
-    for tile in range(2):
+    keys_t[...] = jnp.transpose(chunk[0:CHIP, 0:CHIP].astype(F32)).astype(BF16)
+
+    def part(start, size, unit):
+        return pl.ds(pl.multiple_of(start * unit, unit), size * unit)
+
+    def of_tile(tile, carry):
+        lanes, value_lanes = part(tile, 1, 128), part(tile + HALF_KV // 128, 1, 128)
         for n in range(8):
-            head, span = 8 * tile + n, head_rows(n)
-            at = slice(head, head + 1)
-            s = dot(chunk[0:CHIP, lane_tile(tile)], query_all[head_rows(head), :], NT)
-            dp = dot(
-                chunk[0:CHIP, lane_tile(tile, HALF_KV)], grad_all[head_rows(head), :], NT
-            )
+            span, rows = head_rows(n), part(8 * tile + n, 1, CHIP)
+            at = pl.ds(8 * tile + n, 1)
+            s = dot(chunk[0:CHIP, lanes], query_all[rows, :], NT)
+            dp = dot(chunk[0:CHIP, value_lanes], grad_all[rows, :], NT)
             prob = jnp.exp2((s + bias[...] - tops[at, :]) * EXP2_SCALE) * shares[at, :]
-            weight[tile, :, span] = prob.astype(BF16)
-            dscore[tile, :, span] = (prob * (dp - deltas[at, :])).astype(BF16)
-        rows = slice(8 * tile * CHIP, 8 * (tile + 1) * CHIP)
-        value_part = dot(weight[tile], grad_all[rows, :], NN)
-        key_part = dot(dscore[tile], query_all[rows, :], NN) * SCALE
-        kv_out[:, lane_tile(tile)] = key_part.astype(kv_out.dtype)
-        kv_out[:, lane_tile(tile, HALF_KV)] = value_part.astype(kv_out.dtype)
+            weight[:, span] = prob.astype(BF16)
+            dscore[:, span] = (prob * (dp - deltas[at, :])).astype(BF16)
+        rows = part(tile, 1, 8 * CHIP)
+        value_part = dot(weight[...], grad_all[rows, :], NN)
+        key_part = dot(dscore[...], query_all[rows, :], NN) * SCALE
+        kv_out[:, lanes] = key_part.astype(kv_out.dtype)
+        kv_out[:, value_lanes] = value_part.astype(kv_out.dtype)
         for group in range(2):
-            g = 2 * tile + group
-            rows = slice(g * HEAD_DIM, (g + 1) * HEAD_DIM)
-            dq_t = dot(
-                keys_t[rows, :], dscore[tile, :, group * 1024 : (group + 1) * 1024], NN
-            )
+            rows = part(2 * tile + group, 1, HEAD_DIM)
+            dq_t = dot(keys_t[rows, :], dscore[:, group * 1024 : (group + 1) * 1024], NN)
             if dq_in is not None:
                 dq_t = dq_t + dq_in[rows, :]
             if hop > 0:
@@ -157,8 +168,36 @@
                     [dq_t[:, head_rows(2 * pair)], dq_t[:, head_rows(2 * pair + 1)]], 0
                 )
                 dq = (jnp.transpose(two) * SCALE).astype(BF16)
-                outs[1][:, lane_tile(2 * g + pair)] = dq[:TOK]
-                outs[2][:, lane_tile(2 * g + pair)] = dq[TOK:]
+                at = part(4 * tile + 2 * group + pair, 1, 128)
+                outs[1][:, at] = dq[:TOK]
+                outs[2][:, at] = dq[TOK:]
+        return carry
+
+    if hop in (1, 2):
+        lax.fori_loop(0, 2, of_tile, 0)
+    else:
+        of_tile(1, of_tile(0, 0))
+
+
+def fold_kernel(gathered, out):
+    total = gathered[0:2]
+    for n in range(1, ROW):
+        total = total + gathered[2 * n : 2 * n + 2]
+    out[...] = jnp.concatenate(
+        [jnp.transpose(total[0])[0:1, :], jnp.transpose(total[1])[0:1, :]], 1
+    )
+
+
+def folded(gathered, interpret):
+    return pl.pallas_call(
+        fold_kernel,
+        name="fold",
+        grid=(1,),
+        in_specs=[pl.BlockSpec((2 * ROW, 16, 128), lambda i: (0, 0, 0))],
+        out_specs=pl.BlockSpec((1, 32), lambda i: (0, 0)),
+        out_shape=jax.ShapeDtypeStruct((1, 32), F32),
+        interpret=interpret,
+    )(gathered).reshape(32)
 
 
 SMEM = pl.BlockSpec(memory_space=pltpu.SMEM)
@@ -193,7 +232,7 @@
     return run(
         functools.partial(stats_kernel, hop, last), f"stats_{hop}", 2,
         (place, sinks, *tokens, chunk, own_chunk, *before),
-        [STAT] * 3 + [jax.ShapeDtypeStruct((1, 16), F32)] * last,
+        [STAT] * 3 + [jax.ShapeDtypeStruct((SINK_ROWS, 128), F32)] * last,
         [pltpu.VMEM((CHIP, CHIP), F32), pltpu.VMEM((16, CHIP), F32)], 2 << 30, interpret,
     )
 
@@ -208,24 +247,25 @@
         functools.partial(parts_kernel, hop), f"parts_{hop}", 1,
         (place, *tokens, chunk, own_chunk, *stats, *dq),
         [kv] + dq_shapes,
-        [pltpu.VMEM((2, CHIP, 8 * CHIP), BF16)] * 2 + [pltpu.VMEM((CHIP, CHIP), F32)],
+        [pltpu.VMEM((CHIP, 8 * CHIP), BF16)] * 2
+        + [pltpu.VMEM((CHIP, CHIP), F32), pltpu.VMEM((CHIP, CHIP), BF16)],
         3 << 30, interpret,
     )
 
 
 def per_device(count, interpret, queries, key_heads, value_heads, out_grad, segment, sink_logits):
-    index = lax.axis_index("ctx")
+    index = lax.axis_index(AXES)
     core, chip = index % 2, index // 2
     first = core == 0
 
     def sent(block, route):
-        return lax.ppermute(block, "ctx", route)
+        return lax.ppermute(block, AXES, route)
 
     def shifted(block, chips):
         return sent(block, [(i, (i + 2 * chips) % count) for i in range(count)])
 
     def crossed(block, bit):
-        return lax.ppermute(block, "ctx", [(i, i ^ bit) for i in range(count)])
+        return lax.ppermute(block, AXES, [(i, i ^ bit) for i in range(count)])
 
     def in_row(i, hop):
         return i // 8 * 8 + (i // 2 + hop) % ROW * 2 + i % 2
@@ -266,28 +306,14 @@
         stats = stats_of(
             hop, hop == 3, place, sink_logits, tokens, chunks[hop], chunk, stats, interpret
         )
-    *stats, sink_row = stats
-    sink_grad = sink_row.reshape(16)
-    bits = [bit for bit in (4, 16, 32, 128, 8, 64, 2) if bit < count]
-
-    def widened(value):
-        return value + crossed(value, bits.pop(0)) if bits else value
-
+    *stats, sink_block = stats
+    gathered = lax.all_gather(sink_block, AXES[1:])
     dq, came_back = (), {}
     for hop in range(HOPS, 0, -1):
         part, *dq = parts_of(hop, place, tokens, chunks[hop], chunk, stats, dq, interpret)
-        part, sink_grad = lax.optimization_barrier((part, widened(sink_grad)))
         came_back[hop] = shifted(part, -hop)
-        if hop > 1:
-            sink_grad = widened(sink_grad)
-        else:
-            sink_half, sink_grad = sink_grad, crossed(sink_grad, 1)
-        if hop < HOPS:
-            dq[0], sink_grad, came_back[hop + 1] = lax.optimization_barrier(
-                (dq[0], sink_grad, came_back[hop + 1])
-            )
-        else:
-            dq[0], sink_grad = lax.optimization_barrier((dq[0], sink_grad))
+        if hop + 2 in came_back:
+            dq[0], came_back[hop + 2] = lax.optimization_barrier((dq[0], came_back[hop + 2]))
     total, dq_own, dq_peer = parts_of(0, place, tokens, chunk, chunk, stats, dq, interpret)
 
     def joined(mine, theirs):
@@ -295,27 +321,40 @@
             first, jnp.concatenate([mine, theirs], 1), jnp.concatenate([theirs, mine], 1)
         )
 
-    sink_grad = jnp.where(
-        first,
-        jnp.concatenate([sink_half, sink_grad]),
-        jnp.concatenate([sink_grad, sink_half]),
-    )
-    query_grad = joined(dq_own, crossed(dq_peer, 1))
+    gathered, dq_peer = lax.optimization_barrier((gathered, dq_peer))
+
+    def four_sums(value, low, high):
+        near = value + crossed(value, low)
+        return near + (crossed(value, high) + crossed(value, low | high))
+
+    sink_grad = folded(gathered, interpret)
+    if count > 16:
+        sink_grad = four_sums(sink_grad, 8, 16)
+    dq_came = crossed(dq_peer, 1)
     for part in came_back.values():
         total = total + part.astype(F32)
     total = total.astype(BF16)
-    came, query_grad = lax.optimization_barrier((crossed(total[TOK:], 1), query_grad))
+    came, dq_came, sink_grad = lax.optimization_barrier(
+        (crossed(total[TOK:], 1), dq_came, sink_grad)
+    )
+    if count > 16:
+        sink_grad = four_sums(sink_grad, 64, 128)
+        sink_grad = sink_grad + crossed(sink_grad, 32)
+    else:
+        sink_grad = sink_grad + crossed(sink_grad, 8)
+    query_grad = joined(dq_own, dq_came)
     key_grad = joined(total[:TOK, :HALF_KV], came[:, :HALF_KV])
     value_grad = joined(total[:TOK, HALF_KV:], came[:, HALF_KV:])
     return query_grad, key_grad, value_grad, sink_grad
 
 
 def solution(mesh, interpret=False):
-    rows = P("ctx", None)
+    finer = Mesh(mesh.devices.reshape(-1, ROW, 2), AXES)
+    rows = P(AXES, None)
     return jax.shard_map(
         functools.partial(per_device, mesh.size, interpret),
-        mesh=mesh,
-        in_specs=(rows, rows, rows, rows, P("ctx"), P()),
+        mesh=finer,
+        in_specs=(rows, rows, rows, rows, P(AXES), P()),
         out_specs=(rows, rows, rows, P()),
         check_vma=False,
     )

time: 93.1 us -> 117 us (1.26); the launches traced: 92.9 us -> 115 us
  between operations: 0.93 us -> 14.3 us
  waiting for transfers between devices: 20.1 us -> 27.5 us
  starting transfers between devices: 34 us -> 30.2 us
  Pallas kernels: 30.7 us -> 33.5 us
  local copies, waits for them, and re-layouts: 1.84 us -> 3.43 us
    ppermute x20 -> x19, waiting for transfers between devices: 20.1 us -> 27.5 us  [the longest x8 18.4 us: sent(): return lax.ppermute(block, AXES, route)]
    ppermute x20 -> x19, starting transfers between devices: 34 us -> 30.2 us  [the longest x11 17.3 us: crossed(): return lax.ppermute(block, AXES, [(i, i ^ bit) for i in range(count)])]
    unnamed x6 -> x10, local copies, waits for them, and re-layouts: 0.02 us -> 1.6 us
    pallas_call x0 -> x1, Pallas kernels: none -> 1.51 us  [folded(): pl.pallas_call(fold_kernel, name='fold', grid=(1,), in_specs=[pl.BlockSpe...]
    pallas_call x11, Pallas kernels: 30.7 us -> 32 us  [run(): pl.pallas_call(kernel, name=name, in_specs=[SMEM] * n_scalars + [VMEM] *...]
  transfers between devices with their start and end apart: 20 -> 20, of which waited for: 8 -> 10; matrix products, arithmetic and copies ran while one was open for 3% -> 4% of each run, Pallas kernels for 30% -> 26%
where the time goes in v4:
time: 117 us; the launch traced here: 115 us
  Pallas kernels  33.5 us (29%)
  starting transfers between devices  30.2 us (26%)
  waiting for transfers between devices  27.5 us (24%)
  between operations  14.3 us (12%)
  other arithmetic  5.9 us (5%)
  local copies, waits for them, and re-layouts  3.43 us (3%)
    pallas_call x11, Pallas kernels, run(): pl.pallas_call(kernel, name=name, in_specs=[SMEM] * n_scalars + [VMEM] *...  32 us
    ppermute x8, waiting for transfers between devices, sent(): return lax.ppermute(block, AXES, route)  18.4 us
    ppermute x11, starting transfers between devices, crossed(): return lax.ppermute(block, AXES, [(i, i ^ bit) for i in range(count)])  17.3 us
    ppermute x8, starting transfers between devices, sent(): return lax.ppermute(block, AXES, route)  12.9 us
    ppermute x11, waiting for transfers between devices, crossed(): return lax.ppermute(block, AXES, [(i, i ^ bit) for i in range(count)])  9.09 us
  transfers between devices with their start and end apart: 20, of which 10 were waited for; matrix products, arithmetic and copies ran while one was open for 4% of the time, Pallas kernels for 26%

profile of v4, /device:TPU:1, one launch (start us, length us, event | category | flops | bytes accessed | tf_op | source)
XLA Modules:
  0.0 115.0 jit_solution(17053632442666366422)
XLA Ops:
  7.2 0.9 fusion.2
  8.1 0.9 fusion.3
  9.0 0.7 convert_bitcast_fusion
  9.8 3.3 %collective-permute-start = (bf16[144,512]{1,0:T(8,128)(2,1)S(1)}, bf16[144,512]{1,0:T(8,128)(2,1)S(1)}, u32[]{:S(2)}, u32[]{:S(2)}) collective-permute-start(bf16[144,512]{1,0:T(8,128)(2,1)S(1)} %pad_maximum_fusion.1), channel_id=1, source_target_pairs={{0,1},{1,0},{2,3},{3,2},{4,5},{5,4},{6,7},{7,6},{8,9},{9,8},{10,11... | collective-permute-start | bytes 442376 | tf_op jit(solution)/shard_map/ppermute | solution.py:268
  13.1 1.2 %slice_select_fusion = (bf16[128,1024]{1,0:T(8,128)(2,1)S(1)}, bf16[128,1024]{1,0:T(8,128)(2,1)S(1)}) fusion(bf16[128,2048]{1,0:T(8,128)(2,1)} %g_own, pred[]{:T(512)S(6)} %eq.8, bf16[128,2048]{1,0:T(8,128)(2,1)} %q_own), kind=kLoop, calls=%fused_computation.7 | loop fusion | flops 262144 | bytes 1572865 | tf_op jit(solution)/shard_map/jit(_where)/select_n | solution.py:288
  14.4 0.2 collective-permute-start.1
  14.8 1.5 %collective-permute-done.1.both_peer = bf16[256,1024]{1,0:T(8,128)(2,1)S(1)} collective-permute-done((bf16[256,1024]{1,0:T(8,128)(2,1)S(1)}, bf16[256,1024]{1,0:T(8,128)(2,1)S(1)}, u32[]{:S(2)}, u32[]{:S(2)}) %collective-permute-start.1) | collective-permute-done | bytes 524320 | tf_op jit(solution)/shard_map/ppermute | solution.py:268
  16.4 1.0 prep.1.rows_all
  17.4 2.5 %stats_0.1 = (f32[16,256]{1,0:T(8,128)S(1)}, f32[16,256]{1,0:T(8,128)S(1)}, f32[16,256]{1,0:T(8,128)S(1)}) custom-call(s32[2]{0:T(128)S(1)} %pad_add_fusion.place, f32[32]{0:T(128)S(1)} %copy-done.2, bf16[8192,128]{1,0:T(8,128)(2,1)S(1)} %prep.1.rows_all, bf16[272,512]{1,0:T(8,128)(2,1)S(1)} %maximum_maximum_fusion.chunk.own_chunk, ...), custom_call_target="tpu_custom_call" | custom-call | flops 2147483648 | bytes 1048576 | tf_op jit(solution)/shard_map/stats_0/pallas_call | solution.py:210
  20.0 7.6 %collective-permute-done.2.chunk = bf16[272,512]{1,0:T(8,128)(2,1)S(1)} collective-permute-done((bf16[272,512]{1,0:T(8,128)(2,1)S(1)}, bf16[272,512]{1,0:T(8,128)(2,1)S(1)}, u32[]{:S(2)}, u32[]{:S(2)}) %collective-permute-start.2) | collective-permute-done | bytes 278560 | tf_op jit(solution)/shard_map/ppermute | solution.py:262
  27.7 1.4 %collective-permute-start.5 = (bf16[272,512]{1,0:T(8,128)(2,1)S(1)}, bf16[272,512]{1,0:T(8,128)(2,1)S(1)}, u32[]{:S(2)}, u32[]{:S(2)}) collective-permute-start(bf16[272,512]{1,0:T(8,128)(2,1)S(1)} %get-tuple-element.95), channel_id=1, source_target_pairs={{0,2},{1,3},{2,4},{3,5},{4,6},{5,7},{6,0},{7,1},{8,10},{9,11},{10,... | collective-permute-start | bytes 835592 | tf_op jit(solution)/shard_map/ppermute | solution.py:262
  29.1 2.6 %collective-permute-start.4 = (bf16[272,512]{1,0:T(8,128)(2,1)S(1)}, bf16[272,512]{1,0:T(8,128)(2,1)S(1)}, u32[]{:S(2)}, u32[]{:S(2)}) collective-permute-start(bf16[272,512]{1,0:T(8,128)(2,1)S(1)} %get-tuple-element.94), channel_id=1, source_target_pairs={{0,4},{1,5},{2,6},{3,7},{4,0},{5,1},{6,2},{7,3},{8,12},{9,13},{10,... | collective-permute-start | bytes 835592 | tf_op jit(solution)/shard_map/ppermute | solution.py:262
  31.7 1.1 collective-permute-start.3
  32.8 2.6 %stats_4.1 = (f32[16,256]{1,0:T(8,128)S(1)}, f32[16,256]{1,0:T(8,128)S(1)}, f32[16,256]{1,0:T(8,128)S(1)}) custom-call(s32[2]{0:T(128)S(1)} %pad_add_fusion.place, f32[32]{0:T(128)S(1)} %copy-done.2, bf16[8192,128]{1,0:T(8,128)(2,1)S(1)} %prep.1.rows_all, bf16[272,512]{1,0:T(8,128)(2,1)S(1)} %collective-permute-done.2.chunk, ...), custom_call_target="tpu_custom_call" | custom-call | flops 2147483648 | bytes 1048576 | tf_op jit(solution)/shard_map/stats_4/pallas_call | solution.py:210
  35.4 1.0 collective-permute-done.5.chunk
  36.4 2.6 %stats_1.1 = (f32[16,256]{1,0:T(8,128)S(1)}, f32[16,256]{1,0:T(8,128)S(1)}, f32[16,256]{1,0:T(8,128)S(1)}) custom-call(s32[2]{0:T(128)S(1)} %pad_add_fusion.place, f32[32]{0:T(128)S(1)} %copy-done.2, bf16[8192,128]{1,0:T(8,128)(2,1)S(1)} %prep.1.rows_all, bf16[272,512]{1,0:T(8,128)(2,1)S(1)} %collective-permute-done.5.chunk, ...), custom_call_target="tpu_custom_call" | custom-call | flops 2147483648 | bytes 1048576 | tf_op jit(solution)/shard_map/stats_1/pallas_call | solution.py:210
  39.0 4.4 %collective-permute-done.4.chunk = bf16[272,512]{1,0:T(8,128)(2,1)S(1)} collective-permute-done((bf16[272,512]{1,0:T(8,128)(2,1)S(1)}, bf16[272,512]{1,0:T(8,128)(2,1)S(1)}, u32[]{:S(2)}, u32[]{:S(2)}) %collective-permute-start.4) | collective-permute-done | bytes 278560 | tf_op jit(solution)/shard_map/ppermute | solution.py:262
  43.5 2.6 %stats_2.1 = (f32[16,256]{1,0:T(8,128)S(1)}, f32[16,256]{1,0:T(8,128)S(1)}, f32[16,256]{1,0:T(8,128)S(1)}) custom-call(s32[2]{0:T(128)S(1)} %pad_add_fusion.place, f32[32]{0:T(128)S(1)} %copy-done.2, bf16[8192,128]{1,0:T(8,128)(2,1)S(1)} %prep.1.rows_all, bf16[272,512]{1,0:T(8,128)(2,1)S(1)} %collective-permute-done.4.chunk, ...), custom_call_target="tpu_custom_call" | custom-call | flops 2147483648 | bytes 1048576 | tf_op jit(solution)/shard_map/stats_2/pallas_call | solution.py:210
  46.1 3.4 %stats_3.1 = (f32[16,256]{1,0:T(8,128)S(1)}, f32[16,256]{1,0:T(8,128)S(1)}, f32[16,256]{1,0:T(8,128)S(1)}, f32[256,128]{1,0:T(8,128)}) custom-call(s32[2]{0:T(128)S(1)} %pad_add_fusion.place, f32[32]{0:T(128)S(1)} %copy-done.2, bf16[8192,128]{1,0:T(8,128)(2,1)S(1)} %prep.1.rows_all, bf16[272,512]{1,0:T(8,128)(2,1)S(1)} %collective-permute-done.3.chunk, ...), custom_call_target="tpu_custom_call" | custom-call | flops 2147483648 | bytes 1048576 | tf_op jit(solution)/shard_map/stats_3/pallas_call | solution.py:210
  49.6 1.6 %copy-done.4 = bf16[8192,128]{1,0:T(8,128)(2,1)S(1)} copy-done((bf16[8192,128]{1,0:T(8,128)(2,1)S(1)}, bf16[8192,128]{1,0:T(8,128)(2,1)}, u32[]{:S(2)}) %copy-start.4) | copy-done | bytes 2097176
  51.1 3.3 %parts_4.1 = (bf16[256,512]{1,0:T(8,128)(2,1)S(1)}, f32[256,1024]{1,0:T(8,128)S(1)}) custom-call(s32[2]{0:T(128)S(1)} %pad_add_fusion.place, bf16[8192,128]{1,0:T(8,128)(2,1)S(1)} %copy-done.4, bf16[272,512]{1,0:T(8,128)(2,1)S(1)} %collective-permute-done.2.chunk, bf16[272,512]{1,0:T(8,128)(2,1)S(1)} %maximum_maximum_fusion.chunk.own_chunk, ...), custom_call_target="tpu_custom_call" | custom-call | flops 3221225472 | bytes 1048576 | tf_op jit(solution)/shard_map/parts_4/pallas_call | solution.py:210
  54.4 0.9 collective-permute-start.6
  55.3 3.3 %parts_3.1 = (bf16[256,512]{1,0:T(8,128)(2,1)S(1)}, f32[256,1024]{1,0:T(8,128)S(1)}) custom-call(s32[2]{0:T(128)S(1)} %pad_add_fusion.place, bf16[8192,128]{1,0:T(8,128)(2,1)S(1)} %copy-done.4, bf16[272,512]{1,0:T(8,128)(2,1)S(1)} %collective-permute-done.3.chunk, bf16[272,512]{1,0:T(8,128)(2,1)S(1)} %maximum_maximum_fusion.chunk.own_chunk, ...), custom_call_target="tpu_custom_call" | custom-call | flops 3221225472 | bytes 1048576 | tf_op jit(solution)/shard_map/parts_3/pallas_call | solution.py:210
  58.6 0.3 collective-permute-start.7
  59.0 3.6 %parts_2.1 = (bf16[256,512]{1,0:T(8,128)(2,1)S(1)}, f32[256,1024]{1,0:T(8,128)S(1)}) custom-call(s32[2]{0:T(128)S(1)} %pad_add_fusion.place, bf16[8192,128]{1,0:T(8,128)(2,1)S(1)} %copy-done.4, bf16[272,512]{1,0:T(8,128)(2,1)S(1)} %collective-permute-done.4.chunk, bf16[272,512]{1,0:T(8,128)(2,1)S(1)} %maximum_maximum_fusion.chunk.own_chunk, ...), custom_call_target="tpu_custom_call" | custom-call | flops 3221225472 | bytes 1048576 | tf_op jit(solution)/shard_map/parts_2/pallas_call | solution.py:210
  62.5 3.0 %collective-permute-start.8 = (bf16[256,512]{1,0:T(8,128)(2,1)S(1)}, bf16[256,512]{1,0:T(8,128)(2,1)S(1)}, u32[]{:S(2)}, u32[]{:S(2)}) collective-permute-start(bf16[256,512]{1,0:T(8,128)(2,1)S(1)} %get-tuple-element.85), channel_id=1, source_target_pairs={{0,252},{1,253},{2,254},{3,255},{4,0},{5,1},{6,2},{7,3},{8,4},{9,5... | collective-permute-start | bytes 786440 | tf_op jit(solution)/shard_map/ppermute | solution.py:262
  65.5 3.6 %parts_1.1 = (bf16[256,512]{1,0:T(8,128)(2,1)S(1)}, f32[256,1024]{1,0:T(8,128)S(1)}) custom-call(s32[2]{0:T(128)S(1)} %pad_add_fusion.place, bf16[8192,128]{1,0:T(8,128)(2,1)S(1)} %copy-done.4, bf16[272,512]{1,0:T(8,128)(2,1)S(1)} %collective-permute-done.5.chunk, bf16[272,512]{1,0:T(8,128)(2,1)S(1)} %maximum_maximum_fusion.chunk.own_chunk, ...), custom_call_target="tpu_custom_call" | custom-call | flops 3221225472 | bytes 1048576 | tf_op jit(solution)/shard_map/parts_1/pallas_call | solution.py:210
  69.1 3.6 %collective-permute-start.9 = (bf16[256,512]{1,0:T(8,128)(2,1)S(1)}, bf16[256,512]{1,0:T(8,128)(2,1)S(1)}, u32[]{:S(2)}, u32[]{:S(2)}) collective-permute-start(bf16[256,512]{1,0:T(8,128)(2,1)S(1)} %get-tuple-element.86), channel_id=1, source_target_pairs={{0,254},{1,255},{2,0},{3,1},{4,2},{5,3},{6,4},{7,5},{8,6},{9,7},{1... | collective-permute-start | bytes 786440 | tf_op jit(solution)/shard_map/ppermute | solution.py:262
  72.7 3.4 %parts_0.1 = (f32[256,512]{1,0:T(8,128)S(1)}, bf16[128,1024]{1,0:T(8,128)(2,1)S(1)}, bf16[128,1024]{1,0:T(8,128)(2,1)S(1)}) custom-call(s32[2]{0:T(128)S(1)} %pad_add_fusion.place, bf16[8192,128]{1,0:T(8,128)(2,1)S(1)} %copy-done.4, bf16[272,512]{1,0:T(8,128)(2,1)S(1)} %maximum_maximum_fusion.chunk.own_chunk, ...), custom_call_target="tpu_custom_call" | custom-call | flops 3221225472 | bytes 1048576 | tf_op jit(solution)/shard_map/parts_0/pallas_call | solution.py:210
  76.1 3.2 %collective-permute-done.8 = bf16[256,512]{1,0:T(8,128)(2,1)S(1)} collective-permute-done((bf16[256,512]{1,0:T(8,128)(2,1)S(1)}, bf16[256,512]{1,0:T(8,128)(2,1)S(1)}, u32[]{:S(2)}, u32[]{:S(2)}) %collective-permute-start.8) | collective-permute-done | bytes 262176 | tf_op jit(solution)/shard_map/ppermute | solution.py:262
  79.3 2.2 %collective-permute-done.9 = bf16[256,512]{1,0:T(8,128)(2,1)S(1)} collective-permute-done((bf16[256,512]{1,0:T(8,128)(2,1)S(1)}, bf16[256,512]{1,0:T(8,128)(2,1)S(1)}, u32[]{:S(2)}, u32[]{:S(2)}) %collective-permute-start.9) | collective-permute-done | bytes 262176 | tf_op jit(solution)/shard_map/ppermute | solution.py:262
  81.5 0.2 add_convert_fusion
  81.8 1.4 %collective-permute-start.11 = (bf16[128,1024]{1,0:T(8,128)(2,1)S(1)}, bf16[128,1024]{1,0:T(8,128)(2,1)S(1)}, u32[]{:S(2)}, u32[]{:S(2)}) collective-permute-start(bf16[128,1024]{1,0:T(8,128)(2,1)S(1)} %get-tuple-element.89), channel_id=1, source_target_pairs={{0,1},{1,0},{2,3},{3,2},{4,5},{5,4},{6,7},{7,6},{8,9},{9,8},{10,11... | collective-permute-start | bytes 786440 | tf_op jit(solution)/shard_map/ppermute | solution.py:268
  83.3 1.5 %fold.1 = f32[1,32]{1,0:T(1,128)} custom-call(f32[8,256,128]{2,1,0:T(8,128)} %bitcast.7), custom_call_target="tpu_custom_call" | custom-call | tf_op jit(solution)/shard_map/fold/pallas_call | solution.py:192
  84.8 0.8 collective-permute-start.12
  85.6 3.4 %collective-permute-start.13 = (f32[32]{0:T(128)}, f32[32]{0:T(128)S(1)}, u32[]{:S(2)}, u32[]{:S(2)}) collective-permute-start(f32[32]{0:T(128)} %bitcast.9), channel_id=1, source_target_pairs={{0,16},{1,17},{2,18},{3,19},{4,20},{5,21},{6,22},{7,23},{8,24},{9,... | collective-permute-start | bytes 392 | tf_op jit(solution)/shard_map/ppermute | solution.py:268
  89.0 1.1 collective-permute-done.13
  90.1 3.2 %collective-permute-done.14 = f32[32]{0:T(128)S(1)} collective-permute-done((f32[32]{0:T(128)}, f32[32]{0:T(128)S(1)}, u32[]{:S(2)}, u32[]{:S(2)}) %collective-permute-start.14) | collective-permute-done | bytes 160 | tf_op jit(solution)/shard_map/ppermute | solution.py:268
  93.3 0.7 add_add_fusion.1
  94.0 1.3 %collective-permute-start.15 = (f32[32]{0:T(128)S(1)}, f32[32]{0:T(128)S(1)}, u32[]{:S(2)}, u32[]{:S(2)}) collective-permute-start(f32[32]{0:T(128)S(1)} %add_add_fusion.1), channel_id=1, source_target_pairs={{0,64},{1,65},{2,66},{3,67},{4,68},{5,69},{6,70},{7,71},{8,72},{9,... | collective-permute-start | bytes 392 | tf_op jit(solution)/shard_map/ppermute | solution.py:268
  95.3 2.4 %collective-permute-start.16 = (f32[32]{0:T(128)S(1)}, f32[32]{0:T(128)S(1)}, u32[]{:S(2)}, u32[]{:S(2)}) collective-permute-start(f32[32]{0:T(128)S(1)} %add_add_fusion.1), channel_id=1, source_target_pairs={{0,128},{1,129},{2,130},{3,131},{4,132},{5,133},{6,134},{7,135},{8... | collective-permute-start | bytes 392 | tf_op jit(solution)/shard_map/ppermute | solution.py:268
  97.9 0.9 maximum_select_fusion
  98.8 0.7 maximum_select_fusion.2
  99.5 1.8 %collective-permute-done.17 = f32[32]{0:T(128)S(1)} collective-permute-done((f32[32]{0:T(128)S(1)}, f32[32]{0:T(128)S(1)}, u32[]{:S(2)}, u32[]{:S(2)}) %collective-permute-start.17) | collective-permute-done | bytes 160 | tf_op jit(solution)/shard_map/ppermute | solution.py:268
  101.3 4.2 %collective-permute-start.18 = (f32[32]{0:T(128)S(1)}, f32[32]{0:T(128)S(1)}, u32[]{:S(2)}, u32[]{:S(2)}) collective-permute-start(f32[32]{0:T(128)S(1)} %add_add_fusion), channel_id=1, source_target_pairs={{0,32},{1,33},{2,34},{3,35},{4,36},{5,37},{6,38},{7,39},{8,40},{9,... | collective-permute-start | bytes 392 | tf_op jit(solution)/shard_map/ppermute | solution.py:268
  105.5 0.7 maximum_select_fusion.1
  106.2 1.4 %collective-permute-done.18 = f32[32]{0:T(128)S(1)} collective-permute-done((f32[32]{0:T(128)S(1)}, f32[32]{0:T(128)S(1)}, u32[]{:S(2)}, u32[]{:S(2)}) %collective-permute-start.18) | collective-permute-done | bytes 160 | tf_op jit(solution)/shard_map/ppermute | solution.py:268
  107.6 0.5 add.77
  (40 shorter events, 0.9 us)
Async XLA Ops:
  7.2 74.6 %all-gather.3.cloned.1.call-start = ((), (), s32[]{:S(2)}) async-start(), calls=%async_computation | async-start | bytes 1179648 | tf_op jit(solution)/shard_map/all_gather | solution.py:310
  9.7 6.7 %copy-start = (bf16[128,2048]{1,0:T(8,128)(2,1)S(1)}, bf16[128,2048]{1,0:T(8,128)(2,1)}, u32[]{:S(2)}) copy-start(bf16[128,2048]{1,0:T(8,128)(2,1)} %q_own) | copy-start | bytes 1572868
  9.7 6.7 %copy-start.1 = (bf16[128,2048]{1,0:T(8,128)(2,1)S(1)}, bf16[128,2048]{1,0:T(8,128)(2,1)}, u32[]{:S(2)}) copy-start(bf16[128,2048]{1,0:T(8,128)(2,1)} %g_own) | copy-start | bytes 1572868
  9.8 4.6 %collective-permute-start = (bf16[144,512]{1,0:T(8,128)(2,1)S(1)}, bf16[144,512]{1,0:T(8,128)(2,1)S(1)}, u32[]{:S(2)}, u32[]{:S(2)}) collective-permute-start(bf16[144,512]{1,0:T(8,128)(2,1)S(1)} %pad_maximum_fusion.1), channel_id=1, source_target_pairs={{0,1},{1,0},{2,3},{3,2},{4,5},{5,4},{6,7},{7,6},{8,9},{9,8},{10,11... | collective-permute-start | bytes 442376 | tf_op jit(solution)/shard_map/ppermute | solution.py:268
  14.4 2.0 %collective-permute-start.1 = (bf16[256,1024]{1,0:T(8,128)(2,1)S(1)}, bf16[256,1024]{1,0:T(8,128)(2,1)S(1)}, u32[]{:S(2)}, u32[]{:S(2)}) collective-permute-start(bf16[256,1024]{1,0:T(8,128)(2,1)S(1)} %pad_maximum_fusion), channel_id=1, source_target_pairs={{0,1},{1,0},{2,3},{3,2},{4,5},{5,4},{6,7},{7,6},{8,9},{9,8},{10,11... | collective-permute-start | bytes 1572872 | tf_op jit(solution)/shard_map/ppermute | solution.py:268
  14.7 2.6 %copy-start.2 = (f32[32]{0:T(128)S(1)}, f32[32]{0:T(128)}, u32[]{:S(2)}) copy-start(f32[32]{0:T(128)} %sinks.9) | copy-start | bytes 388
  14.7 12.8 %collective-permute-start.2 = (bf16[272,512]{1,0:T(8,128)(2,1)S(1)}, bf16[272,512]{1,0:T(8,128)(2,1)S(1)}, u32[]{:S(2)}, u32[]{:S(2)}) collective-permute-start(bf16[272,512]{1,0:T(8,128)(2,1)S(1)} %maximum_maximum_fusion.chunk.own_chunk), channel_id=1, source_target_pairs={{0,8},{1,9},{2,10},{3,11},{4,12},{5,13},{6,14},{7,15},{8,16},{9,17... | collective-permute-start | bytes 835592 | tf_op jit(solution)/shard_map/ppermute | solution.py:262
  17.4 28.7 %copy-start.3 = (bf16[8192,128]{1,0:T(8,128)(2,1)}, bf16[8192,128]{1,0:T(8,128)(2,1)S(1)}, u32[]{:S(2)}) copy-start(bf16[8192,128]{1,0:T(8,128)(2,1)S(1)} %prep.1.rows_all) | copy-start | bytes 6291460
  27.7 8.7 %collective-permute-start.5 = (bf16[272,512]{1,0:T(8,128)(2,1)S(1)}, bf16[272,512]{1,0:T(8,128)(2,1)S(1)}, u32[]{:S(2)}, u32[]{:S(2)}) collective-permute-start(bf16[272,512]{1,0:T(8,128)(2,1)S(1)} %get-tuple-element.95), channel_id=1, source_target_pairs={{0,2},{1,3},{2,4},{3,5},{4,6},{5,7},{6,0},{7,1},{8,10},{9,11},{10,... | collective-permute-start | bytes 835592 | tf_op jit(solution)/shard_map/ppermute | solution.py:262
  29.1 14.4 %collective-permute-start.4 = (bf16[272,512]{1,0:T(8,128)(2,1)S(1)}, bf16[272,512]{1,0:T(8,128)(2,1)S(1)}, u32[]{:S(2)}, u32[]{:S(2)}) collective-permute-start(bf16[272,512]{1,0:T(8,128)(2,1)S(1)} %get-tuple-element.94), channel_id=1, source_target_pairs={{0,4},{1,5},{2,6},{3,7},{4,0},{5,1},{6,2},{7,3},{8,12},{9,13},{10,... | collective-permute-start | bytes 835592 | tf_op jit(solution)/shard_map/ppermute | solution.py:262
  31.7 14.4 %collective-permute-start.3 = (bf16[272,512]{1,0:T(8,128)(2,1)S(1)}, bf16[272,512]{1,0:T(8,128)(2,1)S(1)}, u32[]{:S(2)}, u32[]{:S(2)}) collective-permute-start(bf16[272,512]{1,0:T(8,128)(2,1)S(1)} %get-tuple-element.96), channel_id=1, source_target_pairs={{0,6},{1,7},{2,0},{3,1},{4,2},{5,3},{6,4},{7,5},{8,14},{9,15},{10,... | collective-permute-start | bytes 835592 | tf_op jit(solution)/shard_map/ppermute | solution.py:262
  49.5 1.6 %copy-start.4 = (bf16[8192,128]{1,0:T(8,128)(2,1)S(1)}, bf16[8192,128]{1,0:T(8,128)(2,1)}, u32[]{:S(2)}) copy-start(bf16[8192,128]{1,0:T(8,128)(2,1)} %copy-done.3) | copy-start | bytes 6291460
  54.4 11.1 %collective-permute-start.6 = (bf16[256,512]{1,0:T(8,128)(2,1)S(1)}, bf16[256,512]{1,0:T(8,128)(2,1)S(1)}, u32[]{:S(2)}, u32[]{:S(2)}) collective-permute-start(bf16[256,512]{1,0:T(8,128)(2,1)S(1)} %get-tuple-element.76), channel_id=1, source_target_pairs={{0,248},{1,249},{2,250},{3,251},{4,252},{5,253},{6,254},{7,255},{8... | collective-permute-start | bytes 786440 | tf_op jit(solution)/shard_map/ppermute | solution.py:262
  58.6 10.5 %collective-permute-start.7 = (bf16[256,512]{1,0:T(8,128)(2,1)S(1)}, bf16[256,512]{1,0:T(8,128)(2,1)S(1)}, u32[]{:S(2)}, u32[]{:S(2)}) collective-permute-start(bf16[256,512]{1,0:T(8,128)(2,1)S(1)} %get-tuple-element.79), channel_id=1, source_target_pairs={{0,250},{1,251},{2,252},{3,253},{4,254},{5,255},{6,0},{7,1},{8,2},... | collective-permute-start | bytes 786440 | tf_op jit(solution)/shard_map/ppermute | solution.py:262
  62.5 16.8 %collective-permute-start.8 = (bf16[256,512]{1,0:T(8,128)(2,1)S(1)}, bf16[256,512]{1,0:T(8,128)(2,1)S(1)}, u32[]{:S(2)}, u32[]{:S(2)}) collective-permute-start(bf16[256,512]{1,0:T(8,128)(2,1)S(1)} %get-tuple-element.85), channel_id=1, source_target_pairs={{0,252},{1,253},{2,254},{3,255},{4,0},{5,1},{6,2},{7,3},{8,4},{9,5... | collective-permute-start | bytes 786440 | tf_op jit(solution)/shard_map/ppermute | solution.py:262
  69.1 12.4 %collective-permute-start.9 = (bf16[256,512]{1,0:T(8,128)(2,1)S(1)}, bf16[256,512]{1,0:T(8,128)(2,1)S(1)}, u32[]{:S(2)}, u32[]{:S(2)}) collective-permute-start(bf16[256,512]{1,0:T(8,128)(2,1)S(1)} %get-tuple-element.86), channel_id=1, source_target_pairs={{0,254},{1,255},{2,0},{3,1},{4,2},{5,3},{6,4},{7,5},{8,6},{9,7},{1... | collective-permute-start | bytes 786440 | tf_op jit(solution)/shard_map/ppermute | solution.py:262
  81.8 12.2 %collective-permute-start.11 = (bf16[128,1024]{1,0:T(8,128)(2,1)S(1)}, bf16[128,1024]{1,0:T(8,128)(2,1)S(1)}, u32[]{:S(2)}, u32[]{:S(2)}) collective-permute-start(bf16[128,1024]{1,0:T(8,128)(2,1)S(1)} %get-tuple-element.89), channel_id=1, source_target_pairs={{0,1},{1,0},{2,3},{3,2},{4,5},{5,4},{6,7},{7,6},{8,9},{9,8},{10,11... | collective-permute-start | bytes 786440 | tf_op jit(solution)/shard_map/ppermute | solution.py:268
  83.2 10.8 %collective-permute-start.10 = (bf16[128,512]{1,0:T(8,128)(2,1)S(1)}, bf16[128,512]{1,0:T(8,128)(2,1)S(1)}, u32[]{:S(2)}, u32[]{:S(2)}) collective-permute-start(bf16[128,512]{1,0:T(8,128)(2,1)S(1)} %slice.68), channel_id=1, source_target_pairs={{0,1},{1,0},{2,3},{3,2},{4,5},{5,4},{6,7},{7,6},{8,9},{9,8},{10,11... | collective-permute-start | bytes 393224 | tf_op jit(solution)/shard_map/ppermute | solution.py:268
  84.8 4.2 %collective-permute-start.12 = (f32[32]{0:T(128)}, f32[32]{0:T(128)S(1)}, u32[]{:S(2)}, u32[]{:S(2)}) collective-permute-start(f32[32]{0:T(128)} %bitcast.8), channel_id=1, source_target_pairs={{0,8},{1,9},{2,10},{3,11},{4,12},{5,13},{6,14},{7,15},{8,0},{9,1},... | collective-permute-start | bytes 392 | tf_op jit(solution)/shard_map/ppermute | solution.py:268
  85.6 4.5 %collective-permute-start.13 = (f32[32]{0:T(128)}, f32[32]{0:T(128)S(1)}, u32[]{:S(2)}, u32[]{:S(2)}) collective-permute-start(f32[32]{0:T(128)} %bitcast.9), channel_id=1, source_target_pairs={{0,16},{1,17},{2,18},{3,19},{4,20},{5,21},{6,22},{7,23},{8,24},{9,... | collective-permute-start | bytes 392 | tf_op jit(solution)/shard_map/ppermute | solution.py:268
  89.0 4.3 %collective-permute-start.14 = (f32[32]{0:T(128)}, f32[32]{0:T(128)S(1)}, u32[]{:S(2)}, u32[]{:S(2)}) collective-permute-start(f32[32]{0:T(128)} %bitcast.10), channel_id=1, source_target_pairs={{0,24},{1,25},{2,26},{3,27},{4,28},{5,29},{6,30},{7,31},{8,16},{9,... | collective-permute-start | bytes 392 | tf_op jit(solution)/shard_map/ppermute | solution.py:268
  94.0 5.6 %collective-permute-start.15 = (f32[32]{0:T(128)S(1)}, f32[32]{0:T(128)S(1)}, u32[]{:S(2)}, u32[]{:S(2)}) collective-permute-start(f32[32]{0:T(128)S(1)} %add_add_fusion.1), channel_id=1, source_target_pairs={{0,64},{1,65},{2,66},{3,67},{4,68},{5,69},{6,70},{7,71},{8,72},{9,... | collective-permute-start | bytes 392 | tf_op jit(solution)/shard_map/ppermute | solution.py:268
  95.3 4.3 %collective-permute-start.16 = (f32[32]{0:T(128)S(1)}, f32[32]{0:T(128)S(1)}, u32[]{:S(2)}, u32[]{:S(2)}) collective-permute-start(f32[32]{0:T(128)S(1)} %add_add_fusion.1), channel_id=1, source_target_pairs={{0,128},{1,129},{2,130},{3,131},{4,132},{5,133},{6,134},{7,135},{8... | collective-permute-start | bytes 392 | tf_op jit(solution)/shard_map/ppermute | solution.py:268
  97.7 3.6 %collective-permute-start.17 = (f32[32]{0:T(128)S(1)}, f32[32]{0:T(128)S(1)}, u32[]{:S(2)}, u32[]{:S(2)}) collective-permute-start(f32[32]{0:T(128)S(1)} %add_add_fusion.1), channel_id=1, source_target_pairs={{0,192},{1,193},{2,194},{3,195},{4,196},{5,197},{6,198},{7,199},{8... | collective-permute-start | bytes 392 | tf_op jit(solution)/shard_map/ppermute | solution.py:268
  101.3 6.3 %collective-permute-start.18 = (f32[32]{0:T(128)S(1)}, f32[32]{0:T(128)S(1)}, u32[]{:S(2)}, u32[]{:S(2)}) collective-permute-start(f32[32]{0:T(128)S(1)} %add_add_fusion), channel_id=1, source_target_pairs={{0,32},{1,33},{2,34},{3,35},{4,36},{5,37},{6,38},{7,39},{8,40},{9,... | collective-permute-start | bytes 392 | tf_op jit(solution)/shard_map/ppermute | solution.py:268
Sparse Core Ops, SparseCore 0:
  49.7 31.4 all-gather.2

commit v5 on v3

--- a/solution.py
+++ b/solution.py
@@ -276,12 +276,8 @@
     dq, came_back = (), {}
     for hop in range(HOPS, 0, -1):
         part, *dq = parts_of(hop, place, tokens, chunks[hop], chunk, stats, dq, interpret)
-        part, sink_grad = lax.optimization_barrier((part, widened(sink_grad)))
         came_back[hop] = shifted(part, -hop)
-        if hop > 1:
-            sink_grad = widened(sink_grad)
-        else:
-            sink_half, sink_grad = sink_grad, crossed(sink_grad, 1)
+        sink_grad = widened(sink_grad)
         if hop < HOPS:
             dq[0], sink_grad, came_back[hop + 1] = lax.optimization_barrier(
                 (dq[0], sink_grad, came_back[hop + 1])
@@ -289,24 +285,31 @@
         else:
             dq[0], sink_grad = lax.optimization_barrier((dq[0], sink_grad))
     total, dq_own, dq_peer = parts_of(0, place, tokens, chunk, chunk, stats, dq, interpret)
+    dq_own, dq_peer, sink_grad = lax.optimization_barrier(
+        (dq_own, dq_peer, widened(sink_grad))
+    )
 
     def joined(mine, theirs):
         return jnp.where(
             first, jnp.concatenate([mine, theirs], 1), jnp.concatenate([theirs, mine], 1)
         )
 
-    sink_grad = jnp.where(
-        first,
-        jnp.concatenate([sink_half, sink_grad]),
-        jnp.concatenate([sink_grad, sink_half]),
-    )
     query_grad = joined(dq_own, crossed(dq_peer, 1))
     for part in came_back.values():
         total = total + part.astype(F32)
-    total = total.astype(BF16)
-    came, query_grad = lax.optimization_barrier((crossed(total[TOK:], 1), query_grad))
+    total, query_grad, sink_grad = lax.optimization_barrier(
+        (total.astype(BF16), query_grad, widened(sink_grad))
+    )
+    came = crossed(total[TOK:], 1)
     key_grad = joined(total[:TOK, :HALF_KV], came[:, :HALF_KV])
     value_grad = joined(total[:TOK, HALF_KV:], came[:, HALF_KV:])
+    key_grad, value_grad, sink_grad = lax.optimization_barrier(
+        (key_grad, value_grad, widened(sink_grad))
+    )
+    other = crossed(sink_grad, 1)
+    sink_grad = jnp.where(
+        first, jnp.concatenate([sink_grad, other]), jnp.concatenate([other, sink_grad])
+    )
     return query_grad, key_grad, value_grad, sink_grad
 
 

time: 93.1 us -> 89.5 us (0.961)
  waiting for transfers between devices: 20.1 us -> 18 us
  starting transfers between devices: 34 us -> 32.5 us
    ppermute x12, starting transfers between devices: 17.8 us -> 16.3 us  [crossed(): return lax.ppermute(block, 'ctx', [(i, i ^ bit) for i in range(count)])]
    ppermute x12, waiting for transfers between devices: 5.42 us -> 4.32 us  [crossed(): return lax.ppermute(block, 'ctx', [(i, i ^ bit) for i in range(count)])]
    ppermute x8, waiting for transfers between devices: 14.7 us -> 13.7 us  [sent(): return lax.ppermute(block, 'ctx', route)]
  transfers between devices with their start and end apart: 20 -> 20, of which waited for: 8 -> 8; matrix products, arithmetic and copies ran while one was open for 3% -> 2% of each run, Pallas kernels for 30% -> 31%
where the time goes in v5:
time: 89.5 us; the launch traced here: 89.3 us
  starting transfers between devices  32.5 us (36%)
  Pallas kernels  30.7 us (34%)
  waiting for transfers between devices  18 us (20%)
  other arithmetic  5.31 us (6%)
  local copies, waits for them, and re-layouts  1.84 us (2%)
  between operations  0.91 us (1%)
    pallas_call x11, Pallas kernels, run(): pl.pallas_call(kernel, name=name, in_specs=[SMEM] * n_scalars + [VMEM] *...  30.7 us
    ppermute x12, starting transfers between devices, crossed(): return lax.ppermute(block, 'ctx', [(i, i ^ bit) for i in range(count)])  16.3 us
    ppermute x8, starting transfers between devices, sent(): return lax.ppermute(block, 'ctx', route)  16.2 us
    ppermute x8, waiting for transfers between devices, sent(): return lax.ppermute(block, 'ctx', route)  13.7 us
    ppermute x12, waiting for transfers between devices, crossed(): return lax.ppermute(block, 'ctx', [(i, i ^ bit) for i in range(count)])  4.32 us
    select_n x3, other arithmetic, joined(): jnp.where(first, jnp.concatenate([mine, theirs], 1), jnp.concatenate([the...  2.29 us
  transfers between devices with their start and end apart: 20, of which 8 were waited for; matrix products, arithmetic and copies ran while one was open for 2% of the time, Pallas kernels for 31%

profile of v5, /device:TPU:1, one launch (start us, length us, event | category | flops | bytes accessed | tf_op | source)
XLA Modules:
  0.0 89.3 jit_solution(2717437598156694846)
XLA Ops:
  0.6 0.7 convert_bitcast_fusion
  1.3 0.9 fusion.2
  2.2 0.9 fusion.3
  3.2 3.3 %collective-permute-start = (bf16[144,512]{1,0:T(8,128)(2,1)S(1)}, bf16[144,512]{1,0:T(8,128)(2,1)S(1)}, u32[]{:S(2)}, u32[]{:S(2)}) collective-permute-start(bf16[144,512]{1,0:T(8,128)(2,1)S(1)} %pad_maximum_fusion.1), channel_id=1, source_target_pairs={{0,1},{1,0},{2,3},{3,2},{4,5},{5,4},{6,7},{7,6},{8,9},{9,8},{10,11... | collective-permute-start | bytes 442376 | tf_op jit(solution)/shard_map/ppermute | solution.py:228
  6.5 1.2 %slice_select_fusion = (bf16[128,1024]{1,0:T(8,128)(2,1)S(1)}, bf16[128,1024]{1,0:T(8,128)(2,1)S(1)}) fusion(bf16[128,2048]{1,0:T(8,128)(2,1)} %g_own, pred[]{:T(512)S(6)} %eq.8, bf16[128,2048]{1,0:T(8,128)(2,1)} %q_own), kind=kLoop, calls=%fused_computation.7 | loop fusion | flops 262144 | bytes 1572865 | tf_op jit(solution)/shard_map/jit(_where)/select_n | solution.py:248
  7.8 0.2 collective-permute-start.1
  8.0 0.1 pad_add_fusion.place
  8.2 0.1 collective-permute-start.2
  8.3 1.6 %collective-permute-done.1.both_peer = bf16[256,1024]{1,0:T(8,128)(2,1)S(1)} collective-permute-done((bf16[256,1024]{1,0:T(8,128)(2,1)S(1)}, bf16[256,1024]{1,0:T(8,128)(2,1)S(1)}, u32[]{:S(2)}, u32[]{:S(2)}) %collective-permute-start.1) | collective-permute-done | bytes 524320 | tf_op jit(solution)/shard_map/ppermute | solution.py:228
  9.8 1.0 %prep.1.rows_all = bf16[8192,128]{1,0:T(8,128)(2,1)S(1)} custom-call(s32[2]{0:T(128)S(1)} %pad_add_fusion.place, bf16[128,2048]{1,0:T(8,128)(2,1)S(1)} %copy-done, bf16[128,2048]{1,0:T(8,128)(2,1)S(1)} %copy-done.1, bf16[256,1024]{1,0:T(8,128)(2,1)S(1)} %collective-permute-done.1.both_peer), custom_call_target="tpu_custom_call" | custom-call | flops 1073741824 | bytes 1048576 | tf_op jit(solution)/shard_map/prep/pallas_call | solution.py:171
  10.8 2.3 %stats_0.1 = (f32[16,256]{1,0:T(8,128)S(1)}, f32[16,256]{1,0:T(8,128)S(1)}, f32[16,256]{1,0:T(8,128)S(1)}) custom-call(s32[2]{0:T(128)S(1)} %pad_add_fusion.place, f32[32]{0:T(128)S(1)} %copy-done.2, bf16[8192,128]{1,0:T(8,128)(2,1)S(1)} %prep.1.rows_all, bf16[272,512]{1,0:T(8,128)(2,1)S(1)} %maximum_maximum_fusion.chunk.own_chunk, ...), custom_call_target="tpu_custom_call" | custom-call | flops 2147483648 | bytes 1048576 | tf_op jit(solution)/shard_map/stats_0/pallas_call | solution.py:171
  13.2 7.8 %collective-permute-done.2.chunk = bf16[272,512]{1,0:T(8,128)(2,1)S(1)} collective-permute-done((bf16[272,512]{1,0:T(8,128)(2,1)S(1)}, bf16[272,512]{1,0:T(8,128)(2,1)S(1)}, u32[]{:S(2)}, u32[]{:S(2)}) %collective-permute-start.2) | collective-permute-done | bytes 278560 | tf_op jit(solution)/shard_map/ppermute | solution.py:222
  21.0 0.1 broadcast_select_fusion.1
  21.1 1.4 %collective-permute-start.5 = (bf16[272,512]{1,0:T(8,128)(2,1)S(1)}, bf16[272,512]{1,0:T(8,128)(2,1)S(1)}, u32[]{:S(2)}, u32[]{:S(2)}) collective-permute-start(bf16[272,512]{1,0:T(8,128)(2,1)S(1)} %get-tuple-element.117), channel_id=1, source_target_pairs={{0,2},{1,3},{2,4},{3,5},{4,6},{5,7},{6,0},{7,1},{8,10},{9,11},{10,... | collective-permute-start | bytes 835592 | tf_op jit(solution)/shard_map/ppermute | solution.py:222
  22.5 2.6 %collective-permute-start.4 = (bf16[272,512]{1,0:T(8,128)(2,1)S(1)}, bf16[272,512]{1,0:T(8,128)(2,1)S(1)}, u32[]{:S(2)}, u32[]{:S(2)}) collective-permute-start(bf16[272,512]{1,0:T(8,128)(2,1)S(1)} %get-tuple-element.116), channel_id=1, source_target_pairs={{0,4},{1,5},{2,6},{3,7},{4,0},{5,1},{6,2},{7,3},{8,12},{9,13},{10,... | collective-permute-start | bytes 835592 | tf_op jit(solution)/shard_map/ppermute | solution.py:222
  25.1 1.1 %collective-permute-start.3 = (bf16[272,512]{1,0:T(8,128)(2,1)S(1)}, bf16[272,512]{1,0:T(8,128)(2,1)S(1)}, u32[]{:S(2)}, u32[]{:S(2)}) collective-permute-start(bf16[272,512]{1,0:T(8,128)(2,1)S(1)} %get-tuple-element.118), channel_id=1, source_target_pairs={{0,6},{1,7},{2,0},{3,1},{4,2},{5,3},{6,4},{7,5},{8,14},{9,15},{10,... | collective-permute-start | bytes 835592 | tf_op jit(solution)/shard_map/ppermute | solution.py:222
  26.2 2.4 %stats_4.1 = (f32[16,256]{1,0:T(8,128)S(1)}, f32[16,256]{1,0:T(8,128)S(1)}, f32[16,256]{1,0:T(8,128)S(1)}) custom-call(s32[2]{0:T(128)S(1)} %pad_add_fusion.place, f32[32]{0:T(128)S(1)} %copy-done.2, bf16[8192,128]{1,0:T(8,128)(2,1)S(1)} %prep.1.rows_all, bf16[272,512]{1,0:T(8,128)(2,1)S(1)} %collective-permute-done.2.chunk, ...), custom_call_target="tpu_custom_call" | custom-call | flops 2147483648 | bytes 1048576 | tf_op jit(solution)/shard_map/stats_4/pallas_call | solution.py:171
  28.6 1.2 %collective-permute-done.5.chunk = bf16[272,512]{1,0:T(8,128)(2,1)S(1)} collective-permute-done((bf16[272,512]{1,0:T(8,128)(2,1)S(1)}, bf16[272,512]{1,0:T(8,128)(2,1)S(1)}, u32[]{:S(2)}, u32[]{:S(2)}) %collective-permute-start.5) | collective-permute-done | bytes 278560 | tf_op jit(solution)/shard_map/ppermute | solution.py:222
  29.8 2.4 %stats_1.1 = (f32[16,256]{1,0:T(8,128)S(1)}, f32[16,256]{1,0:T(8,128)S(1)}, f32[16,256]{1,0:T(8,128)S(1)}) custom-call(s32[2]{0:T(128)S(1)} %pad_add_fusion.place, f32[32]{0:T(128)S(1)} %copy-done.2, bf16[8192,128]{1,0:T(8,128)(2,1)S(1)} %prep.1.rows_all, bf16[272,512]{1,0:T(8,128)(2,1)S(1)} %collective-permute-done.5.chunk, ...), custom_call_target="tpu_custom_call" | custom-call | flops 2147483648 | bytes 1048576 | tf_op jit(solution)/shard_map/stats_1/pallas_call | solution.py:171
  32.2 4.7 %collective-permute-done.4.chunk = bf16[272,512]{1,0:T(8,128)(2,1)S(1)} collective-permute-done((bf16[272,512]{1,0:T(8,128)(2,1)S(1)}, bf16[272,512]{1,0:T(8,128)(2,1)S(1)}, u32[]{:S(2)}, u32[]{:S(2)}) %collective-permute-start.4) | collective-permute-done | bytes 278560 | tf_op jit(solution)/shard_map/ppermute | solution.py:222
  36.9 2.4 %stats_2.1 = (f32[16,256]{1,0:T(8,128)S(1)}, f32[16,256]{1,0:T(8,128)S(1)}, f32[16,256]{1,0:T(8,128)S(1)}) custom-call(s32[2]{0:T(128)S(1)} %pad_add_fusion.place, f32[32]{0:T(128)S(1)} %copy-done.2, bf16[8192,128]{1,0:T(8,128)(2,1)S(1)} %prep.1.rows_all, bf16[272,512]{1,0:T(8,128)(2,1)S(1)} %collective-permute-done.4.chunk, ...), custom_call_target="tpu_custom_call" | custom-call | flops 2147483648 | bytes 1048576 | tf_op jit(solution)/shard_map/stats_2/pallas_call | solution.py:171
  39.3 2.6 %stats_3.1 = (f32[16,256]{1,0:T(8,128)S(1)}, f32[16,256]{1,0:T(8,128)S(1)}, f32[16,256]{1,0:T(8,128)S(1)}, f32[1,16]{1,0:T(1,128)S(1)}) custom-call(s32[2]{0:T(128)S(1)} %pad_add_fusion.place, f32[32]{0:T(128)S(1)} %copy-done.2, bf16[8192,128]{1,0:T(8,128)(2,1)S(1)} %prep.1.rows_all, bf16[272,512]{1,0:T(8,128)(2,1)S(1)} %collective-permute-done.3.chunk, ...), custom_call_target="tpu_custom_call" | custom-call | flops 2147483648 | bytes 1048576 | tf_op jit(solution)/shard_map/stats_3/pallas_call | solution.py:171
  41.9 0.4 collective-permute-start.6
  42.4 3.5 %parts_4.1 = (bf16[256,512]{1,0:T(8,128)(2,1)S(1)}, f32[256,1024]{1,0:T(8,128)S(1)}) custom-call(s32[2]{0:T(128)S(1)} %pad_add_fusion.place, bf16[8192,128]{1,0:T(8,128)(2,1)S(1)} %prep.1.rows_all, bf16[272,512]{1,0:T(8,128)(2,1)S(1)} %collective-permute-done.2.chunk, bf16[272,512]{1,0:T(8,128)(2,1)S(1)} %maximum_maximum_fusion.chunk.own_chunk, ...), custom_call_target="tpu_custom_call" | custom-call | flops 3221225472 | bytes 1048576 | tf_op jit(solution)/shard_map/parts_4/pallas_call | solution.py:171
  45.9 0.9 collective-permute-start.8
  46.7 3.5 %parts_3.1 = (bf16[256,512]{1,0:T(8,128)(2,1)S(1)}, f32[256,1024]{1,0:T(8,128)S(1)}) custom-call(s32[2]{0:T(128)S(1)} %pad_add_fusion.place, bf16[8192,128]{1,0:T(8,128)(2,1)S(1)} %prep.1.rows_all, bf16[272,512]{1,0:T(8,128)(2,1)S(1)} %collective-permute-done.3.chunk, bf16[272,512]{1,0:T(8,128)(2,1)S(1)} %maximum_maximum_fusion.chunk.own_chunk, ...), custom_call_target="tpu_custom_call" | custom-call | flops 3221225472 | bytes 1048576 | tf_op jit(solution)/shard_map/parts_3/pallas_call | solution.py:171
  50.2 4.2 %collective-permute-start.10 = (bf16[256,512]{1,0:T(8,128)(2,1)S(1)}, bf16[256,512]{1,0:T(8,128)(2,1)S(1)}, u32[]{:S(2)}, u32[]{:S(2)}) collective-permute-start(bf16[256,512]{1,0:T(8,128)(2,1)S(1)} %get-tuple-element.93), channel_id=1, source_target_pairs={{0,250},{1,251},{2,252},{3,253},{4,254},{5,255},{6,0},{7,1},{8,2},... | collective-permute-start | bytes 786440 | tf_op jit(solution)/shard_map/ppermute | solution.py:222
  54.5 1.8 %collective-permute-start.9 = (f32[16]{0:T(128)S(1)}, f32[16]{0:T(128)S(1)}, u32[]{:S(2)}, u32[]{:S(2)}) collective-permute-start(f32[16]{0:T(128)S(1)} %add.60), channel_id=1, source_target_pairs={{0,32},{1,33},{2,34},{3,35},{4,36},{5,37},{6,38},{7,39},{8,40},{9,... | collective-permute-start | bytes 200 | tf_op jit(solution)/shard_map/ppermute | solution.py:228
  56.2 3.5 %parts_2.1 = (bf16[256,512]{1,0:T(8,128)(2,1)S(1)}, f32[256,1024]{1,0:T(8,128)S(1)}) custom-call(s32[2]{0:T(128)S(1)} %pad_add_fusion.place, bf16[8192,128]{1,0:T(8,128)(2,1)S(1)} %prep.1.rows_all, bf16[272,512]{1,0:T(8,128)(2,1)S(1)} %collective-permute-done.4.chunk, bf16[272,512]{1,0:T(8,128)(2,1)S(1)} %maximum_maximum_fusion.chunk.own_chunk, ...), custom_call_target="tpu_custom_call" | custom-call | flops 3221225472 | bytes 1048576 | tf_op jit(solution)/shard_map/parts_2/pallas_call | solution.py:171
  59.7 2.5 %collective-permute-start.12 = (bf16[256,512]{1,0:T(8,128)(2,1)S(1)}, bf16[256,512]{1,0:T(8,128)(2,1)S(1)}, u32[]{:S(2)}, u32[]{:S(2)}) collective-permute-start(bf16[256,512]{1,0:T(8,128)(2,1)S(1)} %get-tuple-element.97), channel_id=1, source_target_pairs={{0,252},{1,253},{2,254},{3,255},{4,0},{5,1},{6,2},{7,3},{8,4},{9,5... | collective-permute-start | bytes 786440 | tf_op jit(solution)/shard_map/ppermute | solution.py:222
  62.2 0.4 collective-permute-start.11
  62.6 3.5 %parts_1.1 = (bf16[256,512]{1,0:T(8,128)(2,1)S(1)}, f32[256,1024]{1,0:T(8,128)S(1)}) custom-call(s32[2]{0:T(128)S(1)} %pad_add_fusion.place, bf16[8192,128]{1,0:T(8,128)(2,1)S(1)} %prep.1.rows_all, bf16[272,512]{1,0:T(8,128)(2,1)S(1)} %collective-permute-done.5.chunk, bf16[272,512]{1,0:T(8,128)(2,1)S(1)} %maximum_maximum_fusion.chunk.own_chunk, ...), custom_call_target="tpu_custom_call" | custom-call | flops 3221225472 | bytes 1048576 | tf_op jit(solution)/shard_map/parts_1/pallas_call | solution.py:171
  66.1 3.5 %collective-permute-start.13 = (bf16[256,512]{1,0:T(8,128)(2,1)S(1)}, bf16[256,512]{1,0:T(8,128)(2,1)S(1)}, u32[]{:S(2)}, u32[]{:S(2)}) collective-permute-start(bf16[256,512]{1,0:T(8,128)(2,1)S(1)} %get-tuple-element.103), channel_id=1, source_target_pairs={{0,254},{1,255},{2,0},{3,1},{4,2},{5,3},{6,4},{7,5},{8,6},{9,7},{1... | collective-permute-start | bytes 786440 | tf_op jit(solution)/shard_map/ppermute | solution.py:222
  69.6 0.4 collective-permute-start.14
  70.0 3.6 %parts_0.1 = (f32[256,512]{1,0:T(8,128)S(1)}, bf16[128,1024]{1,0:T(8,128)(2,1)S(1)}, bf16[128,1024]{1,0:T(8,128)(2,1)S(1)}) custom-call(s32[2]{0:T(128)S(1)} %pad_add_fusion.place, bf16[8192,128]{1,0:T(8,128)(2,1)S(1)} %prep.1.rows_all, bf16[272,512]{1,0:T(8,128)(2,1)S(1)} %maximum_maximum_fusion.chunk.own_chunk, ...), custom_call_target="tpu_custom_call" | custom-call | flops 3221225472 | bytes 1048576 | tf_op jit(solution)/shard_map/parts_0/pallas_call | solution.py:171
  73.6 0.7 collective-permute-start.16
  74.3 5.0 %collective-permute-start.15 = (bf16[128,1024]{1,0:T(8,128)(2,1)S(1)}, bf16[128,1024]{1,0:T(8,128)(2,1)S(1)}, u32[]{:S(2)}, u32[]{:S(2)}) collective-permute-start(bf16[128,1024]{1,0:T(8,128)(2,1)S(1)} %get-tuple-element.108), channel_id=1, source_target_pairs={{0,1},{1,0},{2,3},{3,2},{4,5},{5,4},{6,7},{7,6},{8,9},{9,8},{10,11... | collective-permute-start | bytes 786440 | tf_op jit(solution)/shard_map/ppermute | solution.py:228
  79.4 0.2 add_convert_fusion
  79.6 1.0 %collective-permute-done.15 = bf16[128,1024]{1,0:T(8,128)(2,1)S(1)} collective-permute-done((bf16[128,1024]{1,0:T(8,128)(2,1)S(1)}, bf16[128,1024]{1,0:T(8,128)(2,1)S(1)}, u32[]{:S(2)}, u32[]{:S(2)}) %collective-permute-start.15) | collective-permute-done | bytes 262176 | tf_op jit(solution)/shard_map/ppermute | solution.py:228
  80.5 0.9 %maximum_select_fusion = bf16[128,2048]{1,0:T(8,128)(2,1)} fusion(bf16[128,1024]{1,0:T(8,128)(2,1)S(1)} %collective-permute-done.15, bf16[128,1024]{1,0:T(8,128)(2,1)S(1)} %get-tuple-element.107, pred[]{:T(512)S(6)} %eq.8), kind=kLoop, calls=%fused_computation.1 | loop fusion | flops 2359296 | bytes 1048577 | tf_op jit(solution)/shard_map/jit(_where)/select_n | solution.py:293
  81.5 1.6 %collective-permute-start.17 = (bf16[128,512]{1,0:T(8,128)(2,1)S(1)}, bf16[128,512]{1,0:T(8,128)(2,1)S(1)}, u32[]{:S(2)}, u32[]{:S(2)}) collective-permute-start(bf16[128,512]{1,0:T(8,128)(2,1)S(1)} %slice.64), channel_id=1, source_target_pairs={{0,1},{1,0},{2,3},{3,2},{4,5},{5,4},{6,7},{7,6},{8,9},{9,8},{10,11... | collective-permute-start | bytes 393224 | tf_op jit(solution)/shard_map/ppermute | solution.py:228
  83.1 0.8 collective-permute-done.18
  83.9 0.2 collective-permute-done.17
  84.1 0.7 maximum_select_fusion.2
  84.8 0.7 maximum_select_fusion.1
  85.4 2.5 %collective-permute-start.19 = (f32[16]{0:T(128)S(1)}, f32[16]{0:T(128)S(1)}, u32[]{:S(2)}, u32[]{:S(2)}) collective-permute-start(f32[16]{0:T(128)S(1)} %add.69), channel_id=1, source_target_pairs={{0,1},{1,0},{2,3},{3,2},{4,5},{5,4},{6,7},{7,6},{8,9},{9,8},{10,11... | collective-permute-start | bytes 200 | tf_op jit(solution)/shard_map/ppermute | solution.py:228
  87.9 0.8 collective-permute-done.19
  88.7 0.6 broadcast_select_fusion.5
  (39 shorter events, 0.3 us)
Async XLA Ops:
  3.1 6.7 %copy-start = (bf16[128,2048]{1,0:T(8,128)(2,1)S(1)}, bf16[128,2048]{1,0:T(8,128)(2,1)}, u32[]{:S(2)}) copy-start(bf16[128,2048]{1,0:T(8,128)(2,1)} %q_own) | copy-start | bytes 1572868
  3.1 6.7 %copy-start.1 = (bf16[128,2048]{1,0:T(8,128)(2,1)S(1)}, bf16[128,2048]{1,0:T(8,128)(2,1)}, u32[]{:S(2)}) copy-start(bf16[128,2048]{1,0:T(8,128)(2,1)} %g_own) | copy-start | bytes 1572868
  3.2 4.6 %collective-permute-start = (bf16[144,512]{1,0:T(8,128)(2,1)S(1)}, bf16[144,512]{1,0:T(8,128)(2,1)S(1)}, u32[]{:S(2)}, u32[]{:S(2)}) collective-permute-start(bf16[144,512]{1,0:T(8,128)(2,1)S(1)} %pad_maximum_fusion.1), channel_id=1, source_target_pairs={{0,1},{1,0},{2,3},{3,2},{4,5},{5,4},{6,7},{7,6},{8,9},{9,8},{10,11... | collective-permute-start | bytes 442376 | tf_op jit(solution)/shard_map/ppermute | solution.py:228
  7.8 2.0 %collective-permute-start.1 = (bf16[256,1024]{1,0:T(8,128)(2,1)S(1)}, bf16[256,1024]{1,0:T(8,128)(2,1)S(1)}, u32[]{:S(2)}, u32[]{:S(2)}) collective-permute-start(bf16[256,1024]{1,0:T(8,128)(2,1)S(1)} %pad_maximum_fusion), channel_id=1, source_target_pairs={{0,1},{1,0},{2,3},{3,2},{4,5},{5,4},{6,7},{7,6},{8,9},{9,8},{10,11... | collective-permute-start | bytes 1572872 | tf_op jit(solution)/shard_map/ppermute | solution.py:228
  8.2 2.7 %copy-start.2 = (f32[32]{0:T(128)S(1)}, f32[32]{0:T(128)}, u32[]{:S(2)}) copy-start(f32[32]{0:T(128)} %sinks.9) | copy-start | bytes 388
  8.2 12.8 %collective-permute-start.2 = (bf16[272,512]{1,0:T(8,128)(2,1)S(1)}, bf16[272,512]{1,0:T(8,128)(2,1)S(1)}, u32[]{:S(2)}, u32[]{:S(2)}) collective-permute-start(bf16[272,512]{1,0:T(8,128)(2,1)S(1)} %maximum_maximum_fusion.chunk.own_chunk), channel_id=1, source_target_pairs={{0,8},{1,9},{2,10},{3,11},{4,12},{5,13},{6,14},{7,15},{8,16},{9,17... | collective-permute-start | bytes 835592 | tf_op jit(solution)/shard_map/ppermute | solution.py:222
  21.1 8.7 %collective-permute-start.5 = (bf16[272,512]{1,0:T(8,128)(2,1)S(1)}, bf16[272,512]{1,0:T(8,128)(2,1)S(1)}, u32[]{:S(2)}, u32[]{:S(2)}) collective-permute-start(bf16[272,512]{1,0:T(8,128)(2,1)S(1)} %get-tuple-element.117), channel_id=1, source_target_pairs={{0,2},{1,3},{2,4},{3,5},{4,6},{5,7},{6,0},{7,1},{8,10},{9,11},{10,... | collective-permute-start | bytes 835592 | tf_op jit(solution)/shard_map/ppermute | solution.py:222
  22.5 14.4 %collective-permute-start.4 = (bf16[272,512]{1,0:T(8,128)(2,1)S(1)}, bf16[272,512]{1,0:T(8,128)(2,1)S(1)}, u32[]{:S(2)}, u32[]{:S(2)}) collective-permute-start(bf16[272,512]{1,0:T(8,128)(2,1)S(1)} %get-tuple-element.116), channel_id=1, source_target_pairs={{0,4},{1,5},{2,6},{3,7},{4,0},{5,1},{6,2},{7,3},{8,12},{9,13},{10,... | collective-permute-start | bytes 835592 | tf_op jit(solution)/shard_map/ppermute | solution.py:222
  25.1 14.2 %collective-permute-start.3 = (bf16[272,512]{1,0:T(8,128)(2,1)S(1)}, bf16[272,512]{1,0:T(8,128)(2,1)S(1)}, u32[]{:S(2)}, u32[]{:S(2)}) collective-permute-start(bf16[272,512]{1,0:T(8,128)(2,1)S(1)} %get-tuple-element.118), channel_id=1, source_target_pairs={{0,6},{1,7},{2,0},{3,1},{4,2},{5,3},{6,4},{7,5},{8,14},{9,15},{10,... | collective-permute-start | bytes 835592 | tf_op jit(solution)/shard_map/ppermute | solution.py:222
  41.9 4.8 %collective-permute-start.6 = (f32[16]{0:T(128)S(1)}, f32[16]{0:T(128)S(1)}, u32[]{:S(2)}, u32[]{:S(2)}) collective-permute-start(f32[16]{0:T(128)S(1)} %bitcast.6), channel_id=1, source_target_pairs={{0,4},{1,5},{2,6},{3,7},{4,0},{5,1},{6,2},{7,3},{8,12},{9,13},{10,... | collective-permute-start | bytes 200 | tf_op jit(solution)/shard_map/ppermute | solution.py:228
  45.9 8.6 %collective-permute-start.8 = (bf16[256,512]{1,0:T(8,128)(2,1)S(1)}, bf16[256,512]{1,0:T(8,128)(2,1)S(1)}, u32[]{:S(2)}, u32[]{:S(2)}) collective-permute-start(bf16[256,512]{1,0:T(8,128)(2,1)S(1)} %get-tuple-element.89), channel_id=1, source_target_pairs={{0,248},{1,249},{2,250},{3,251},{4,252},{5,253},{6,254},{7,255},{8... | collective-permute-start | bytes 786440 | tf_op jit(solution)/shard_map/ppermute | solution.py:222
  46.7 7.7 %collective-permute-start.7 = (f32[16]{0:T(128)S(1)}, f32[16]{0:T(128)S(1)}, u32[]{:S(2)}, u32[]{:S(2)}) collective-permute-start(f32[16]{0:T(128)S(1)} %bitcast_add_fusion), channel_id=1, source_target_pairs={{0,16},{1,17},{2,18},{3,19},{4,20},{5,21},{6,22},{7,23},{8,24},{9,... | collective-permute-start | bytes 200 | tf_op jit(solution)/shard_map/ppermute | solution.py:228
  50.2 12.0 %collective-permute-start.10 = (bf16[256,512]{1,0:T(8,128)(2,1)S(1)}, bf16[256,512]{1,0:T(8,128)(2,1)S(1)}, u32[]{:S(2)}, u32[]{:S(2)}) collective-permute-start(bf16[256,512]{1,0:T(8,128)(2,1)S(1)} %get-tuple-element.93), channel_id=1, source_target_pairs={{0,250},{1,251},{2,252},{3,253},{4,254},{5,255},{6,0},{7,1},{8,2},... | collective-permute-start | bytes 786440 | tf_op jit(solution)/shard_map/ppermute | solution.py:222
  54.5 7.8 %collective-permute-start.9 = (f32[16]{0:T(128)S(1)}, f32[16]{0:T(128)S(1)}, u32[]{:S(2)}, u32[]{:S(2)}) collective-permute-start(f32[16]{0:T(128)S(1)} %add.60), channel_id=1, source_target_pairs={{0,32},{1,33},{2,34},{3,35},{4,36},{5,37},{6,38},{7,39},{8,40},{9,... | collective-permute-start | bytes 200 | tf_op jit(solution)/shard_map/ppermute | solution.py:228
  59.7 9.9 %collective-permute-start.12 = (bf16[256,512]{1,0:T(8,128)(2,1)S(1)}, bf16[256,512]{1,0:T(8,128)(2,1)S(1)}, u32[]{:S(2)}, u32[]{:S(2)}) collective-permute-start(bf16[256,512]{1,0:T(8,128)(2,1)S(1)} %get-tuple-element.97), channel_id=1, source_target_pairs={{0,252},{1,253},{2,254},{3,255},{4,0},{5,1},{6,2},{7,3},{8,4},{9,5... | collective-permute-start | bytes 786440 | tf_op jit(solution)/shard_map/ppermute | solution.py:222
  62.2 7.4 %collective-permute-start.11 = (f32[16]{0:T(128)S(1)}, f32[16]{0:T(128)S(1)}, u32[]{:S(2)}, u32[]{:S(2)}) collective-permute-start(f32[16]{0:T(128)S(1)} %add.61), channel_id=1, source_target_pairs={{0,128},{1,129},{2,130},{3,131},{4,132},{5,133},{6,134},{7,135},{8... | collective-permute-start | bytes 200 | tf_op jit(solution)/shard_map/ppermute | solution.py:228
  66.1 13.3 %collective-permute-start.13 = (bf16[256,512]{1,0:T(8,128)(2,1)S(1)}, bf16[256,512]{1,0:T(8,128)(2,1)S(1)}, u32[]{:S(2)}, u32[]{:S(2)}) collective-permute-start(bf16[256,512]{1,0:T(8,128)(2,1)S(1)} %get-tuple-element.103), channel_id=1, source_target_pairs={{0,254},{1,255},{2,0},{3,1},{4,2},{5,3},{6,4},{7,5},{8,6},{9,7},{1... | collective-permute-start | bytes 786440 | tf_op jit(solution)/shard_map/ppermute | solution.py:222
  69.6 4.0 %collective-permute-start.14 = (f32[16]{0:T(128)S(1)}, f32[16]{0:T(128)S(1)}, u32[]{:S(2)}, u32[]{:S(2)}) collective-permute-start(f32[16]{0:T(128)S(1)} %add.62), channel_id=1, source_target_pairs={{0,8},{1,9},{2,10},{3,11},{4,12},{5,13},{6,14},{7,15},{8,0},{9,1},... | collective-permute-start | bytes 200 | tf_op jit(solution)/shard_map/ppermute | solution.py:228
  73.6 5.9 %collective-permute-start.16 = (f32[16]{0:T(128)S(1)}, f32[16]{0:T(128)S(1)}, u32[]{:S(2)}, u32[]{:S(2)}) collective-permute-start(f32[16]{0:T(128)S(1)} %add.67), channel_id=1, source_target_pairs={{0,64},{1,65},{2,66},{3,67},{4,68},{5,69},{6,70},{7,71},{8,72},{9,... | collective-permute-start | bytes 200 | tf_op jit(solution)/shard_map/ppermute | solution.py:228
  74.3 6.2 %collective-permute-start.15 = (bf16[128,1024]{1,0:T(8,128)(2,1)S(1)}, bf16[128,1024]{1,0:T(8,128)(2,1)S(1)}, u32[]{:S(2)}, u32[]{:S(2)}) collective-permute-start(bf16[128,1024]{1,0:T(8,128)(2,1)S(1)} %get-tuple-element.108), channel_id=1, source_target_pairs={{0,1},{1,0},{2,3},{3,2},{4,5},{5,4},{6,7},{7,6},{8,9},{9,8},{10,11... | collective-permute-start | bytes 786440 | tf_op jit(solution)/shard_map/ppermute | solution.py:228
  81.5 2.4 %collective-permute-start.18 = (f32[16]{0:T(128)S(1)}, f32[16]{0:T(128)S(1)}, u32[]{:S(2)}, u32[]{:S(2)}) collective-permute-start(f32[16]{0:T(128)S(1)} %add.68), channel_id=1, source_target_pairs={{0,2},{1,3},{2,0},{3,1},{4,6},{5,7},{6,4},{7,5},{8,10},{9,11},{10,... | collective-permute-start | bytes 200 | tf_op jit(solution)/shard_map/ppermute | solution.py:228
  81.5 2.6 %collective-permute-start.17 = (bf16[128,512]{1,0:T(8,128)(2,1)S(1)}, bf16[128,512]{1,0:T(8,128)(2,1)S(1)}, u32[]{:S(2)}, u32[]{:S(2)}) collective-permute-start(bf16[128,512]{1,0:T(8,128)(2,1)S(1)} %slice.64), channel_id=1, source_target_pairs={{0,1},{1,0},{2,3},{3,2},{4,5},{5,4},{6,7},{7,6},{8,9},{9,8},{10,11... | collective-permute-start | bytes 393224 | tf_op jit(solution)/shard_map/ppermute | solution.py:228
  85.4 3.3 %collective-permute-start.19 = (f32[16]{0:T(128)S(1)}, f32[16]{0:T(128)S(1)}, u32[]{:S(2)}, u32[]{:S(2)}) collective-permute-start(f32[16]{0:T(128)S(1)} %add.69), channel_id=1, source_target_pairs={{0,1},{1,0},{2,3},{3,2},{4,5},{5,4},{6,7},{7,6},{8,9},{9,8},{10,11... | collective-permute-start | bytes 200 | tf_op jit(solution)/shard_map/ppermute | solution.py:228

commit v6 on v5

--- a/solution.py
+++ b/solution.py
@@ -257,14 +257,20 @@
         0, False, place, sink_logits, tokens, chunk, chunk, (), interpret
     )
     *stats, chunks[HOPS] = lax.optimization_barrier((*stats, chunks[HOPS]))
-    for hop in range(1, HOPS):
+    def row_place(i):
+        return i // 2 % ROW
+
+    for hop in (1, 3):
         within = chip % ROW + hop < ROW
         chunks[hop] = sent(
             jnp.where(within, chunk, chunks[HOPS]), [(i, in_row(i, hop)) for i in range(count)]
         )
-    for hop in (HOPS, 1, 2, 3):
+    crossing = [(i, in_row(i, 2)) for i in range(count) if row_place(i) == 2]
+    relayed = [(i, in_row(i, 1)) for i in range(count) if row_place(i) < ROW - 1]
+    chunks[2] = sent(chunks[HOPS], crossing) + sent(chunks[1], relayed)
+    for hop in (HOPS, 1, 3, 2):
         stats = stats_of(
-            hop, hop == 3, place, sink_logits, tokens, chunks[hop], chunk, stats, interpret
+            hop, hop == 2, place, sink_logits, tokens, chunks[hop], chunk, stats, interpret
         )
     *stats, sink_row = stats
     sink_grad = sink_row.reshape(16)
@@ -297,15 +303,12 @@
     query_grad = joined(dq_own, crossed(dq_peer, 1))
     for part in came_back.values():
         total = total + part.astype(F32)
-    total, query_grad, sink_grad = lax.optimization_barrier(
-        (total.astype(BF16), query_grad, widened(sink_grad))
-    )
-    came = crossed(total[TOK:], 1)
+    total, sink_grad = lax.optimization_barrier((total.astype(BF16), widened(sink_grad)))
+    came, query_grad, sink_grad = lax.optimization_barrier(
+        (crossed(total[TOK:], 1), query_grad, widened(sink_grad))
+    )
     key_grad = joined(total[:TOK, :HALF_KV], came[:, :HALF_KV])
     value_grad = joined(total[:TOK, HALF_KV:], came[:, HALF_KV:])
-    key_grad, value_grad, sink_grad = lax.optimization_barrier(
-        (key_grad, value_grad, widened(sink_grad))
-    )
     other = crossed(sink_grad, 1)
     sink_grad = jnp.where(
         first, jnp.concatenate([sink_grad, other]), jnp.concatenate([other, sink_grad])

time: 89.5 us -> 91.6 us (1.023)
  starting transfers between devices: 32.5 us -> 40.2 us
  waiting for transfers between devices: 18 us -> 12.3 us
    ppermute x12, starting transfers between devices: 16.3 us -> 25 us  [crossed(): return lax.ppermute(block, 'ctx', [(i, i ^ bit) for i in range(count)])]
    ppermute x8 -> x9, waiting for transfers between devices: 13.7 us -> 10.7 us  [sent(): return lax.ppermute(block, 'ctx', route)]
    ppermute x12, waiting for transfers between devices: 4.32 us -> 1.63 us  [crossed(): return lax.ppermute(block, 'ctx', [(i, i ^ bit) for i in range(count)])]
    ppermute x8 -> x9, starting transfers between devices: 16.2 us -> 15.1 us  [sent(): return lax.ppermute(block, 'ctx', route)]
  transfers between devices with their start and end apart: 20 -> 21, of which waited for: 8 -> 5; matrix products, arithmetic and copies ran while one was open for 2% -> 4% of each run, Pallas kernels for 31% -> 31%
where the time goes in v6:
time: 91.6 us; the launch traced here: 91.3 us
  starting transfers between devices  40.2 us (44%)
  Pallas kernels  30.7 us (34%)
  waiting for transfers between devices  12.3 us (13%)
  other arithmetic  5.35 us (6%)
  local copies, waits for them, and re-layouts  1.84 us (2%)
  between operations  0.95 us (1%)
    pallas_call x11, Pallas kernels, run(): pl.pallas_call(kernel, name=name, in_specs=[SMEM] * n_scalars + [VMEM] *...  30.7 us
    ppermute x12, starting transfers between devices, crossed(): return lax.ppermute(block, 'ctx', [(i, i ^ bit) for i in range(count)])  25 us
    ppermute x9, starting transfers between devices, sent(): return lax.ppermute(block, 'ctx', route)  15.1 us
    ppermute x9, waiting for transfers between devices, sent(): return lax.ppermute(block, 'ctx', route)  10.7 us
    select_n x3, other arithmetic, joined(): jnp.where(first, jnp.concatenate([mine, theirs], 1), jnp.concatenate([the...  2.29 us
  transfers between devices with their start and end apart: 21, of which 5 were waited for; matrix products, arithmetic and copies ran while one was open for 4% of the time, Pallas kernels for 31%

profile of v6, /device:TPU:1, one launch (start us, length us, event | category | flops | bytes accessed | tf_op | source)
XLA Modules:
  0.0 91.3 jit_solution(16305917747991448176)
XLA Ops:
  0.6 0.7 convert_bitcast_fusion
  1.3 0.9 fusion.2
  2.2 0.9 fusion.3
  3.2 3.3 %collective-permute-start = (bf16[144,512]{1,0:T(8,128)(2,1)S(1)}, bf16[144,512]{1,0:T(8,128)(2,1)S(1)}, u32[]{:S(2)}, u32[]{:S(2)}) collective-permute-start(bf16[144,512]{1,0:T(8,128)(2,1)S(1)} %pad_maximum_fusion.1), channel_id=1, source_target_pairs={{0,1},{1,0},{2,3},{3,2},{4,5},{5,4},{6,7},{7,6},{8,9},{9,8},{10,11... | collective-permute-start | bytes 442376 | tf_op jit(solution)/shard_map/ppermute | solution.py:228
  6.5 1.2 %slice_select_fusion = (bf16[128,1024]{1,0:T(8,128)(2,1)S(1)}, bf16[128,1024]{1,0:T(8,128)(2,1)S(1)}) fusion(bf16[128,2048]{1,0:T(8,128)(2,1)} %g_own, pred[]{:T(512)S(6)} %eq.7, bf16[128,2048]{1,0:T(8,128)(2,1)} %q_own), kind=kLoop, calls=%fused_computation.6 | loop fusion | flops 262144 | bytes 1572865 | tf_op jit(solution)/shard_map/jit(_where)/select_n | solution.py:248
  7.8 0.2 collective-permute-start.1
  8.0 0.1 pad_add_fusion.place
  8.2 0.1 collective-permute-start.2
  8.3 1.6 %collective-permute-done.1.both_peer = bf16[256,1024]{1,0:T(8,128)(2,1)S(1)} collective-permute-done((bf16[256,1024]{1,0:T(8,128)(2,1)S(1)}, bf16[256,1024]{1,0:T(8,128)(2,1)S(1)}, u32[]{:S(2)}, u32[]{:S(2)}) %collective-permute-start.1) | collective-permute-done | bytes 524320 | tf_op jit(solution)/shard_map/ppermute | solution.py:228
  9.8 1.0 %prep.1.rows_all = bf16[8192,128]{1,0:T(8,128)(2,1)S(1)} custom-call(s32[2]{0:T(128)S(1)} %pad_add_fusion.place, bf16[128,2048]{1,0:T(8,128)(2,1)S(1)} %copy-done, bf16[128,2048]{1,0:T(8,128)(2,1)S(1)} %copy-done.1, bf16[256,1024]{1,0:T(8,128)(2,1)S(1)} %collective-permute-done.1.both_peer), custom_call_target="tpu_custom_call" | custom-call | flops 1073741824 | bytes 1048576 | tf_op jit(solution)/shard_map/prep/pallas_call | solution.py:171
  10.8 2.3 %stats_0.1 = (f32[16,256]{1,0:T(8,128)S(1)}, f32[16,256]{1,0:T(8,128)S(1)}, f32[16,256]{1,0:T(8,128)S(1)}) custom-call(s32[2]{0:T(128)S(1)} %pad_add_fusion.place, f32[32]{0:T(128)S(1)} %copy-done.2, bf16[8192,128]{1,0:T(8,128)(2,1)S(1)} %prep.1.rows_all, bf16[272,512]{1,0:T(8,128)(2,1)S(1)} %maximum_maximum_fusion.chunk.own_chunk, ...), custom_call_target="tpu_custom_call" | custom-call | flops 2147483648 | bytes 1048576 | tf_op jit(solution)/shard_map/stats_0/pallas_call | solution.py:171
  13.2 7.8 %collective-permute-done.2.chunk = bf16[272,512]{1,0:T(8,128)(2,1)S(1)} collective-permute-done((bf16[272,512]{1,0:T(8,128)(2,1)S(1)}, bf16[272,512]{1,0:T(8,128)(2,1)S(1)}, u32[]{:S(2)}, u32[]{:S(2)}) %collective-permute-start.2) | collective-permute-done | bytes 278560 | tf_op jit(solution)/shard_map/ppermute | solution.py:222
  21.0 0.1 broadcast_select_fusion
  21.1 1.4 %collective-permute-start.4 = (bf16[272,512]{1,0:T(8,128)(2,1)S(1)}, bf16[272,512]{1,0:T(8,128)(2,1)S(1)}, u32[]{:S(2)}, u32[]{:S(2)}) collective-permute-start(bf16[272,512]{1,0:T(8,128)(2,1)S(1)} %get-tuple-element.115), channel_id=1, source_target_pairs={{0,2},{1,3},{2,4},{3,5},{4,6},{5,7},{6,0},{7,1},{8,10},{9,11},{10,... | collective-permute-start | bytes 835592 | tf_op jit(solution)/shard_map/ppermute | solution.py:222
  22.5 1.3 %collective-permute-start.3 = (bf16[272,512]{1,0:T(8,128)(2,1)S(1)}, bf16[272,512]{1,0:T(8,128)(2,1)S(1)}, u32[]{:S(2)}, u32[]{:S(2)}) collective-permute-start(bf16[272,512]{1,0:T(8,128)(2,1)S(1)} %collective-permute-done.2.chunk), channel_id=1, source_target_pairs={{4,0},{5,1},{12,8},{13,9},{20,16},{21,17},{28,24},{29,25},{36,32},... | collective-permute-start | bytes 835592 | tf_op jit(solution)/shard_map/ppermute | solution.py:222
  23.8 0.9 %collective-permute-start.6 = (bf16[272,512]{1,0:T(8,128)(2,1)S(1)}, bf16[272,512]{1,0:T(8,128)(2,1)S(1)}, u32[]{:S(2)}, u32[]{:S(2)}) collective-permute-start(bf16[272,512]{1,0:T(8,128)(2,1)S(1)} %get-tuple-element.114), channel_id=1, source_target_pairs={{0,6},{1,7},{2,0},{3,1},{4,2},{5,3},{6,4},{7,5},{8,14},{9,15},{10,... | collective-permute-start | bytes 835592 | tf_op jit(solution)/shard_map/ppermute | solution.py:222
  24.7 2.4 %stats_4.1 = (f32[16,256]{1,0:T(8,128)S(1)}, f32[16,256]{1,0:T(8,128)S(1)}, f32[16,256]{1,0:T(8,128)S(1)}) custom-call(s32[2]{0:T(128)S(1)} %pad_add_fusion.place, f32[32]{0:T(128)S(1)} %copy-done.2, bf16[8192,128]{1,0:T(8,128)(2,1)S(1)} %prep.1.rows_all, bf16[272,512]{1,0:T(8,128)(2,1)S(1)} %collective-permute-done.2.chunk, ...), custom_call_target="tpu_custom_call" | custom-call | flops 2147483648 | bytes 1048576 | tf_op jit(solution)/shard_map/stats_4/pallas_call | solution.py:171
  27.1 2.7 %collective-permute-done.4.chunk = bf16[272,512]{1,0:T(8,128)(2,1)S(1)} collective-permute-done((bf16[272,512]{1,0:T(8,128)(2,1)S(1)}, bf16[272,512]{1,0:T(8,128)(2,1)S(1)}, u32[]{:S(2)}, u32[]{:S(2)}) %collective-permute-start.4) | collective-permute-done | bytes 278560 | tf_op jit(solution)/shard_map/ppermute | solution.py:222
  29.8 2.0 %collective-permute-start.5 = (bf16[272,512]{1,0:T(8,128)(2,1)S(1)}, bf16[272,512]{1,0:T(8,128)(2,1)S(1)}, u32[]{:S(2)}, u32[]{:S(2)}) collective-permute-start(bf16[272,512]{1,0:T(8,128)(2,1)S(1)} %collective-permute-done.4.chunk), channel_id=1, source_target_pairs={{0,2},{1,3},{2,4},{3,5},{4,6},{5,7},{8,10},{9,11},{10,12},{11,13},... | collective-permute-start | bytes 835592 | tf_op jit(solution)/shard_map/ppermute | solution.py:222
  31.8 2.4 %stats_1.1 = (f32[16,256]{1,0:T(8,128)S(1)}, f32[16,256]{1,0:T(8,128)S(1)}, f32[16,256]{1,0:T(8,128)S(1)}) custom-call(s32[2]{0:T(128)S(1)} %pad_add_fusion.place, f32[32]{0:T(128)S(1)} %copy-done.2, bf16[8192,128]{1,0:T(8,128)(2,1)S(1)} %prep.1.rows_all, bf16[272,512]{1,0:T(8,128)(2,1)S(1)} %collective-permute-done.4.chunk, ...), custom_call_target="tpu_custom_call" | custom-call | flops 2147483648 | bytes 1048576 | tf_op jit(solution)/shard_map/stats_1/pallas_call | solution.py:171
  34.2 2.4 %stats_3.1 = (f32[16,256]{1,0:T(8,128)S(1)}, f32[16,256]{1,0:T(8,128)S(1)}, f32[16,256]{1,0:T(8,128)S(1)}) custom-call(s32[2]{0:T(128)S(1)} %pad_add_fusion.place, f32[32]{0:T(128)S(1)} %copy-done.2, bf16[8192,128]{1,0:T(8,128)(2,1)S(1)} %prep.1.rows_all, bf16[272,512]{1,0:T(8,128)(2,1)S(1)} %collective-permute-done.6.chunk, ...), custom_call_target="tpu_custom_call" | custom-call | flops 2147483648 | bytes 1048576 | tf_op jit(solution)/shard_map/stats_3/pallas_call | solution.py:171
  36.7 0.2 collective-permute-done.3
  36.8 0.1 add.56.chunk
  36.9 2.6 %stats_2.1 = (f32[16,256]{1,0:T(8,128)S(1)}, f32[16,256]{1,0:T(8,128)S(1)}, f32[16,256]{1,0:T(8,128)S(1)}, f32[1,16]{1,0:T(1,128)S(1)}) custom-call(s32[2]{0:T(128)S(1)} %pad_add_fusion.place, f32[32]{0:T(128)S(1)} %copy-done.2, bf16[8192,128]{1,0:T(8,128)(2,1)S(1)} %prep.1.rows_all, bf16[272,512]{1,0:T(8,128)(2,1)S(1)} %add.56.chunk, ...), custom_call_target="tpu_custom_call" | custom-call | flops 2147483648 | bytes 1048576 | tf_op jit(solution)/shard_map/stats_2/pallas_call | solution.py:171
  39.6 5.3 %collective-permute-start.7 = (f32[16]{0:T(128)S(1)}, f32[16]{0:T(128)S(1)}, u32[]{:S(2)}, u32[]{:S(2)}) collective-permute-start(f32[16]{0:T(128)S(1)} %bitcast.6), channel_id=1, source_target_pairs={{0,4},{1,5},{2,6},{3,7},{4,0},{5,1},{6,2},{7,3},{8,12},{9,13},{10,... | collective-permute-start | bytes 200 | tf_op jit(solution)/shard_map/ppermute | solution.py:228
  44.8 3.5 %parts_4.1 = (bf16[256,512]{1,0:T(8,128)(2,1)S(1)}, f32[256,1024]{1,0:T(8,128)S(1)}) custom-call(s32[2]{0:T(128)S(1)} %pad_add_fusion.place, bf16[8192,128]{1,0:T(8,128)(2,1)S(1)} %prep.1.rows_all, bf16[272,512]{1,0:T(8,128)(2,1)S(1)} %collective-permute-done.2.chunk, bf16[272,512]{1,0:T(8,128)(2,1)S(1)} %maximum_maximum_fusion.chunk.own_chunk, ...), custom_call_target="tpu_custom_call" | custom-call | flops 3221225472 | bytes 1048576 | tf_op jit(solution)/shard_map/parts_4/pallas_call | solution.py:171
  48.3 0.9 collective-permute-start.9
  49.2 3.5 %parts_3.1 = (bf16[256,512]{1,0:T(8,128)(2,1)S(1)}, f32[256,1024]{1,0:T(8,128)S(1)}) custom-call(s32[2]{0:T(128)S(1)} %pad_add_fusion.place, bf16[8192,128]{1,0:T(8,128)(2,1)S(1)} %prep.1.rows_all, bf16[272,512]{1,0:T(8,128)(2,1)S(1)} %collective-permute-done.6.chunk, bf16[272,512]{1,0:T(8,128)(2,1)S(1)} %maximum_maximum_fusion.chunk.own_chunk, ...), custom_call_target="tpu_custom_call" | custom-call | flops 3221225472 | bytes 1048576 | tf_op jit(solution)/shard_map/parts_3/pallas_call | solution.py:171
  52.7 4.5 %collective-permute-start.11 = (bf16[256,512]{1,0:T(8,128)(2,1)S(1)}, bf16[256,512]{1,0:T(8,128)(2,1)S(1)}, u32[]{:S(2)}, u32[]{:S(2)}) collective-permute-start(bf16[256,512]{1,0:T(8,128)(2,1)S(1)} %get-tuple-element.92), channel_id=1, source_target_pairs={{0,250},{1,251},{2,252},{3,253},{4,254},{5,255},{6,0},{7,1},{8,2},... | collective-permute-start | bytes 786440 | tf_op jit(solution)/shard_map/ppermute | solution.py:222
  57.2 2.1 %collective-permute-start.10 = (f32[16]{0:T(128)S(1)}, f32[16]{0:T(128)S(1)}, u32[]{:S(2)}, u32[]{:S(2)}) collective-permute-start(f32[16]{0:T(128)S(1)} %add.59), channel_id=1, source_target_pairs={{0,32},{1,33},{2,34},{3,35},{4,36},{5,37},{6,38},{7,39},{8,40},{9,... | collective-permute-start | bytes 200 | tf_op jit(solution)/shard_map/ppermute | solution.py:228
  59.3 3.5 %parts_2.1 = (bf16[256,512]{1,0:T(8,128)(2,1)S(1)}, f32[256,1024]{1,0:T(8,128)S(1)}) custom-call(s32[2]{0:T(128)S(1)} %pad_add_fusion.place, bf16[8192,128]{1,0:T(8,128)(2,1)S(1)} %prep.1.rows_all, bf16[272,512]{1,0:T(8,128)(2,1)S(1)} %add.56.chunk, bf16[272,512]{1,0:T(8,128)(2,1)S(1)} %maximum_maximum_fusion.chunk.own_chunk, ...), custom_call_target="tpu_custom_call" | custom-call | flops 3221225472 | bytes 1048576 | tf_op jit(solution)/shard_map/parts_2/pallas_call | solution.py:171
  62.8 1.5 %collective-permute-start.13 = (bf16[256,512]{1,0:T(8,128)(2,1)S(1)}, bf16[256,512]{1,0:T(8,128)(2,1)S(1)}, u32[]{:S(2)}, u32[]{:S(2)}) collective-permute-start(bf16[256,512]{1,0:T(8,128)(2,1)S(1)} %get-tuple-element.96), channel_id=1, source_target_pairs={{0,252},{1,253},{2,254},{3,255},{4,0},{5,1},{6,2},{7,3},{8,4},{9,5... | collective-permute-start | bytes 786440 | tf_op jit(solution)/shard_map/ppermute | solution.py:222
  64.3 0.3 collective-permute-start.12
  64.6 3.5 %parts_1.1 = (bf16[256,512]{1,0:T(8,128)(2,1)S(1)}, f32[256,1024]{1,0:T(8,128)S(1)}) custom-call(s32[2]{0:T(128)S(1)} %pad_add_fusion.place, bf16[8192,128]{1,0:T(8,128)(2,1)S(1)} %prep.1.rows_all, bf16[272,512]{1,0:T(8,128)(2,1)S(1)} %collective-permute-done.4.chunk, bf16[272,512]{1,0:T(8,128)(2,1)S(1)} %maximum_maximum_fusion.chunk.own_chunk, ...), custom_call_target="tpu_custom_call" | custom-call | flops 3221225472 | bytes 1048576 | tf_op jit(solution)/shard_map/parts_1/pallas_call | solution.py:171
  68.1 2.6 %collective-permute-start.14 = (bf16[256,512]{1,0:T(8,128)(2,1)S(1)}, bf16[256,512]{1,0:T(8,128)(2,1)S(1)}, u32[]{:S(2)}, u32[]{:S(2)}) collective-permute-start(bf16[256,512]{1,0:T(8,128)(2,1)S(1)} %get-tuple-element.102), channel_id=1, source_target_pairs={{0,254},{1,255},{2,0},{3,1},{4,2},{5,3},{6,4},{7,5},{8,6},{9,7},{1... | collective-permute-start | bytes 786440 | tf_op jit(solution)/shard_map/ppermute | solution.py:222
  70.7 0.4 collective-permute-start.15
  71.0 3.6 %parts_0.1 = (f32[256,512]{1,0:T(8,128)S(1)}, bf16[128,1024]{1,0:T(8,128)(2,1)S(1)}, bf16[128,1024]{1,0:T(8,128)(2,1)S(1)}) custom-call(s32[2]{0:T(128)S(1)} %pad_add_fusion.place, bf16[8192,128]{1,0:T(8,128)(2,1)S(1)} %prep.1.rows_all, bf16[272,512]{1,0:T(8,128)(2,1)S(1)} %maximum_maximum_fusion.chunk.own_chunk, ...), custom_call_target="tpu_custom_call" | custom-call | flops 3221225472 | bytes 1048576 | tf_op jit(solution)/shard_map/parts_0/pallas_call | solution.py:171
  74.7 0.7 collective-permute-start.16
  75.4 6.6 %collective-permute-start.18 = (bf16[128,1024]{1,0:T(8,128)(2,1)S(1)}, bf16[128,1024]{1,0:T(8,128)(2,1)S(1)}, u32[]{:S(2)}, u32[]{:S(2)}) collective-permute-start(bf16[128,1024]{1,0:T(8,128)(2,1)S(1)} %get-tuple-element.109), channel_id=1, source_target_pairs={{0,1},{1,0},{2,3},{3,2},{4,5},{5,4},{6,7},{7,6},{8,9},{9,8},{10,11... | collective-permute-start | bytes 786440 | tf_op jit(solution)/shard_map/ppermute | solution.py:228
  82.0 0.2 add_convert_fusion
  82.2 0.1 collective-permute-start.19
  82.3 2.7 %collective-permute-start.17 = (bf16[128,512]{1,0:T(8,128)(2,1)S(1)}, bf16[128,512]{1,0:T(8,128)(2,1)S(1)}, u32[]{:S(2)}, u32[]{:S(2)}) collective-permute-start(bf16[128,512]{1,0:T(8,128)(2,1)S(1)} %slice.63), channel_id=1, source_target_pairs={{0,1},{1,0},{2,3},{3,2},{4,5},{5,4},{6,7},{7,6},{8,9},{9,8},{10,11... | collective-permute-start | bytes 393224 | tf_op jit(solution)/shard_map/ppermute | solution.py:228
  85.0 0.9 %maximum_select_fusion = bf16[128,2048]{1,0:T(8,128)(2,1)} fusion(bf16[128,1024]{1,0:T(8,128)(2,1)S(1)} %collective-permute-done.18, bf16[128,1024]{1,0:T(8,128)(2,1)S(1)} %get-tuple-element.108, pred[]{:T(512)S(6)} %eq.7), kind=kLoop, calls=%fused_computation.1 | loop fusion | flops 2359296 | bytes 1048577 | tf_op jit(solution)/shard_map/jit(_where)/select_n | solution.py:299
  86.0 0.1 collective-permute-done.17
  86.0 3.4 %collective-permute-start.20 = (f32[16]{0:T(128)S(1)}, f32[16]{0:T(128)S(1)}, u32[]{:S(2)}, u32[]{:S(2)}) collective-permute-start(f32[16]{0:T(128)S(1)} %add.68), channel_id=1, source_target_pairs={{0,1},{1,0},{2,3},{3,2},{4,5},{5,4},{6,7},{7,6},{8,9},{9,8},{10,11... | collective-permute-start | bytes 200 | tf_op jit(solution)/shard_map/ppermute | solution.py:228
  89.4 0.7 maximum_select_fusion.2
  90.1 0.7 maximum_select_fusion.1
  90.8 0.6 broadcast_select_fusion.4
  (42 shorter events, 0.3 us)
Async XLA Ops:
  3.1 6.7 %copy-start = (bf16[128,2048]{1,0:T(8,128)(2,1)S(1)}, bf16[128,2048]{1,0:T(8,128)(2,1)}, u32[]{:S(2)}) copy-start(bf16[128,2048]{1,0:T(8,128)(2,1)} %q_own) | copy-start | bytes 1572868
  3.1 6.7 %copy-start.1 = (bf16[128,2048]{1,0:T(8,128)(2,1)S(1)}, bf16[128,2048]{1,0:T(8,128)(2,1)}, u32[]{:S(2)}) copy-start(bf16[128,2048]{1,0:T(8,128)(2,1)} %g_own) | copy-start | bytes 1572868
  3.2 4.6 %collective-permute-start = (bf16[144,512]{1,0:T(8,128)(2,1)S(1)}, bf16[144,512]{1,0:T(8,128)(2,1)S(1)}, u32[]{:S(2)}, u32[]{:S(2)}) collective-permute-start(bf16[144,512]{1,0:T(8,128)(2,1)S(1)} %pad_maximum_fusion.1), channel_id=1, source_target_pairs={{0,1},{1,0},{2,3},{3,2},{4,5},{5,4},{6,7},{7,6},{8,9},{9,8},{10,11... | collective-permute-start | bytes 442376 | tf_op jit(solution)/shard_map/ppermute | solution.py:228
  7.8 2.0 %collective-permute-start.1 = (bf16[256,1024]{1,0:T(8,128)(2,1)S(1)}, bf16[256,1024]{1,0:T(8,128)(2,1)S(1)}, u32[]{:S(2)}, u32[]{:S(2)}) collective-permute-start(bf16[256,1024]{1,0:T(8,128)(2,1)S(1)} %pad_maximum_fusion), channel_id=1, source_target_pairs={{0,1},{1,0},{2,3},{3,2},{4,5},{5,4},{6,7},{7,6},{8,9},{9,8},{10,11... | collective-permute-start | bytes 1572872 | tf_op jit(solution)/shard_map/ppermute | solution.py:228
  8.2 2.7 %copy-start.2 = (f32[32]{0:T(128)S(1)}, f32[32]{0:T(128)}, u32[]{:S(2)}) copy-start(f32[32]{0:T(128)} %sinks.9) | copy-start | bytes 388
  8.2 12.8 %collective-permute-start.2 = (bf16[272,512]{1,0:T(8,128)(2,1)S(1)}, bf16[272,512]{1,0:T(8,128)(2,1)S(1)}, u32[]{:S(2)}, u32[]{:S(2)}) collective-permute-start(bf16[272,512]{1,0:T(8,128)(2,1)S(1)} %maximum_maximum_fusion.chunk.own_chunk), channel_id=1, source_target_pairs={{0,8},{1,9},{2,10},{3,11},{4,12},{5,13},{6,14},{7,15},{8,16},{9,17... | collective-permute-start | bytes 835592 | tf_op jit(solution)/shard_map/ppermute | solution.py:222
  21.1 8.7 %collective-permute-start.4 = (bf16[272,512]{1,0:T(8,128)(2,1)S(1)}, bf16[272,512]{1,0:T(8,128)(2,1)S(1)}, u32[]{:S(2)}, u32[]{:S(2)}) collective-permute-start(bf16[272,512]{1,0:T(8,128)(2,1)S(1)} %get-tuple-element.115), channel_id=1, source_target_pairs={{0,2},{1,3},{2,4},{3,5},{4,6},{5,7},{6,0},{7,1},{8,10},{9,11},{10,... | collective-permute-start | bytes 835592 | tf_op jit(solution)/shard_map/ppermute | solution.py:222
  22.5 14.4 %collective-permute-start.3 = (bf16[272,512]{1,0:T(8,128)(2,1)S(1)}, bf16[272,512]{1,0:T(8,128)(2,1)S(1)}, u32[]{:S(2)}, u32[]{:S(2)}) collective-permute-start(bf16[272,512]{1,0:T(8,128)(2,1)S(1)} %collective-permute-done.2.chunk), channel_id=1, source_target_pairs={{4,0},{5,1},{12,8},{13,9},{20,16},{21,17},{28,24},{29,25},{36,32},... | collective-permute-start | bytes 835592 | tf_op jit(solution)/shard_map/ppermute | solution.py:222
  23.8 10.5 %collective-permute-start.6 = (bf16[272,512]{1,0:T(8,128)(2,1)S(1)}, bf16[272,512]{1,0:T(8,128)(2,1)S(1)}, u32[]{:S(2)}, u32[]{:S(2)}) collective-permute-start(bf16[272,512]{1,0:T(8,128)(2,1)S(1)} %get-tuple-element.114), channel_id=1, source_target_pairs={{0,6},{1,7},{2,0},{3,1},{4,2},{5,3},{6,4},{7,5},{8,14},{9,15},{10,... | collective-permute-start | bytes 835592 | tf_op jit(solution)/shard_map/ppermute | solution.py:222
  29.8 7.1 %collective-permute-start.5 = (bf16[272,512]{1,0:T(8,128)(2,1)S(1)}, bf16[272,512]{1,0:T(8,128)(2,1)S(1)}, u32[]{:S(2)}, u32[]{:S(2)}) collective-permute-start(bf16[272,512]{1,0:T(8,128)(2,1)S(1)} %collective-permute-done.4.chunk), channel_id=1, source_target_pairs={{0,2},{1,3},{2,4},{3,5},{4,6},{5,7},{8,10},{9,11},{10,12},{11,13},... | collective-permute-start | bytes 835592 | tf_op jit(solution)/shard_map/ppermute | solution.py:222
  39.6 9.6 %collective-permute-start.7 = (f32[16]{0:T(128)S(1)}, f32[16]{0:T(128)S(1)}, u32[]{:S(2)}, u32[]{:S(2)}) collective-permute-start(f32[16]{0:T(128)S(1)} %bitcast.6), channel_id=1, source_target_pairs={{0,4},{1,5},{2,6},{3,7},{4,0},{5,1},{6,2},{7,3},{8,12},{9,13},{10,... | collective-permute-start | bytes 200 | tf_op jit(solution)/shard_map/ppermute | solution.py:228
  48.3 8.9 %collective-permute-start.9 = (bf16[256,512]{1,0:T(8,128)(2,1)S(1)}, bf16[256,512]{1,0:T(8,128)(2,1)S(1)}, u32[]{:S(2)}, u32[]{:S(2)}) collective-permute-start(bf16[256,512]{1,0:T(8,128)(2,1)S(1)} %get-tuple-element.88), channel_id=1, source_target_pairs={{0,248},{1,249},{2,250},{3,251},{4,252},{5,253},{6,254},{7,255},{8... | collective-permute-start | bytes 786440 | tf_op jit(solution)/shard_map/ppermute | solution.py:222
  49.2 8.0 %collective-permute-start.8 = (f32[16]{0:T(128)S(1)}, f32[16]{0:T(128)S(1)}, u32[]{:S(2)}, u32[]{:S(2)}) collective-permute-start(f32[16]{0:T(128)S(1)} %bitcast_add_fusion), channel_id=1, source_target_pairs={{0,16},{1,17},{2,18},{3,19},{4,20},{5,21},{6,22},{7,23},{8,24},{9,... | collective-permute-start | bytes 200 | tf_op jit(solution)/shard_map/ppermute | solution.py:228
  52.7 11.6 %collective-permute-start.11 = (bf16[256,512]{1,0:T(8,128)(2,1)S(1)}, bf16[256,512]{1,0:T(8,128)(2,1)S(1)}, u32[]{:S(2)}, u32[]{:S(2)}) collective-permute-start(bf16[256,512]{1,0:T(8,128)(2,1)S(1)} %get-tuple-element.92), channel_id=1, source_target_pairs={{0,250},{1,251},{2,252},{3,253},{4,254},{5,255},{6,0},{7,1},{8,2},... | collective-permute-start | bytes 786440 | tf_op jit(solution)/shard_map/ppermute | solution.py:222
  57.2 7.1 %collective-permute-start.10 = (f32[16]{0:T(128)S(1)}, f32[16]{0:T(128)S(1)}, u32[]{:S(2)}, u32[]{:S(2)}) collective-permute-start(f32[16]{0:T(128)S(1)} %add.59), channel_id=1, source_target_pairs={{0,32},{1,33},{2,34},{3,35},{4,36},{5,37},{6,38},{7,39},{8,40},{9,... | collective-permute-start | bytes 200 | tf_op jit(solution)/shard_map/ppermute | solution.py:228
  62.8 7.9 %collective-permute-start.13 = (bf16[256,512]{1,0:T(8,128)(2,1)S(1)}, bf16[256,512]{1,0:T(8,128)(2,1)S(1)}, u32[]{:S(2)}, u32[]{:S(2)}) collective-permute-start(bf16[256,512]{1,0:T(8,128)(2,1)S(1)} %get-tuple-element.96), channel_id=1, source_target_pairs={{0,252},{1,253},{2,254},{3,255},{4,0},{5,1},{6,2},{7,3},{8,4},{9,5... | collective-permute-start | bytes 786440 | tf_op jit(solution)/shard_map/ppermute | solution.py:222
  64.3 6.4 %collective-permute-start.12 = (f32[16]{0:T(128)S(1)}, f32[16]{0:T(128)S(1)}, u32[]{:S(2)}, u32[]{:S(2)}) collective-permute-start(f32[16]{0:T(128)S(1)} %add.60), channel_id=1, source_target_pairs={{0,128},{1,129},{2,130},{3,131},{4,132},{5,133},{6,134},{7,135},{8... | collective-permute-start | bytes 200 | tf_op jit(solution)/shard_map/ppermute | solution.py:228
  68.1 13.9 %collective-permute-start.14 = (bf16[256,512]{1,0:T(8,128)(2,1)S(1)}, bf16[256,512]{1,0:T(8,128)(2,1)S(1)}, u32[]{:S(2)}, u32[]{:S(2)}) collective-permute-start(bf16[256,512]{1,0:T(8,128)(2,1)S(1)} %get-tuple-element.102), channel_id=1, source_target_pairs={{0,254},{1,255},{2,0},{3,1},{4,2},{5,3},{6,4},{7,5},{8,6},{9,7},{1... | collective-permute-start | bytes 786440 | tf_op jit(solution)/shard_map/ppermute | solution.py:222
  70.7 4.0 %collective-permute-start.15 = (f32[16]{0:T(128)S(1)}, f32[16]{0:T(128)S(1)}, u32[]{:S(2)}, u32[]{:S(2)}) collective-permute-start(f32[16]{0:T(128)S(1)} %add.61), channel_id=1, source_target_pairs={{0,8},{1,9},{2,10},{3,11},{4,12},{5,13},{6,14},{7,15},{8,0},{9,1},... | collective-permute-start | bytes 200 | tf_op jit(solution)/shard_map/ppermute | solution.py:228
  74.7 7.5 %collective-permute-start.16 = (f32[16]{0:T(128)S(1)}, f32[16]{0:T(128)S(1)}, u32[]{:S(2)}, u32[]{:S(2)}) collective-permute-start(f32[16]{0:T(128)S(1)} %add.66), channel_id=1, source_target_pairs={{0,64},{1,65},{2,66},{3,67},{4,68},{5,69},{6,70},{7,71},{8,72},{9,... | collective-permute-start | bytes 200 | tf_op jit(solution)/shard_map/ppermute | solution.py:228
  75.4 9.6 %collective-permute-start.18 = (bf16[128,1024]{1,0:T(8,128)(2,1)S(1)}, bf16[128,1024]{1,0:T(8,128)(2,1)S(1)}, u32[]{:S(2)}, u32[]{:S(2)}) collective-permute-start(bf16[128,1024]{1,0:T(8,128)(2,1)S(1)} %get-tuple-element.109), channel_id=1, source_target_pairs={{0,1},{1,0},{2,3},{3,2},{4,5},{5,4},{6,7},{7,6},{8,9},{9,8},{10,11... | collective-permute-start | bytes 786440 | tf_op jit(solution)/shard_map/ppermute | solution.py:228
  82.2 2.9 %collective-permute-start.19 = (f32[16]{0:T(128)S(1)}, f32[16]{0:T(128)S(1)}, u32[]{:S(2)}, u32[]{:S(2)}) collective-permute-start(f32[16]{0:T(128)S(1)} %add.67), channel_id=1, source_target_pairs={{0,2},{1,3},{2,0},{3,1},{4,6},{5,7},{6,4},{7,5},{8,10},{9,11},{10,... | collective-permute-start | bytes 200 | tf_op jit(solution)/shard_map/ppermute | solution.py:228
  82.3 3.7 %collective-permute-start.17 = (bf16[128,512]{1,0:T(8,128)(2,1)S(1)}, bf16[128,512]{1,0:T(8,128)(2,1)S(1)}, u32[]{:S(2)}, u32[]{:S(2)}) collective-permute-start(bf16[128,512]{1,0:T(8,128)(2,1)S(1)} %slice.63), channel_id=1, source_target_pairs={{0,1},{1,0},{2,3},{3,2},{4,5},{5,4},{6,7},{7,6},{8,9},{9,8},{10,11... | collective-permute-start | bytes 393224 | tf_op jit(solution)/shard_map/ppermute | solution.py:228
  86.0 4.8 %collective-permute-start.20 = (f32[16]{0:T(128)S(1)}, f32[16]{0:T(128)S(1)}, u32[]{:S(2)}, u32[]{:S(2)}) collective-permute-start(f32[16]{0:T(128)S(1)} %add.68), channel_id=1, source_target_pairs={{0,1},{1,0},{2,3},{3,2},{4,5},{5,4},{6,7},{7,6},{8,9},{9,8},{10,11... | collective-permute-start | bytes 200 | tf_op jit(solution)/shard_map/ppermute | solution.py:228

commit v7 on v6

--- a/solution.py
+++ b/solution.py
@@ -257,17 +257,11 @@
         0, False, place, sink_logits, tokens, chunk, chunk, (), interpret
     )
     *stats, chunks[HOPS] = lax.optimization_barrier((*stats, chunks[HOPS]))
-    def row_place(i):
-        return i // 2 % ROW
-
-    for hop in (1, 3):
+    for hop in range(1, HOPS):
         within = chip % ROW + hop < ROW
         chunks[hop] = sent(
             jnp.where(within, chunk, chunks[HOPS]), [(i, in_row(i, hop)) for i in range(count)]
         )
-    crossing = [(i, in_row(i, 2)) for i in range(count) if row_place(i) == 2]
-    relayed = [(i, in_row(i, 1)) for i in range(count) if row_place(i) < ROW - 1]
-    chunks[2] = sent(chunks[HOPS], crossing) + sent(chunks[1], relayed)
     for hop in (HOPS, 1, 3, 2):
         stats = stats_of(
             hop, hop == 2, place, sink_logits, tokens, chunks[hop], chunk, stats, interpret
@@ -284,9 +278,9 @@
         part, *dq = parts_of(hop, place, tokens, chunks[hop], chunk, stats, dq, interpret)
         came_back[hop] = shifted(part, -hop)
         sink_grad = widened(sink_grad)
-        if hop < HOPS:
-            dq[0], sink_grad, came_back[hop + 1] = lax.optimization_barrier(
-                (dq[0], sink_grad, came_back[hop + 1])
+        if hop + 2 in came_back:
+            dq[0], sink_grad, came_back[hop + 2] = lax.optimization_barrier(
+                (dq[0], sink_grad, came_back[hop + 2])
             )
         else:
             dq[0], sink_grad = lax.optimization_barrier((dq[0], sink_grad))

time: 91.6 us -> 89.2 us (0.974)
  starting transfers between devices: 40.2 us -> 34.7 us
  waiting for transfers between devices: 12.3 us -> 15.5 us
    ppermute x12, starting transfers between devices: 25 us -> 20.2 us  [crossed(): return lax.ppermute(block, 'ctx', [(i, i ^ bit) for i in range(count)])]
    ppermute x12, waiting for transfers between devices: 1.63 us -> 3.56 us  [crossed(): return lax.ppermute(block, 'ctx', [(i, i ^ bit) for i in range(count)])]
    ppermute x9 -> x8, waiting for transfers between devices: 10.7 us -> 11.9 us  [sent(): return lax.ppermute(block, 'ctx', route)]
    ppermute x9 -> x8, starting transfers between devices: 15.1 us -> 14.5 us  [sent(): return lax.ppermute(block, 'ctx', route)]
  transfers between devices with their start and end apart: 21 -> 20, of which waited for: 5 -> 6; matrix products, arithmetic and copies ran while one was open for 4% -> 4% of each run, Pallas kernels for 31% -> 32%
where the time goes in v7:
time: 89.2 us; the launch traced here: 88.9 us
  starting transfers between devices  34.7 us (39%)
  Pallas kernels  30.7 us (34%)
  waiting for transfers between devices  15.5 us (17%)
  other arithmetic  5.32 us (6%)
  local copies, waits for them, and re-layouts  1.84 us (2%)
  between operations  0.91 us (1%)
    pallas_call x11, Pallas kernels, run(): pl.pallas_call(kernel, name=name, in_specs=[SMEM] * n_scalars + [VMEM] *...  30.7 us
    ppermute x12, starting transfers between devices, crossed(): return lax.ppermute(block, 'ctx', [(i, i ^ bit) for i in range(count)])  20.2 us
    ppermute x8, starting transfers between devices, sent(): return lax.ppermute(block, 'ctx', route)  14.5 us
    ppermute x8, waiting for transfers between devices, sent(): return lax.ppermute(block, 'ctx', route)  11.9 us
    ppermute x12, waiting for transfers between devices, crossed(): return lax.ppermute(block, 'ctx', [(i, i ^ bit) for i in range(count)])  3.56 us
    select_n x3, other arithmetic, joined(): jnp.where(first, jnp.concatenate([mine, theirs], 1), jnp.concatenate([the...  2.29 us
  transfers between devices with their start and end apart: 20, of which 6 were waited for; matrix products, arithmetic and copies ran while one was open for 4% of the time, Pallas kernels for 32%

profile of v7, /device:TPU:1, one launch (start us, length us, event | category | flops | bytes accessed | tf_op | source)
XLA Modules:
  0.0 88.9 jit_solution(543291486213166554)
XLA Ops:
  0.6 0.7 convert_bitcast_fusion
  1.3 0.9 fusion.2
  2.2 0.9 fusion.3
  3.1 0.0 copy-start
  3.2 3.3 %collective-permute-start = (bf16[144,512]{1,0:T(8,128)(2,1)S(1)}, bf16[144,512]{1,0:T(8,128)(2,1)S(1)}, u32[]{:S(2)}, u32[]{:S(2)}) collective-permute-start(bf16[144,512]{1,0:T(8,128)(2,1)S(1)} %pad_maximum_fusion.1), channel_id=1, source_target_pairs={{0,1},{1,0},{2,3},{3,2},{4,5},{5,4},{6,7},{7,6},{8,9},{9,8},{10,11... | collective-permute-start | bytes 442376 | tf_op jit(solution)/shard_map/ppermute | solution.py:228
  6.5 1.2 %slice_select_fusion = (bf16[128,1024]{1,0:T(8,128)(2,1)S(1)}, bf16[128,1024]{1,0:T(8,128)(2,1)S(1)}) fusion(bf16[128,2048]{1,0:T(8,128)(2,1)} %g_own, pred[]{:T(512)S(6)} %eq.8, bf16[128,2048]{1,0:T(8,128)(2,1)} %q_own), kind=kLoop, calls=%fused_computation.7 | loop fusion | flops 262144 | bytes 1572865 | tf_op jit(solution)/shard_map/jit(_where)/select_n | solution.py:248
  7.8 0.2 collective-permute-start.1
  8.0 0.1 pad_add_fusion.place
  8.2 0.1 collective-permute-start.2
  8.3 1.6 %collective-permute-done.1.both_peer = bf16[256,1024]{1,0:T(8,128)(2,1)S(1)} collective-permute-done((bf16[256,1024]{1,0:T(8,128)(2,1)S(1)}, bf16[256,1024]{1,0:T(8,128)(2,1)S(1)}, u32[]{:S(2)}, u32[]{:S(2)}) %collective-permute-start.1) | collective-permute-done | bytes 524320 | tf_op jit(solution)/shard_map/ppermute | solution.py:228
  9.8 1.0 %prep.1.rows_all = bf16[8192,128]{1,0:T(8,128)(2,1)S(1)} custom-call(s32[2]{0:T(128)S(1)} %pad_add_fusion.place, bf16[128,2048]{1,0:T(8,128)(2,1)S(1)} %copy-done, bf16[128,2048]{1,0:T(8,128)(2,1)S(1)} %copy-done.1, bf16[256,1024]{1,0:T(8,128)(2,1)S(1)} %collective-permute-done.1.both_peer), custom_call_target="tpu_custom_call" | custom-call | flops 1073741824 | bytes 1048576 | tf_op jit(solution)/shard_map/prep/pallas_call | solution.py:171
  10.8 2.3 %stats_0.1 = (f32[16,256]{1,0:T(8,128)S(1)}, f32[16,256]{1,0:T(8,128)S(1)}, f32[16,256]{1,0:T(8,128)S(1)}) custom-call(s32[2]{0:T(128)S(1)} %pad_add_fusion.place, f32[32]{0:T(128)S(1)} %copy-done.2, bf16[8192,128]{1,0:T(8,128)(2,1)S(1)} %prep.1.rows_all, bf16[272,512]{1,0:T(8,128)(2,1)S(1)} %maximum_maximum_fusion.chunk.own_chunk, ...), custom_call_target="tpu_custom_call" | custom-call | flops 2147483648 | bytes 1048576 | tf_op jit(solution)/shard_map/stats_0/pallas_call | solution.py:171
  13.2 7.8 %collective-permute-done.2.chunk = bf16[272,512]{1,0:T(8,128)(2,1)S(1)} collective-permute-done((bf16[272,512]{1,0:T(8,128)(2,1)S(1)}, bf16[272,512]{1,0:T(8,128)(2,1)S(1)}, u32[]{:S(2)}, u32[]{:S(2)}) %collective-permute-start.2) | collective-permute-done | bytes 278560 | tf_op jit(solution)/shard_map/ppermute | solution.py:222
  21.0 0.1 broadcast_select_fusion.1
  21.1 1.4 %collective-permute-start.5 = (bf16[272,512]{1,0:T(8,128)(2,1)S(1)}, bf16[272,512]{1,0:T(8,128)(2,1)S(1)}, u32[]{:S(2)}, u32[]{:S(2)}) collective-permute-start(bf16[272,512]{1,0:T(8,128)(2,1)S(1)} %get-tuple-element.113), channel_id=1, source_target_pairs={{0,2},{1,3},{2,4},{3,5},{4,6},{5,7},{6,0},{7,1},{8,10},{9,11},{10,... | collective-permute-start | bytes 835592 | tf_op jit(solution)/shard_map/ppermute | solution.py:222
  22.5 1.5 %collective-permute-start.4 = (bf16[272,512]{1,0:T(8,128)(2,1)S(1)}, bf16[272,512]{1,0:T(8,128)(2,1)S(1)}, u32[]{:S(2)}, u32[]{:S(2)}) collective-permute-start(bf16[272,512]{1,0:T(8,128)(2,1)S(1)} %get-tuple-element.112), channel_id=1, source_target_pairs={{0,6},{1,7},{2,0},{3,1},{4,2},{5,3},{6,4},{7,5},{8,14},{9,15},{10,... | collective-permute-start | bytes 835592 | tf_op jit(solution)/shard_map/ppermute | solution.py:222
  24.0 1.6 %collective-permute-start.3 = (bf16[272,512]{1,0:T(8,128)(2,1)S(1)}, bf16[272,512]{1,0:T(8,128)(2,1)S(1)}, u32[]{:S(2)}, u32[]{:S(2)}) collective-permute-start(bf16[272,512]{1,0:T(8,128)(2,1)S(1)} %get-tuple-element.114), channel_id=1, source_target_pairs={{0,4},{1,5},{2,6},{3,7},{4,0},{5,1},{6,2},{7,3},{8,12},{9,13},{10,... | collective-permute-start | bytes 835592 | tf_op jit(solution)/shard_map/ppermute | solution.py:222
  25.6 2.4 %stats_4.1 = (f32[16,256]{1,0:T(8,128)S(1)}, f32[16,256]{1,0:T(8,128)S(1)}, f32[16,256]{1,0:T(8,128)S(1)}) custom-call(s32[2]{0:T(128)S(1)} %pad_add_fusion.place, f32[32]{0:T(128)S(1)} %copy-done.2, bf16[8192,128]{1,0:T(8,128)(2,1)S(1)} %prep.1.rows_all, bf16[272,512]{1,0:T(8,128)(2,1)S(1)} %collective-permute-done.2.chunk, ...), custom_call_target="tpu_custom_call" | custom-call | flops 2147483648 | bytes 1048576 | tf_op jit(solution)/shard_map/stats_4/pallas_call | solution.py:171
  28.0 1.8 %collective-permute-done.5.chunk = bf16[272,512]{1,0:T(8,128)(2,1)S(1)} collective-permute-done((bf16[272,512]{1,0:T(8,128)(2,1)S(1)}, bf16[272,512]{1,0:T(8,128)(2,1)S(1)}, u32[]{:S(2)}, u32[]{:S(2)}) %collective-permute-start.5) | collective-permute-done | bytes 278560 | tf_op jit(solution)/shard_map/ppermute | solution.py:222
  29.8 2.4 %stats_1.1 = (f32[16,256]{1,0:T(8,128)S(1)}, f32[16,256]{1,0:T(8,128)S(1)}, f32[16,256]{1,0:T(8,128)S(1)}) custom-call(s32[2]{0:T(128)S(1)} %pad_add_fusion.place, f32[32]{0:T(128)S(1)} %copy-done.2, bf16[8192,128]{1,0:T(8,128)(2,1)S(1)} %prep.1.rows_all, bf16[272,512]{1,0:T(8,128)(2,1)S(1)} %collective-permute-done.5.chunk, ...), custom_call_target="tpu_custom_call" | custom-call | flops 2147483648 | bytes 1048576 | tf_op jit(solution)/shard_map/stats_1/pallas_call | solution.py:171
  32.2 2.4 %stats_3.1 = (f32[16,256]{1,0:T(8,128)S(1)}, f32[16,256]{1,0:T(8,128)S(1)}, f32[16,256]{1,0:T(8,128)S(1)}) custom-call(s32[2]{0:T(128)S(1)} %pad_add_fusion.place, f32[32]{0:T(128)S(1)} %copy-done.2, bf16[8192,128]{1,0:T(8,128)(2,1)S(1)} %prep.1.rows_all, bf16[272,512]{1,0:T(8,128)(2,1)S(1)} %collective-permute-done.4.chunk, ...), custom_call_target="tpu_custom_call" | custom-call | flops 2147483648 | bytes 1048576 | tf_op jit(solution)/shard_map/stats_3/pallas_call | solution.py:171
  34.7 2.2 %collective-permute-done.3.chunk = bf16[272,512]{1,0:T(8,128)(2,1)S(1)} collective-permute-done((bf16[272,512]{1,0:T(8,128)(2,1)S(1)}, bf16[272,512]{1,0:T(8,128)(2,1)S(1)}, u32[]{:S(2)}, u32[]{:S(2)}) %collective-permute-start.3) | collective-permute-done | bytes 278560 | tf_op jit(solution)/shard_map/ppermute | solution.py:222
  36.9 2.6 %stats_2.1 = (f32[16,256]{1,0:T(8,128)S(1)}, f32[16,256]{1,0:T(8,128)S(1)}, f32[16,256]{1,0:T(8,128)S(1)}, f32[1,16]{1,0:T(1,128)S(1)}) custom-call(s32[2]{0:T(128)S(1)} %pad_add_fusion.place, f32[32]{0:T(128)S(1)} %copy-done.2, bf16[8192,128]{1,0:T(8,128)(2,1)S(1)} %prep.1.rows_all, bf16[272,512]{1,0:T(8,128)(2,1)S(1)} %collective-permute-done.3.chunk, ...), custom_call_target="tpu_custom_call" | custom-call | flops 2147483648 | bytes 1048576 | tf_op jit(solution)/shard_map/stats_2/pallas_call | solution.py:171
  39.5 0.4 collective-permute-start.6
  39.9 3.5 %parts_4.1 = (bf16[256,512]{1,0:T(8,128)(2,1)S(1)}, f32[256,1024]{1,0:T(8,128)S(1)}) custom-call(s32[2]{0:T(128)S(1)} %pad_add_fusion.place, bf16[8192,128]{1,0:T(8,128)(2,1)S(1)} %prep.1.rows_all, bf16[272,512]{1,0:T(8,128)(2,1)S(1)} %collective-permute-done.2.chunk, bf16[272,512]{1,0:T(8,128)(2,1)S(1)} %maximum_maximum_fusion.chunk.own_chunk, ...), custom_call_target="tpu_custom_call" | custom-call | flops 3221225472 | bytes 1048576 | tf_op jit(solution)/shard_map/parts_4/pallas_call | solution.py:171
  43.4 0.9 collective-permute-start.9
  44.3 3.5 %parts_3.1 = (bf16[256,512]{1,0:T(8,128)(2,1)S(1)}, f32[256,1024]{1,0:T(8,128)S(1)}) custom-call(s32[2]{0:T(128)S(1)} %pad_add_fusion.place, bf16[8192,128]{1,0:T(8,128)(2,1)S(1)} %prep.1.rows_all, bf16[272,512]{1,0:T(8,128)(2,1)S(1)} %collective-permute-done.4.chunk, bf16[272,512]{1,0:T(8,128)(2,1)S(1)} %maximum_maximum_fusion.chunk.own_chunk, ...), custom_call_target="tpu_custom_call" | custom-call | flops 3221225472 | bytes 1048576 | tf_op jit(solution)/shard_map/parts_3/pallas_call | solution.py:171
  47.8 4.1 %collective-permute-start.11 = (bf16[256,512]{1,0:T(8,128)(2,1)S(1)}, bf16[256,512]{1,0:T(8,128)(2,1)S(1)}, u32[]{:S(2)}, u32[]{:S(2)}) collective-permute-start(bf16[256,512]{1,0:T(8,128)(2,1)S(1)} %get-tuple-element.94), channel_id=1, source_target_pairs={{0,250},{1,251},{2,252},{3,253},{4,254},{5,255},{6,0},{7,1},{8,2},... | collective-permute-start | bytes 786440 | tf_op jit(solution)/shard_map/ppermute | solution.py:222
  51.9 2.0 %collective-permute-start.8 = (f32[16]{0:T(128)S(1)}, f32[16]{0:T(128)S(1)}, u32[]{:S(2)}, u32[]{:S(2)}) collective-permute-start(f32[16]{0:T(128)S(1)} %add.60), channel_id=1, source_target_pairs={{0,32},{1,33},{2,34},{3,35},{4,36},{5,37},{6,38},{7,39},{8,40},{9,... | collective-permute-start | bytes 200 | tf_op jit(solution)/shard_map/ppermute | solution.py:228
  53.9 3.5 %parts_2.1 = (bf16[256,512]{1,0:T(8,128)(2,1)S(1)}, f32[256,1024]{1,0:T(8,128)S(1)}) custom-call(s32[2]{0:T(128)S(1)} %pad_add_fusion.place, bf16[8192,128]{1,0:T(8,128)(2,1)S(1)} %prep.1.rows_all, bf16[272,512]{1,0:T(8,128)(2,1)S(1)} %collective-permute-done.3.chunk, bf16[272,512]{1,0:T(8,128)(2,1)S(1)} %maximum_maximum_fusion.chunk.own_chunk, ...), custom_call_target="tpu_custom_call" | custom-call | flops 3221225472 | bytes 1048576 | tf_op jit(solution)/shard_map/parts_2/pallas_call | solution.py:171
  57.4 3.4 %collective-permute-start.12 = (bf16[256,512]{1,0:T(8,128)(2,1)S(1)}, bf16[256,512]{1,0:T(8,128)(2,1)S(1)}, u32[]{:S(2)}, u32[]{:S(2)}) collective-permute-start(bf16[256,512]{1,0:T(8,128)(2,1)S(1)} %get-tuple-element.99), channel_id=1, source_target_pairs={{0,252},{1,253},{2,254},{3,255},{4,0},{5,1},{6,2},{7,3},{8,4},{9,5... | collective-permute-start | bytes 786440 | tf_op jit(solution)/shard_map/ppermute | solution.py:222
  60.9 0.3 collective-permute-start.10
  61.2 3.5 %parts_1.1 = (bf16[256,512]{1,0:T(8,128)(2,1)S(1)}, f32[256,1024]{1,0:T(8,128)S(1)}) custom-call(s32[2]{0:T(128)S(1)} %pad_add_fusion.place, bf16[8192,128]{1,0:T(8,128)(2,1)S(1)} %prep.1.rows_all, bf16[272,512]{1,0:T(8,128)(2,1)S(1)} %collective-permute-done.5.chunk, bf16[272,512]{1,0:T(8,128)(2,1)S(1)} %maximum_maximum_fusion.chunk.own_chunk, ...), custom_call_target="tpu_custom_call" | custom-call | flops 3221225472 | bytes 1048576 | tf_op jit(solution)/shard_map/parts_1/pallas_call | solution.py:171
  64.7 1.6 %collective-permute-start.13 = (bf16[256,512]{1,0:T(8,128)(2,1)S(1)}, bf16[256,512]{1,0:T(8,128)(2,1)S(1)}, u32[]{:S(2)}, u32[]{:S(2)}) collective-permute-start(bf16[256,512]{1,0:T(8,128)(2,1)S(1)} %get-tuple-element.100), channel_id=1, source_target_pairs={{0,254},{1,255},{2,0},{3,1},{4,2},{5,3},{6,4},{7,5},{8,6},{9,7},{1... | collective-permute-start | bytes 786440 | tf_op jit(solution)/shard_map/ppermute | solution.py:222
  66.2 0.4 collective-permute-start.14
  66.7 3.6 %parts_0.1 = (f32[256,512]{1,0:T(8,128)S(1)}, bf16[128,1024]{1,0:T(8,128)(2,1)S(1)}, bf16[128,1024]{1,0:T(8,128)(2,1)S(1)}) custom-call(s32[2]{0:T(128)S(1)} %pad_add_fusion.place, bf16[8192,128]{1,0:T(8,128)(2,1)S(1)} %prep.1.rows_all, bf16[272,512]{1,0:T(8,128)(2,1)S(1)} %maximum_maximum_fusion.chunk.own_chunk, ...), custom_call_target="tpu_custom_call" | custom-call | flops 3221225472 | bytes 1048576 | tf_op jit(solution)/shard_map/parts_0/pallas_call | solution.py:171
  70.3 1.9 %collective-permute-done.14 = f32[16]{0:T(128)S(1)} collective-permute-done((f32[16]{0:T(128)S(1)}, f32[16]{0:T(128)S(1)}, u32[]{:S(2)}, u32[]{:S(2)}) %collective-permute-start.14) | collective-permute-done | bytes 96 | tf_op jit(solution)/shard_map/ppermute | solution.py:228
  72.2 1.1 %collective-permute-start.15 = (f32[16]{0:T(128)S(1)}, f32[16]{0:T(128)S(1)}, u32[]{:S(2)}, u32[]{:S(2)}) collective-permute-start(f32[16]{0:T(128)S(1)} %add.67), channel_id=1, source_target_pairs={{0,64},{1,65},{2,66},{3,67},{4,68},{5,69},{6,70},{7,71},{8,72},{9,... | collective-permute-start | bytes 200 | tf_op jit(solution)/shard_map/ppermute | solution.py:228
  73.3 6.0 %collective-permute-start.17 = (bf16[128,1024]{1,0:T(8,128)(2,1)S(1)}, bf16[128,1024]{1,0:T(8,128)(2,1)S(1)}, u32[]{:S(2)}, u32[]{:S(2)}) collective-permute-start(bf16[128,1024]{1,0:T(8,128)(2,1)S(1)} %get-tuple-element.107), channel_id=1, source_target_pairs={{0,1},{1,0},{2,3},{3,2},{4,5},{5,4},{6,7},{7,6},{8,9},{9,8},{10,11... | collective-permute-start | bytes 786440 | tf_op jit(solution)/shard_map/ppermute | solution.py:228
  79.3 0.2 add_convert_fusion
  79.5 0.1 collective-permute-start.18
  79.6 3.0 %collective-permute-start.16 = (bf16[128,512]{1,0:T(8,128)(2,1)S(1)}, bf16[128,512]{1,0:T(8,128)(2,1)S(1)}, u32[]{:S(2)}, u32[]{:S(2)}) collective-permute-start(bf16[128,512]{1,0:T(8,128)(2,1)S(1)} %slice.63), channel_id=1, source_target_pairs={{0,1},{1,0},{2,3},{3,2},{4,5},{5,4},{6,7},{7,6},{8,9},{9,8},{10,11... | collective-permute-start | bytes 393224 | tf_op jit(solution)/shard_map/ppermute | solution.py:228
  82.6 0.9 %maximum_select_fusion = bf16[128,2048]{1,0:T(8,128)(2,1)} fusion(bf16[128,1024]{1,0:T(8,128)(2,1)S(1)} %collective-permute-done.17, bf16[128,1024]{1,0:T(8,128)(2,1)S(1)} %get-tuple-element.106, pred[]{:T(512)S(6)} %eq.8), kind=kLoop, calls=%fused_computation.1 | loop fusion | flops 2359296 | bytes 1048577 | tf_op jit(solution)/shard_map/jit(_where)/select_n | solution.py:293
  83.6 0.1 collective-permute-done.16
  83.6 3.3 %collective-permute-start.19 = (f32[16]{0:T(128)S(1)}, f32[16]{0:T(128)S(1)}, u32[]{:S(2)}, u32[]{:S(2)}) collective-permute-start(f32[16]{0:T(128)S(1)} %add.69), channel_id=1, source_target_pairs={{0,1},{1,0},{2,3},{3,2},{4,5},{5,4},{6,7},{7,6},{8,9},{9,8},{10,11... | collective-permute-start | bytes 200 | tf_op jit(solution)/shard_map/ppermute | solution.py:228
  87.0 0.7 maximum_select_fusion.2
  87.7 0.7 maximum_select_fusion.1
  88.4 0.6 broadcast_select_fusion.5
  (39 shorter events, 0.3 us)
Async XLA Ops:
  3.1 6.7 %copy-start = (bf16[128,2048]{1,0:T(8,128)(2,1)S(1)}, bf16[128,2048]{1,0:T(8,128)(2,1)}, u32[]{:S(2)}) copy-start(bf16[128,2048]{1,0:T(8,128)(2,1)} %q_own) | copy-start | bytes 1572868
  3.1 6.7 %copy-start.1 = (bf16[128,2048]{1,0:T(8,128)(2,1)S(1)}, bf16[128,2048]{1,0:T(8,128)(2,1)}, u32[]{:S(2)}) copy-start(bf16[128,2048]{1,0:T(8,128)(2,1)} %g_own) | copy-start | bytes 1572868
  3.2 4.6 %collective-permute-start = (bf16[144,512]{1,0:T(8,128)(2,1)S(1)}, bf16[144,512]{1,0:T(8,128)(2,1)S(1)}, u32[]{:S(2)}, u32[]{:S(2)}) collective-permute-start(bf16[144,512]{1,0:T(8,128)(2,1)S(1)} %pad_maximum_fusion.1), channel_id=1, source_target_pairs={{0,1},{1,0},{2,3},{3,2},{4,5},{5,4},{6,7},{7,6},{8,9},{9,8},{10,11... | collective-permute-start | bytes 442376 | tf_op jit(solution)/shard_map/ppermute | solution.py:228
  7.8 2.0 %collective-permute-start.1 = (bf16[256,1024]{1,0:T(8,128)(2,1)S(1)}, bf16[256,1024]{1,0:T(8,128)(2,1)S(1)}, u32[]{:S(2)}, u32[]{:S(2)}) collective-permute-start(bf16[256,1024]{1,0:T(8,128)(2,1)S(1)} %pad_maximum_fusion), channel_id=1, source_target_pairs={{0,1},{1,0},{2,3},{3,2},{4,5},{5,4},{6,7},{7,6},{8,9},{9,8},{10,11... | collective-permute-start | bytes 1572872 | tf_op jit(solution)/shard_map/ppermute | solution.py:228
  8.2 2.7 %copy-start.2 = (f32[32]{0:T(128)S(1)}, f32[32]{0:T(128)}, u32[]{:S(2)}) copy-start(f32[32]{0:T(128)} %sinks.9) | copy-start | bytes 388
  8.2 12.8 %collective-permute-start.2 = (bf16[272,512]{1,0:T(8,128)(2,1)S(1)}, bf16[272,512]{1,0:T(8,128)(2,1)S(1)}, u32[]{:S(2)}, u32[]{:S(2)}) collective-permute-start(bf16[272,512]{1,0:T(8,128)(2,1)S(1)} %maximum_maximum_fusion.chunk.own_chunk), channel_id=1, source_target_pairs={{0,8},{1,9},{2,10},{3,11},{4,12},{5,13},{6,14},{7,15},{8,16},{9,17... | collective-permute-start | bytes 835592 | tf_op jit(solution)/shard_map/ppermute | solution.py:222
  21.1 8.7 %collective-permute-start.5 = (bf16[272,512]{1,0:T(8,128)(2,1)S(1)}, bf16[272,512]{1,0:T(8,128)(2,1)S(1)}, u32[]{:S(2)}, u32[]{:S(2)}) collective-permute-start(bf16[272,512]{1,0:T(8,128)(2,1)S(1)} %get-tuple-element.113), channel_id=1, source_target_pairs={{0,2},{1,3},{2,4},{3,5},{4,6},{5,7},{6,0},{7,1},{8,10},{9,11},{10,... | collective-permute-start | bytes 835592 | tf_op jit(solution)/shard_map/ppermute | solution.py:222
  22.5 9.7 %collective-permute-start.4 = (bf16[272,512]{1,0:T(8,128)(2,1)S(1)}, bf16[272,512]{1,0:T(8,128)(2,1)S(1)}, u32[]{:S(2)}, u32[]{:S(2)}) collective-permute-start(bf16[272,512]{1,0:T(8,128)(2,1)S(1)} %get-tuple-element.112), channel_id=1, source_target_pairs={{0,6},{1,7},{2,0},{3,1},{4,2},{5,3},{6,4},{7,5},{8,14},{9,15},{10,... | collective-permute-start | bytes 835592 | tf_op jit(solution)/shard_map/ppermute | solution.py:222
  24.0 12.9 %collective-permute-start.3 = (bf16[272,512]{1,0:T(8,128)(2,1)S(1)}, bf16[272,512]{1,0:T(8,128)(2,1)S(1)}, u32[]{:S(2)}, u32[]{:S(2)}) collective-permute-start(bf16[272,512]{1,0:T(8,128)(2,1)S(1)} %get-tuple-element.114), channel_id=1, source_target_pairs={{0,4},{1,5},{2,6},{3,7},{4,0},{5,1},{6,2},{7,3},{8,12},{9,13},{10,... | collective-permute-start | bytes 835592 | tf_op jit(solution)/shard_map/ppermute | solution.py:222
  39.5 4.8 %collective-permute-start.6 = (f32[16]{0:T(128)S(1)}, f32[16]{0:T(128)S(1)}, u32[]{:S(2)}, u32[]{:S(2)}) collective-permute-start(f32[16]{0:T(128)S(1)} %bitcast.6), channel_id=1, source_target_pairs={{0,4},{1,5},{2,6},{3,7},{4,0},{5,1},{6,2},{7,3},{8,12},{9,13},{10,... | collective-permute-start | bytes 200 | tf_op jit(solution)/shard_map/ppermute | solution.py:228
  43.4 17.4 %collective-permute-start.9 = (bf16[256,512]{1,0:T(8,128)(2,1)S(1)}, bf16[256,512]{1,0:T(8,128)(2,1)S(1)}, u32[]{:S(2)}, u32[]{:S(2)}) collective-permute-start(bf16[256,512]{1,0:T(8,128)(2,1)S(1)} %get-tuple-element.90), channel_id=1, source_target_pairs={{0,248},{1,249},{2,250},{3,251},{4,252},{5,253},{6,254},{7,255},{8... | collective-permute-start | bytes 786440 | tf_op jit(solution)/shard_map/ppermute | solution.py:222
  44.3 7.6 %collective-permute-start.7 = (f32[16]{0:T(128)S(1)}, f32[16]{0:T(128)S(1)}, u32[]{:S(2)}, u32[]{:S(2)}) collective-permute-start(f32[16]{0:T(128)S(1)} %bitcast_add_fusion), channel_id=1, source_target_pairs={{0,16},{1,17},{2,18},{3,19},{4,20},{5,21},{6,22},{7,23},{8,24},{9,... | collective-permute-start | bytes 200 | tf_op jit(solution)/shard_map/ppermute | solution.py:228
  47.8 18.4 %collective-permute-start.11 = (bf16[256,512]{1,0:T(8,128)(2,1)S(1)}, bf16[256,512]{1,0:T(8,128)(2,1)S(1)}, u32[]{:S(2)}, u32[]{:S(2)}) collective-permute-start(bf16[256,512]{1,0:T(8,128)(2,1)S(1)} %get-tuple-element.94), channel_id=1, source_target_pairs={{0,250},{1,251},{2,252},{3,253},{4,254},{5,255},{6,0},{7,1},{8,2},... | collective-permute-start | bytes 786440 | tf_op jit(solution)/shard_map/ppermute | solution.py:222
  51.9 8.9 %collective-permute-start.8 = (f32[16]{0:T(128)S(1)}, f32[16]{0:T(128)S(1)}, u32[]{:S(2)}, u32[]{:S(2)}) collective-permute-start(f32[16]{0:T(128)S(1)} %add.60), channel_id=1, source_target_pairs={{0,32},{1,33},{2,34},{3,35},{4,36},{5,37},{6,38},{7,39},{8,40},{9,... | collective-permute-start | bytes 200 | tf_op jit(solution)/shard_map/ppermute | solution.py:228
  57.4 21.9 %collective-permute-start.12 = (bf16[256,512]{1,0:T(8,128)(2,1)S(1)}, bf16[256,512]{1,0:T(8,128)(2,1)S(1)}, u32[]{:S(2)}, u32[]{:S(2)}) collective-permute-start(bf16[256,512]{1,0:T(8,128)(2,1)S(1)} %get-tuple-element.99), channel_id=1, source_target_pairs={{0,252},{1,253},{2,254},{3,255},{4,0},{5,1},{6,2},{7,3},{8,4},{9,5... | collective-permute-start | bytes 786440 | tf_op jit(solution)/shard_map/ppermute | solution.py:222
  60.9 5.4 %collective-permute-start.10 = (f32[16]{0:T(128)S(1)}, f32[16]{0:T(128)S(1)}, u32[]{:S(2)}, u32[]{:S(2)}) collective-permute-start(f32[16]{0:T(128)S(1)} %add.61), channel_id=1, source_target_pairs={{0,128},{1,129},{2,130},{3,131},{4,132},{5,133},{6,134},{7,135},{8... | collective-permute-start | bytes 200 | tf_op jit(solution)/shard_map/ppermute | solution.py:228
  64.7 14.6 %collective-permute-start.13 = (bf16[256,512]{1,0:T(8,128)(2,1)S(1)}, bf16[256,512]{1,0:T(8,128)(2,1)S(1)}, u32[]{:S(2)}, u32[]{:S(2)}) collective-permute-start(bf16[256,512]{1,0:T(8,128)(2,1)S(1)} %get-tuple-element.100), channel_id=1, source_target_pairs={{0,254},{1,255},{2,0},{3,1},{4,2},{5,3},{6,4},{7,5},{8,6},{9,7},{1... | collective-permute-start | bytes 786440 | tf_op jit(solution)/shard_map/ppermute | solution.py:222
  66.2 6.0 %collective-permute-start.14 = (f32[16]{0:T(128)S(1)}, f32[16]{0:T(128)S(1)}, u32[]{:S(2)}, u32[]{:S(2)}) collective-permute-start(f32[16]{0:T(128)S(1)} %add.62), channel_id=1, source_target_pairs={{0,8},{1,9},{2,10},{3,11},{4,12},{5,13},{6,14},{7,15},{8,0},{9,1},... | collective-permute-start | bytes 200 | tf_op jit(solution)/shard_map/ppermute | solution.py:228
  72.2 7.1 %collective-permute-start.15 = (f32[16]{0:T(128)S(1)}, f32[16]{0:T(128)S(1)}, u32[]{:S(2)}, u32[]{:S(2)}) collective-permute-start(f32[16]{0:T(128)S(1)} %add.67), channel_id=1, source_target_pairs={{0,64},{1,65},{2,66},{3,67},{4,68},{5,69},{6,70},{7,71},{8,72},{9,... | collective-permute-start | bytes 200 | tf_op jit(solution)/shard_map/ppermute | solution.py:228
  73.3 9.3 %collective-permute-start.17 = (bf16[128,1024]{1,0:T(8,128)(2,1)S(1)}, bf16[128,1024]{1,0:T(8,128)(2,1)S(1)}, u32[]{:S(2)}, u32[]{:S(2)}) collective-permute-start(bf16[128,1024]{1,0:T(8,128)(2,1)S(1)} %get-tuple-element.107), channel_id=1, source_target_pairs={{0,1},{1,0},{2,3},{3,2},{4,5},{5,4},{6,7},{7,6},{8,9},{9,8},{10,11... | collective-permute-start | bytes 786440 | tf_op jit(solution)/shard_map/ppermute | solution.py:228
  79.5 3.1 %collective-permute-start.18 = (f32[16]{0:T(128)S(1)}, f32[16]{0:T(128)S(1)}, u32[]{:S(2)}, u32[]{:S(2)}) collective-permute-start(f32[16]{0:T(128)S(1)} %add.68), channel_id=1, source_target_pairs={{0,2},{1,3},{2,0},{3,1},{4,6},{5,7},{6,4},{7,5},{8,10},{9,11},{10,... | collective-permute-start | bytes 200 | tf_op jit(solution)/shard_map/ppermute | solution.py:228
  79.6 4.0 %collective-permute-start.16 = (bf16[128,512]{1,0:T(8,128)(2,1)S(1)}, bf16[128,512]{1,0:T(8,128)(2,1)S(1)}, u32[]{:S(2)}, u32[]{:S(2)}) collective-permute-start(bf16[128,512]{1,0:T(8,128)(2,1)S(1)} %slice.63), channel_id=1, source_target_pairs={{0,1},{1,0},{2,3},{3,2},{4,5},{5,4},{6,7},{7,6},{8,9},{9,8},{10,11... | collective-permute-start | bytes 393224 | tf_op jit(solution)/shard_map/ppermute | solution.py:228
  83.6 4.7 %collective-permute-start.19 = (f32[16]{0:T(128)S(1)}, f32[16]{0:T(128)S(1)}, u32[]{:S(2)}, u32[]{:S(2)}) collective-permute-start(f32[16]{0:T(128)S(1)} %add.69), channel_id=1, source_target_pairs={{0,1},{1,0},{2,3},{3,2},{4,5},{5,4},{6,7},{7,6},{8,9},{9,8},{10,11... | collective-permute-start | bytes 200 | tf_op jit(solution)/shard_map/ppermute | solution.py:228
